TPU v7x, 32 devices: a whole 2x2x4 slice. The times are simulated.
32 devices in a mesh: seq: 16 (over z, x, core), ch: 2 (over y).
Axes of the slice: x: 2, y: 2, z: 4, core: 2. Of those that a mesh axis runs over, the one named last changes fastest.
Arguments:
- query_feat: bfloat16 [4096, 4096], P('seq', 'ch'), may hold values from -6 to 6
- key_feat: bfloat16 [4096, 4096], P('seq', 'ch'), may hold values from -6 to 6
- value_feat: bfloat16 [4096, 4096], P('seq', 'ch'), may hold values from -6 to 6
- short_filter: float32 [3, 3, 4096], P(None, None, 'ch'), may hold values from -3.5 to 3.5
- long_filter: float32 [2048, 4096], P('ch', 'seq'), may hold values from -0.09375 to 0.09375
- direct_gain: float32 [4096], P('ch'), may hold values from 0.25 to 1.5
- out_weight: bfloat16 [4096, 4096], P('seq', 'ch'), may hold values from -0.09375 to 0.09375
Outputs:
- layer_out: bfloat16 [4096, 4096], P('seq', 'ch')
All inputs are finite; a program needn't handle non-finite values.
Results may differ from a plain program's by a relative error of at most 0.0049.
Values may be sent and summed in bfloat16 or wider, within the bound.
No kernel may reach another device: no remote copies, remote signals or barrier semaphores. Data moves between devices by JAX's collectives and lax.ppermute only.
A program may use at most 64 MiB of HBM per device.

v0:
```python
import functools

import jax
import jax.numpy as jnp
from jax import lax
from jax.experimental import pallas as pl
from jax.experimental.pallas import tpu as pltpu
from jax.sharding import PartitionSpec as P


TAPS = 3
PARTS = 2
LANES = 128
PACK = 16


def shifted(block, axis, distance):
    devices = range(lax.axis_size(axis))
    route = [(i - distance, i) for i in devices if i - distance in devices]
    return lax.ppermute(block, axis, route)


def featurized(inputs, edge, taps):
    rows = inputs.astype(jnp.float32)
    index = lax.broadcasted_iota(jnp.int32, rows.shape, 0)
    total = taps[0:1] * rows
    for tap in range(1, TAPS):
        moved = pltpu.roll(rows, tap, 0)
        for row in range(tap):
            first = TAPS - 1 - tap + row
            moved = jnp.where(index == row, edge[first : first + 1], moved)
        total = total + taps[tap : tap + 1] * moved
    return total


def mix_kernel(key_ref, value_ref, edge_ref, short_ref, turned_ref):
    edge = edge_ref[...].astype(jnp.float32)
    mixed = featurized(key_ref[...], edge[1], short_ref[1]) * featurized(
        value_ref[...], edge[2], short_ref[2]
    )
    turned_ref[...] = mixed.T.astype(jnp.bfloat16).reshape(turned_ref.shape)


def gate_kernel(query_ref, edge_ref, short_ref, conv_ref, gated_ref):
    edge = edge_ref[...].astype(jnp.float32)
    query_short = featurized(query_ref[...], edge, short_ref[0])
    summed = conv_ref[...].astype(jnp.float32).reshape(query_short.shape[1], query_short.shape[0]).T
    gated_ref[0] = (query_short * summed).astype(jnp.bfloat16)


def conv_kernel(n, tok, width, place, x_ref, f_ref, gain_ref, y_ref, xi, xs, ys):
    halves = tok // LANES
    groups = LANES // PACK
    for e in range(halves):
        for i in range(n):
            xi[e, i * width : (i + 1) * width, :] = x_ref[
                i, :, e * LANES : (e + 1) * LANES
            ].astype(jnp.float32)
        for c in range(width):
            xs[e, c, 0:n, :] = jnp.zeros((n, LANES), jnp.float32)
            xs[e, c, n : 2 * n, :] = xi[e, pl.ds(c, n, stride=width), :]
    lane = lax.broadcasted_iota(jnp.int32, (PACK, LANES), 1)
    sub = lax.broadcasted_iota(jnp.int32, (PACK, LANES), 0)

    def one(p, carry):
        def skewed(m):
            if m == 0:
                return jnp.zeros((PACK, LANES), jnp.float32)
            row = f_ref[p, m - 1 : m, :]
            return pltpu.roll(
                jnp.broadcast_to(row, (PACK, LANES)), 0, 1, stride=1, stride_axis=0
            )

        def turns(m, part):
            now = skewed(m)
            base = jnp.where(lane >= sub, now, part).astype(jnp.bfloat16)
            return now, [base] + [
                pltpu.roll(base, LANES - PACK * k, 1) for k in range(1, groups)
            ]

        def stack(before, after):
            tiles = [after[0]]
            for k in range(groups - 1, 0, -1):
                tiles.append(jnp.where(lane < LANES - PACK * k, before[k], after[k]))
            return jnp.concatenate(tiles, axis=0)

        part, before = turns(0, skewed(0))
        old = jnp.zeros((LANES, LANES), jnp.bfloat16)
        acc = None
        for d in range(n):
            cols = [old]
            for e in range(halves):
                part, after = turns(d * halves + e + 1, part)
                cols.append(stack(before, after))
                before = after
            old = cols[-1]
            rhs = jnp.concatenate(
                [jnp.concatenate(cols[1:], axis=1), jnp.concatenate(cols[:-1], axis=1)], axis=0
            )
            lhs = jnp.concatenate(
                [
                    jnp.concatenate(
                        [
                            xs[e, 2 * p + c, n - d : 2 * n - d, :].astype(jnp.bfloat16)
                            for e in range(halves)
                        ],
                        axis=1,
                    )
                    for c in range(2)
                ],
                axis=0,
            )
            out = jnp.dot(lhs, rhs, preferred_element_type=jnp.float32)
            acc = out if acc is None else acc + out
        for e in range(halves):
            for c in range(2):
                ys[e, pl.ds(2 * p + c, n, stride=width), :] = acc[
                    c * n : (c + 1) * n, e * LANES : (e + 1) * LANES
                ]
        return carry

    lax.fori_loop(0, width // 2, one, 0, unroll=4 if n <= 16 else 1)
    for e in range(halves):
        for i in range(n):
            rows = slice(i * width, (i + 1) * width)
            total = ys[e, rows, :] + gain_ref[...] * xi[e, rows, :]
            y_ref[place(i), :, e * LANES : (e + 1) * LANES] = total.astype(jnp.bfloat16)


def convolve(x, f, gain, part, place):
    n, chans, tok = x.shape
    width = min(16, chans)
    halves = tok // LANES
    assert halves == 2
    return pl.pallas_call(
        functools.partial(conv_kernel, n, tok, width, place),
        grid=(chans // width,),
        in_specs=[
            pl.BlockSpec((n, width, tok), lambda g: (0, g, 0)),
            pl.BlockSpec(
                (width // 2, n * halves, LANES), lambda g: (g + part * (chans // width), 0, 0)
            ),
            pl.BlockSpec((width, LANES), lambda g: (g + part * (chans // width), 0)),
        ],
        out_specs=pl.BlockSpec((n, width, tok), lambda g: (0, g, 0)),
        out_shape=jax.ShapeDtypeStruct(x.shape, jnp.bfloat16),
        scratch_shapes=[
            pltpu.VMEM((halves, n * width, LANES), jnp.float32),
            pltpu.VMEM((halves, width, 2 * n, LANES), jnp.float32),
            pltpu.VMEM((halves, n * width, LANES), jnp.float32),
        ],
        name="convolve",
    )(x, f, gain)


def mix(key_feat, value_feat, edges, short_filter, part, parts, outer, inner):
    tokens, channels = key_feat.shape
    wide = channels // (2 * parts)
    return pl.pallas_call(
        mix_kernel,
        grid=(2,),
        in_specs=[
            pl.BlockSpec((tokens, wide), lambda g: (0, g * parts + part)),
            pl.BlockSpec((tokens, wide), lambda g: (0, g * parts + part)),
            pl.BlockSpec((3, TAPS - 1, wide), lambda g: (0, 0, g * parts + part)),
            pl.BlockSpec((3, TAPS, wide), lambda g: (0, 0, g * parts + part)),
        ],
        out_specs=pl.BlockSpec(
            (outer, 1, inner, wide // (outer * inner), tokens), lambda g: (0, g, 0, 0, 0)
        ),
        out_shape=jax.ShapeDtypeStruct(
            (outer, 2, inner, wide // (outer * inner), tokens), jnp.bfloat16
        ),
        name="mix",
    )(key_feat, value_feat, edges, short_filter)


def gate(spot, query, edge, short_filter, conv, first, wide):
    sources, _, each, tokens = conv.shape
    blocks = sources * each // wide
    per = wide // each
    return pl.pallas_call(
        lambda spot_ref, *refs: gate_kernel(*refs),
        grid_spec=pltpu.PrefetchScalarGridSpec(
            num_scalar_prefetch=1,
            grid=(blocks,),
            in_specs=[
                pl.BlockSpec((tokens, wide), lambda g, spot: (0, spot[0] + g + first * blocks)),
                pl.BlockSpec((TAPS - 1, wide), lambda g, spot: (0, spot[0] + g + first * blocks)),
                pl.BlockSpec((3, TAPS, wide), lambda g, spot: (0, 0, spot[1] + g + first * blocks)),
                pl.BlockSpec((per, 1, each, tokens), lambda g, spot: (g, spot[2], 0, 0)),
            ],
            out_specs=pl.BlockSpec((1, tokens, wide), lambda g, spot: (g, 0, 0)),
        ),
        out_shape=jax.ShapeDtypeStruct((blocks, tokens, wide), jnp.bfloat16),
        name="gate",
    )(spot, query, edge, short_filter, conv)


def plain(query_feat, key_feat, value_feat, short_filter, long_filter, direct_gain, out_weight):
    tokens, channels = query_feat.shape
    devices = lax.axis_size("seq")
    pairs = long_filter.shape[0] // devices
    here = lax.axis_index("seq")
    weights = lax.all_gather(out_weight, "seq", axis=0, tiled=True)
    last = slice(tokens - (TAPS - 1), None)
    edges = shifted(jnp.stack([query_feat[last], key_feat[last], value_feat[last]]), "seq", 1)
    sent = long_filter.astype(jnp.bfloat16).reshape(devices, pairs, tokens)
    taps = lax.all_to_all(sent, "seq", split_axis=0, concat_axis=0, tiled=True)
    taps = taps.astype(jnp.float32).transpose(1, 0, 2)
    taps = taps.reshape(pairs, devices * tokens // LANES, LANES)
    gain = lax.dynamic_index_in_dim(direct_gain.reshape(devices, 2 * pairs, 1), here, 0, False)
    gain = jnp.broadcast_to(gain, (2 * pairs, LANES))
    turned = mix(key_feat, value_feat, edges, short_filter, 0, 1, 1, devices // 2)
    turned = turned.reshape(devices, 2 * pairs, tokens)
    spread = lax.all_to_all(turned, "seq", split_axis=0, concat_axis=0, tiled=True)
    conv = convolve(spread, taps, gain, 0, lambda i: i)
    conv = lax.all_to_all(conv, "seq", split_axis=0, concat_axis=0, tiled=True)
    wide = min(256, channels)
    spot = jnp.zeros((3,), jnp.int32)
    gated = gate(spot, query_feat, edges[0], short_filter, conv[:, None], 0, wide)
    gated = gated.transpose(1, 0, 2).reshape(tokens, channels)
    features = lax.all_gather(gated, "ch", axis=1, tiled=True)
    return jnp.dot(features, weights, preferred_element_type=jnp.float32).astype(jnp.bfloat16)


def project_kernel(count, parts, spots, *refs):
    gated, pieces = refs[: 2 * parts], refs[2 * parts : 2 * parts + count]
    out_ref, rows = refs[2 * parts + count :]
    blocks, _, wide = gated[0].shape

    @pl.when(pl.program_id(0) == 0)
    def _():
        for piece in range(count):
            spot = spots[piece]
            for source in range(2 * parts):

                @pl.when(spot // blocks == source)
                def _():
                    rows[:, piece * wide : (piece + 1) * wide] = gated[source][lax.rem(spot, blocks)]

    total = None
    for piece in range(count):
        out = jnp.dot(
            rows[:, piece * wide : (piece + 1) * wide],
            pieces[piece][...],
            preferred_element_type=jnp.float32,
        )
        total = out if total is None else total + out
    out_ref[...] = total.astype(out_ref.dtype)


def project(spots, gated, pieces, parts, kind):
    blocks, tokens, wide = gated[0].shape
    count = len(pieces)
    columns = pieces[0].shape[1]
    step = min(512, columns)
    whole = pl.BlockSpec((blocks, tokens, wide), lambda j, spots: (0, 0, 0))
    return pl.pallas_call(
        functools.partial(project_kernel, count, parts),
        grid_spec=pltpu.PrefetchScalarGridSpec(
            num_scalar_prefetch=1,
            grid=(columns // step,),
            in_specs=[whole] * len(gated)
            + [pl.BlockSpec((wide, step), lambda j, spots: (0, j))] * count,
            out_specs=pl.BlockSpec((tokens, step), lambda j, spots: (0, j)),
            scratch_shapes=[pltpu.VMEM((tokens, count * wide), jnp.bfloat16)],
        ),
        out_shape=jax.ShapeDtypeStruct((tokens, columns), kind),
        name="project",
    )(spots, *gated, *pieces)


def layer(query_feat, key_feat, value_feat, short_filter, long_filter, direct_gain, out_weight):
    tokens, channels = query_feat.shape
    devices = lax.axis_size("seq")
    sides = lax.axis_size("ch")
    here = lax.axis_index("seq")
    place = lax.axis_index("ch")
    depth, _ = out_weight.shape
    pairs = long_filter.shape[0] // devices
    inner, outer = 4, devices // 8
    small = sides == 2 and outer == 2 and depth % 256 == 0
    if not small:
        return plain(query_feat, key_feat, value_feat, short_filter, long_filter, direct_gain, out_weight)
    parts = PARTS
    twin = here // inner % 2
    rank = here // (2 * inner) * inner + here % inner

    def swap(block, axis, mask):
        return lax.ppermute(block, axis, [(i ^ mask, i) for i in range(lax.axis_size(axis))])

    last = slice(tokens - (TAPS - 1), None)
    edges = shifted(jnp.stack([query_feat[last], key_feat[last], value_feat[last]]), "seq", 1)

    far = swap(out_weight, "seq", 2 * inner)
    near = swap(out_weight, "seq", 2)
    mate = swap(out_weight, "seq", 1)
    far_near = swap(far, "seq", 2)
    far_mate = swap(far, "seq", 1)
    near_mate = swap(near, "seq", 1)
    far_near_mate = swap(far_near, "seq", 1)
    pieces = [out_weight, mate, near, near_mate, far, far_mate, far_near, far_near_mate]
    masks = [0, 1, 2, 3, 2 * inner, 2 * inner + 1, 2 * inner + 2, 2 * inner + 3]
    spots = []
    for mask in masks:
        owner = here ^ mask
        spots.append((owner // (2 * inner) != place) * inner + owner % inner)
    spots = jnp.stack(spots).astype(jnp.int32)

    sent = long_filter.astype(jnp.bfloat16)
    sent = sent.reshape(2, parts, outer, inner, pairs // parts, tokens).transpose(2, 0, 3, 1, 4, 5)
    taps = lax.all_to_all(sent.reshape(devices, pairs, tokens), "seq", split_axis=0, concat_axis=0, tiled=True)
    taps = taps.astype(jnp.float32).transpose(1, 0, 2)
    taps = taps.reshape(pairs, devices * tokens // LANES, LANES)
    gain = direct_gain.reshape(2, parts, devices // 2, 2 * pairs // parts)
    gain = lax.dynamic_index_in_dim(lax.dynamic_index_in_dim(gain, twin, 0, False), rank, 1, False)
    gain = jnp.broadcast_to(gain.reshape(2 * pairs, 1), (2 * pairs, LANES))

    half = channels // 2
    wide = depth
    padded = jnp.pad(edges[0], ((0, PACK - (TAPS - 1)), (0, 0)))
    asked = jnp.concatenate([query_feat, padded], axis=0)
    asked = lax.dynamic_slice_in_dim(asked, (1 - twin) * half, half, 1)
    asked = swap(asked, "seq", inner)
    asked_edge = asked[tokens : tokens + TAPS - 1]

    def at(i):
        return (i // (2 * inner) * inner + i % inner) * 2 + i // inner % 2

    groups = [[o * 2 * inner + t * inner + i for o in range(outer) for i in range(inner)] for t in range(2)]
    spreads, backs = [], []
    for part in range(parts):
        turned = mix(key_feat, value_feat, edges, short_filter, part, parts, outer, inner)
        turned = turned.reshape(devices, 2 * pairs // parts, tokens)
        spreads.append(lax.all_to_all(turned, "seq", split_axis=0, concat_axis=0, tiled=True))
    for part in range(parts):
        conv = convolve(spreads[part], taps, gain, part, at)
        conv = conv.reshape(devices // 2, 2, 2 * pairs // parts, tokens)
        backs.append(
            lax.all_to_all(conv, "seq", split_axis=0, concat_axis=0, tiled=True, axis_index_groups=groups)
        )
    blocks = half // wide
    kept_spot = jnp.stack([twin * blocks, twin * blocks, twin]).astype(jnp.int32)
    given_spot = jnp.stack([0 * twin, twin * blocks, 1 - twin]).astype(jnp.int32)
    kept, given = [], []
    for part in range(parts):
        given.append(gate(given_spot, asked, asked_edge, short_filter, backs[part], part, wide))
        kept.append(gate(kept_spot, query_feat, edges[0], short_filter, backs[part], part, wide))
    given_far, kept_far = [], []
    for part in range(parts):
        given_far.append(swap(given[part], "ch", 1))
        kept_far.append(swap(kept[part], "ch", 1))
    sums = project(spots, given + given_far, pieces, parts, jnp.bfloat16)
    taken = swap(sums, "seq", inner)
    sums = project(spots, kept + kept_far, pieces, parts, jnp.float32)
    return (sums + taken.astype(jnp.float32)).astype(jnp.bfloat16)


def solution(mesh):
    in_specs = (
        P("seq", "ch"),
        P("seq", "ch"),
        P("seq", "ch"),
        P(None, None, "ch"),
        P("ch", "seq"),
        P("ch"),
        P("seq", "ch"),
    )
    return jax.shard_map(layer, mesh=mesh, in_specs=in_specs, out_specs=P("seq", "ch"), check_vma=False)
```

profile of v0, /device:TPU:0, one launch (start us, length us, event | category | flops | bytes accessed | tf_op | source)
XLA Modules:
  0.0 226.2 jit_solution(9326247002735236668)
XLA Ops:
  2.1 7.4 %all-to-all-start.1 = ((bf16[16,64,256]{2,1,0:T(8,128)(2,1)}), bf16[16,64,256]{2,1,0:T(8,128)(2,1)S(1)}, u32[]{:S(2)}, u32[]{:S(2)}) async-start(bf16[16,64,256]{2,1,0:T(8,128)(2,1)} %bitcast.17), calls=%async_computation.1 | async-start | bytes 1048576 | tf_op jit(solution)/shard_map/all_to_all | solution.py:313
  14.3 2.8 %mix.2 = bf16[2,2,4,64,256]{4,3,2,1,0:T(8,128)(2,1)} custom-call(bf16[256,2048]{1,0:T(8,128)(2,1)} %key_ref.3, bf16[256,2048]{1,0:T(8,128)(2,1)} %value_ref.3, bf16[3,2,2048]{2,1,0:T(2,128)(2,1)} %copy-done.10, f32[3,3,2048]{2,1,0:T(4,128)} %refs_2_.7), custom_call_target="tpu_custom_call" | custom-call | tf_op jit(solution)/shard_map/mix/pallas_call | solution.py:159
  17.1 6.7 %all-to-all-done.1 = bf16[16,64,256]{2,1,0:T(8,128)(2,1)S(1)} async-done(((bf16[16,64,256]{2,1,0:T(8,128)(2,1)}), bf16[16,64,256]{2,1,0:T(8,128)(2,1)S(1)}, u32[]{:S(2)}, u32[]{:S(2)}) %all-to-all-start.1) | async-done | bytes 524320 | tf_op jit(solution)/shard_map/all_to_all | solution.py:313
  23.8 7.3 %all-to-all-start = ((bf16[16,64,256]{2,1,0:T(8,128)(2,1)}), bf16[16,64,256]{2,1,0:T(8,128)(2,1)S(1)}, u32[]{:S(2)}, u32[]{:S(2)}) async-start(bf16[16,64,256]{2,1,0:T(8,128)(2,1)} %bitcast.33), calls=%async_computation | async-start | bytes 1048576 | tf_op jit(solution)/shard_map/all_to_all | solution.py:336
  31.1 2.9 %collective-permute-start.6 = (bf16[256,2048]{1,0:T(8,128)(2,1)S(1)}, bf16[256,2048]{1,0:T(8,128)(2,1)}, u32[]{:S(2)}, u32[]{:S(2)}) collective-permute-start(bf16[256,2048]{1,0:T(8,128)(2,1)S(1)} %copy-done.3), channel_id=1, source_target_pairs={{16,0},{18,2},{20,4},{22,6},{24,8},{26,10},{28,12},{30,14},{0,16},... | collective-permute-start | bytes 3145736 | tf_op jit(solution)/shard_map/ppermute | solution.py:291
  34.0 2.8 %mix.3 = bf16[2,2,4,64,256]{4,3,2,1,0:T(8,128)(2,1)} custom-call(bf16[256,2048]{1,0:T(8,128)(2,1)} %key_ref.3, bf16[256,2048]{1,0:T(8,128)(2,1)} %value_ref.3, bf16[3,2,2048]{2,1,0:T(2,128)(2,1)} %copy-done.10, f32[3,3,2048]{2,1,0:T(4,128)} %refs_2_.7), custom_call_target="tpu_custom_call" | custom-call | tf_op jit(solution)/shard_map/mix/pallas_call | solution.py:159
  36.7 9.2 %all-to-all-done.x_ref = bf16[16,64,256]{2,1,0:T(8,128)(2,1)S(1)} async-done(((bf16[16,64,256]{2,1,0:T(8,128)(2,1)}), bf16[16,64,256]{2,1,0:T(8,128)(2,1)S(1)}, u32[]{:S(2)}, u32[]{:S(2)}) %all-to-all-start) | async-done | bytes 524320 | tf_op jit(solution)/shard_map/all_to_all | solution.py:336
  45.9 26.7 %all-to-all-start.3 = ((bf16[16,64,256]{2,1,0:T(8,128)(2,1)}), bf16[16,64,256]{2,1,0:T(8,128)(2,1)}, u32[]{:S(2)}, u32[]{:S(2)}) async-start(bf16[16,64,256]{2,1,0:T(8,128)(2,1)} %bitcast.30), calls=%async_computation.3 | async-start | bytes 1048576 | tf_op jit(solution)/shard_map/all_to_all | solution.py:336
  74.7 22.9 %collective-permute-done.6.refs_8_ = bf16[256,2048]{1,0:T(8,128)(2,1)} collective-permute-done((bf16[256,2048]{1,0:T(8,128)(2,1)S(1)}, bf16[256,2048]{1,0:T(8,128)(2,1)}, u32[]{:S(2)}, u32[]{:S(2)}) %collective-permute-start.6) | collective-permute-done | bytes 1048608 | tf_op jit(solution)/shard_map/ppermute | solution.py:291
  101.5 19.6 %convolve.2 = bf16[16,64,256]{2,1,0:T(8,128)(2,1)} custom-call(bf16[16,64,256]{2,1,0:T(8,128)(2,1)} %copy-done.5, f32[64,32,128]{2,1,0:T(8,128)} %reshape.41.f_ref, f32[128,128]{1,0:T(8,128)} %broadcast_in_dim.8.gain_ref), custom_call_target="tpu_custom_call" | custom-call | tf_op jit(solution)/shard_map/convolve/pallas_call | solution.py:135
  121.1 3.5 %all-to-all-start.2 = ((bf16[8,2,64,256]{3,2,1,0:T(8,128)(2,1)}), bf16[8,2,64,256]{3,2,1,0:T(8,128)(2,1)S(1)}, u32[]{:S(2)}, u32[]{:S(2)}) async-start(bf16[8,2,64,256]{3,2,1,0:T(8,128)(2,1)} %bitcast.32), calls=%async_computation.2 | async-start | bytes 1048576 | tf_op jit(solution)/shard_map/all_to_all | solution.py:341
  125.0 19.6 %convolve.3 = bf16[16,64,256]{2,1,0:T(8,128)(2,1)} custom-call(bf16[16,64,256]{2,1,0:T(8,128)(2,1)} %all-to-all-done.3.x_ref, f32[64,32,128]{2,1,0:T(8,128)} %reshape.41.f_ref, f32[128,128]{1,0:T(8,128)} %broadcast_in_dim.8.gain_ref), custom_call_target="tpu_custom_call" | custom-call | tf_op jit(solution)/shard_map/convolve/pallas_call | solution.py:135
  145.2 5.0 %all-to-all-start.4 = ((bf16[8,2,64,256]{3,2,1,0:T(8,128)(2,1)}), bf16[8,2,64,256]{3,2,1,0:T(8,128)(2,1)S(1)}, u32[]{:S(2)}, u32[]{:S(2)}) async-start(bf16[8,2,64,256]{3,2,1,0:T(8,128)(2,1)} %bitcast.31), calls=%async_computation.4 | async-start | bytes 1048576 | tf_op jit(solution)/shard_map/all_to_all | solution.py:341
  152.4 20.1 %collective-permute-done.10.refs_0_ = bf16[272,1024]{1,0:T(8,128)(2,1)S(1)} collective-permute-done((bf16[272,1024]{1,0:T(8,128)(2,1)}, bf16[272,1024]{1,0:T(8,128)(2,1)S(1)}, u32[]{:S(2)}, u32[]{:S(2)}) %collective-permute-start.10) | collective-permute-done | bytes 557088 | tf_op jit(solution)/shard_map/ppermute | solution.py:291
  173.4 2.7 %gate.6.refs_0_ = bf16[2,256,256]{2,1,0:T(8,128)(2,1)} custom-call(s32[3]{0:T(128)} %pad_add_fusion.1.spot_ref, bf16[272,1024]{1,0:T(8,128)(2,1)} %copy-done.4, bf16[2,1024]{1,0:T(2,128)(2,1)} %slice.23.refs_1_, f32[3,3,2048]{2,1,0:T(4,128)} %refs_2_.7, bf16[8,2,64,256]{3,2,1,0:T(8,128)(2,1)} %copy-done.1), custom_call_target="tpu_custom_call" | custom-call | tf_op jit(solution)/shard_map/gate/pallas_call | solution.py:182
  178.4 2.7 %gate.7.refs_1_ = bf16[2,256,256]{2,1,0:T(8,128)(2,1)} custom-call(s32[3]{0:T(128)} %pad_add_fusion.1.spot_ref, bf16[272,1024]{1,0:T(8,128)(2,1)} %copy-done.4, bf16[2,1024]{1,0:T(2,128)(2,1)} %slice.23.refs_1_, f32[3,3,2048]{2,1,0:T(4,128)} %refs_2_.7, bf16[8,2,64,256]{3,2,1,0:T(8,128)(2,1)} %copy-done.2), custom_call_target="tpu_custom_call" | custom-call | tf_op jit(solution)/shard_map/gate/pallas_call | solution.py:182
  182.2 2.9 %collective-permute-done.11.refs_2_ = bf16[2,256,256]{2,1,0:T(8,128)(2,1)S(1)} collective-permute-done((bf16[2,256,256]{2,1,0:T(8,128)(2,1)}, bf16[2,256,256]{2,1,0:T(8,128)(2,1)S(1)}, u32[]{:S(2)}, u32[]{:S(2)}) %collective-permute-start.11) | collective-permute-done | bytes 262176 | tf_op jit(solution)/shard_map/ppermute | solution.py:291
  185.0 4.7 %collective-permute-done.12.refs_3_ = bf16[2,256,256]{2,1,0:T(8,128)(2,1)S(1)} collective-permute-done((bf16[2,256,256]{2,1,0:T(8,128)(2,1)}, bf16[2,256,256]{2,1,0:T(8,128)(2,1)S(1)}, u32[]{:S(2)}, u32[]{:S(2)}) %collective-permute-start.12) | collective-permute-done | bytes 262176 | tf_op jit(solution)/shard_map/ppermute | solution.py:291
  190.4 7.7 %project.3 = bf16[256,2048]{1,0:T(8,128)(2,1)} custom-call(s32[8]{0:T(128)} %stack.64.spots, bf16[2,256,256]{2,1,0:T(8,128)(2,1)} %gate.6.refs_0_, bf16[2,256,256]{2,1,0:T(8,128)(2,1)} %gate.7.refs_1_, bf16[2,256,256]{2,1,0:T(8,128)(2,1)} %copy-done.8, bf16[2,256,256]{2,1,0:T(8,128)(2,1)} %copy-done.9, bf16[256,2048]{1,0:T(8,128)(2,1)} %refs_4_.3, ...), custom_call_target="tpu_custom_call" | custom-call | tf_op jit(solution)/shard_map/project/pallas_call | solution.py:259
  198.8 2.7 %gate.5.refs_1_ = bf16[2,256,256]{2,1,0:T(8,128)(2,1)} custom-call(s32[3]{0:T(128)} %pad_add_fusion.spot_ref, bf16[256,2048]{1,0:T(8,128)(2,1)} %refs_0_.3, bf16[2,2048]{1,0:T(2,128)(2,1)} %copy-done.11, f32[3,3,2048]{2,1,0:T(4,128)} %refs_2_.7, bf16[8,2,64,256]{3,2,1,0:T(8,128)(2,1)} %copy-done.2), custom_call_target="tpu_custom_call" | custom-call | tf_op jit(solution)/shard_map/gate/pallas_call | solution.py:182
  206.1 4.7 %collective-permute-done.2.refs_3_ = bf16[2,256,256]{2,1,0:T(8,128)(2,1)S(1)} collective-permute-done((bf16[2,256,256]{2,1,0:T(8,128)(2,1)}, bf16[2,256,256]{2,1,0:T(8,128)(2,1)S(1)}, u32[]{:S(2)}, u32[]{:S(2)}) %collective-permute-start.2) | collective-permute-done | bytes 262176 | tf_op jit(solution)/shard_map/ppermute | solution.py:291
  210.8 3.9 %collective-permute-done.1.refs_2_ = bf16[2,256,256]{2,1,0:T(8,128)(2,1)S(1)} collective-permute-done((bf16[2,256,256]{2,1,0:T(8,128)(2,1)}, bf16[2,256,256]{2,1,0:T(8,128)(2,1)S(1)}, u32[]{:S(2)}, u32[]{:S(2)}) %collective-permute-start.1) | collective-permute-done | bytes 262176 | tf_op jit(solution)/shard_map/ppermute | solution.py:291
  215.4 8.0 %project.2 = f32[256,2048]{1,0:T(8,128)} custom-call(s32[8]{0:T(128)} %stack.64.spots, bf16[2,256,256]{2,1,0:T(8,128)(2,1)} %gate.4.refs_0_, bf16[2,256,256]{2,1,0:T(8,128)(2,1)} %gate.5.refs_1_, bf16[2,256,256]{2,1,0:T(8,128)(2,1)} %copy-done.7, bf16[2,256,256]{2,1,0:T(8,128)(2,1)} %copy-done.6, bf16[256,2048]{1,0:T(8,128)(2,1)} %refs_4_.3, ...), custom_call_target="tpu_custom_call" | custom-call | tf_op jit(solution)/shard_map/project/pallas_call | solution.py:259
  223.4 2.8 %add_convert_fusion = bf16[256,2048]{1,0:T(8,128)(2,1)} fusion(f32[256,2048]{1,0:T(8,128)} %project.2, bf16[256,2048]{1,0:T(8,128)(2,1)S(1)} %collective-permute-done.13), kind=kLoop, calls=%fused_computation | loop fusion | flops 1572864 | bytes 4194304 | tf_op jit(solution)/shard_map/convert_element_type | solution.py:357
  (69 shorter events, 27.1 us)
Async XLA Ops:
  1.3 8.2 %copy-start = (bf16[256,2048]{1,0:T(8,128)(2,1)S(1)}, bf16[256,2048]{1,0:T(8,128)(2,1)}, u32[]{:S(2)}) copy-start(bf16[256,2048]{1,0:T(8,128)(2,1)} %refs_0_.3) | copy-start | bytes 3145732
  2.1 21.7 %all-to-all-start.1 = ((bf16[16,64,256]{2,1,0:T(8,128)(2,1)}), bf16[16,64,256]{2,1,0:T(8,128)(2,1)S(1)}, u32[]{:S(2)}, u32[]{:S(2)}) async-start(bf16[16,64,256]{2,1,0:T(8,128)(2,1)} %bitcast.17), calls=%async_computation.1 | async-start | bytes 1048576 | tf_op jit(solution)/shard_map/all_to_all | solution.py:313
  10.4 20.7 %copy-start.3 = (bf16[256,2048]{1,0:T(8,128)(2,1)S(1)}, bf16[256,2048]{1,0:T(8,128)(2,1)}, u32[]{:S(2)}) copy-start(bf16[256,2048]{1,0:T(8,128)(2,1)} %refs_4_.3) | copy-start | bytes 3145732
  10.4 3.3 %collective-permute-start = (bf16[3,2,2048]{2,1,0:T(2,128)(2,1)S(1)}, bf16[3,2,2048]{2,1,0:T(2,128)(2,1)S(1)}, u32[]{:S(2)}, u32[]{:S(2)}) collective-permute-start(bf16[3,2,2048]{2,1,0:T(2,128)(2,1)S(1)} %pad_maximum_fusion), channel_id=1, source_target_pairs={{0,2},{2,4},{4,6},{6,8},{8,10},{10,12},{12,14},{14,16},{16,18},{18... | collective-permute-start | bytes 73736 | tf_op jit(solution)/shard_map/ppermute | solution.py:20
  23.8 22.1 %all-to-all-start = ((bf16[16,64,256]{2,1,0:T(8,128)(2,1)}), bf16[16,64,256]{2,1,0:T(8,128)(2,1)S(1)}, u32[]{:S(2)}, u32[]{:S(2)}) async-start(bf16[16,64,256]{2,1,0:T(8,128)(2,1)} %bitcast.33), calls=%async_computation | async-start | bytes 1048576 | tf_op jit(solution)/shard_map/all_to_all | solution.py:336
  31.1 66.5 %collective-permute-start.6 = (bf16[256,2048]{1,0:T(8,128)(2,1)S(1)}, bf16[256,2048]{1,0:T(8,128)(2,1)}, u32[]{:S(2)}, u32[]{:S(2)}) collective-permute-start(bf16[256,2048]{1,0:T(8,128)(2,1)S(1)} %copy-done.3), channel_id=1, source_target_pairs={{16,0},{18,2},{20,4},{22,6},{24,8},{26,10},{28,12},{30,14},{0,16},... | collective-permute-start | bytes 3145736 | tf_op jit(solution)/shard_map/ppermute | solution.py:291
  36.7 37.7 %copy-start.12 = (f32[2048]{0:T(1024)S(1)}, f32[2048]{0:T(1024)}, u32[]{:S(2)}) copy-start(f32[2048]{0:T(1024)} %param.12) | copy-start | bytes 24580
  45.9 53.1 %copy-start.5 = (bf16[16,64,256]{2,1,0:T(8,128)(2,1)}, bf16[16,64,256]{2,1,0:T(8,128)(2,1)S(1)}, u32[]{:S(2)}) copy-start(bf16[16,64,256]{2,1,0:T(8,128)(2,1)S(1)} %all-to-all-done.x_ref) | copy-start | bytes 1572868
  45.9 75.2 %all-to-all-start.3 = ((bf16[16,64,256]{2,1,0:T(8,128)(2,1)}), bf16[16,64,256]{2,1,0:T(8,128)(2,1)}, u32[]{:S(2)}, u32[]{:S(2)}) async-start(bf16[16,64,256]{2,1,0:T(8,128)(2,1)} %bitcast.30), calls=%async_computation.3 | async-start | bytes 1048576 | tf_op jit(solution)/shard_map/all_to_all | solution.py:336
  72.6 72.1 %collective-permute-start.4 = (bf16[256,2048]{1,0:T(8,128)(2,1)S(1)}, bf16[256,2048]{1,0:T(8,128)(2,1)}, u32[]{:S(2)}, u32[]{:S(2)}) collective-permute-start(bf16[256,2048]{1,0:T(8,128)(2,1)S(1)} %copy-done.3), channel_id=1, source_target_pairs={{4,0},{6,2},{0,4},{2,6},{12,8},{14,10},{8,12},{10,14},{20,16},{22,... | collective-permute-start | bytes 3145736 | tf_op jit(solution)/shard_map/ppermute | solution.py:291
  97.6 47.5 %collective-permute-start.8 = (bf16[256,2048]{1,0:T(8,128)(2,1)}, bf16[256,2048]{1,0:T(8,128)(2,1)}, u32[]{:S(2)}, u32[]{:S(2)}) collective-permute-start(bf16[256,2048]{1,0:T(8,128)(2,1)} %collective-permute-done.6.refs_8_), channel_id=1, source_target_pairs={{4,0},{6,2},{0,4},{2,6},{12,8},{14,10},{8,12},{10,14},{20,16},{22,... | collective-permute-start | bytes 3145736 | tf_op jit(solution)/shard_map/ppermute | solution.py:291
  121.1 24.2 %all-to-all-start.2 = ((bf16[8,2,64,256]{3,2,1,0:T(8,128)(2,1)}), bf16[8,2,64,256]{3,2,1,0:T(8,128)(2,1)S(1)}, u32[]{:S(2)}, u32[]{:S(2)}) async-start(bf16[8,2,64,256]{3,2,1,0:T(8,128)(2,1)} %bitcast.32), calls=%async_computation.2 | async-start | bytes 1048576 | tf_op jit(solution)/shard_map/all_to_all | solution.py:341
  124.6 56.5 %collective-permute-start.3 = (bf16[256,2048]{1,0:T(8,128)(2,1)S(1)}, bf16[256,2048]{1,0:T(8,128)(2,1)}, u32[]{:S(2)}, u32[]{:S(2)}) collective-permute-start(bf16[256,2048]{1,0:T(8,128)(2,1)S(1)} %copy-done.3), channel_id=1, source_target_pairs={{2,0},{0,2},{6,4},{4,6},{10,8},{8,10},{14,12},{12,14},{18,16},{16,... | collective-permute-start | bytes 3145736 | tf_op jit(solution)/shard_map/ppermute | solution.py:291
  144.5 37.6 %collective-permute-start.7 = (bf16[256,2048]{1,0:T(8,128)(2,1)}, bf16[256,2048]{1,0:T(8,128)(2,1)}, u32[]{:S(2)}, u32[]{:S(2)}) collective-permute-start(bf16[256,2048]{1,0:T(8,128)(2,1)} %collective-permute-done.6.refs_8_), channel_id=1, source_target_pairs={{2,0},{0,2},{6,4},{4,6},{10,8},{8,10},{14,12},{12,14},{18,16},{16,... | collective-permute-start | bytes 3145736 | tf_op jit(solution)/shard_map/ppermute | solution.py:291
  144.7 37.5 %collective-permute-start.5 = (bf16[256,2048]{1,0:T(8,128)(2,1)}, bf16[256,2048]{1,0:T(8,128)(2,1)}, u32[]{:S(2)}, u32[]{:S(2)}) collective-permute-start(bf16[256,2048]{1,0:T(8,128)(2,1)} %collective-permute-done.4.refs_6_), channel_id=1, source_target_pairs={{2,0},{0,2},{6,4},{4,6},{10,8},{8,10},{14,12},{12,14},{18,16},{16,... | collective-permute-start | bytes 3145736 | tf_op jit(solution)/shard_map/ppermute | solution.py:291
  145.0 44.7 %collective-permute-start.9 = (bf16[256,2048]{1,0:T(8,128)(2,1)}, bf16[256,2048]{1,0:T(8,128)(2,1)}, u32[]{:S(2)}, u32[]{:S(2)}) collective-permute-start(bf16[256,2048]{1,0:T(8,128)(2,1)} %collective-permute-done.8.refs_10_), channel_id=1, source_target_pairs={{2,0},{0,2},{6,4},{4,6},{10,8},{8,10},{14,12},{12,14},{18,16},{16,... | collective-permute-start | bytes 3145736 | tf_op jit(solution)/shard_map/ppermute | solution.py:291
  145.2 32.3 %all-to-all-start.4 = ((bf16[8,2,64,256]{3,2,1,0:T(8,128)(2,1)}), bf16[8,2,64,256]{3,2,1,0:T(8,128)(2,1)S(1)}, u32[]{:S(2)}, u32[]{:S(2)}) async-start(bf16[8,2,64,256]{3,2,1,0:T(8,128)(2,1)} %bitcast.31), calls=%async_computation.4 | async-start | bytes 1048576 | tf_op jit(solution)/shard_map/all_to_all | solution.py:341
  150.9 25.1 %copy-start.11 = (bf16[2,2048]{1,0:T(2,128)(2,1)}, bf16[2,2048]{1,0:T(2,128)(2,1)S(1)}, u32[]{:S(2)}) copy-start(bf16[2,2048]{1,0:T(2,128)(2,1)S(1)} %slice_bitcast_fusion.refs_1_) | copy-start | bytes 24580
  151.8 20.8 %collective-permute-start.10 = (bf16[272,1024]{1,0:T(8,128)(2,1)}, bf16[272,1024]{1,0:T(8,128)(2,1)S(1)}, u32[]{:S(2)}, u32[]{:S(2)}) collective-permute-start(bf16[272,1024]{1,0:T(8,128)(2,1)} %fusion.1), channel_id=1, source_target_pairs={{8,0},{10,2},{12,4},{14,6},{0,8},{2,10},{4,12},{6,14},{24,16},{26,... | collective-permute-start | bytes 1671176 | tf_op jit(solution)/shard_map/ppermute | solution.py:291
  176.0 9.0 %collective-permute-start.11 = (bf16[2,256,256]{2,1,0:T(8,128)(2,1)}, bf16[2,256,256]{2,1,0:T(8,128)(2,1)S(1)}, u32[]{:S(2)}, u32[]{:S(2)}) collective-permute-start(bf16[2,256,256]{2,1,0:T(8,128)(2,1)} %gate.6.refs_0_), channel_id=1, source_target_pairs={{1,0},{0,1},{3,2},{2,3},{5,4},{4,5},{7,6},{6,7},{9,8},{8,9},{11,10... | collective-permute-start | bytes 786440 | tf_op jit(solution)/shard_map/ppermute | solution.py:291
  181.0 8.7 %collective-permute-start.12 = (bf16[2,256,256]{2,1,0:T(8,128)(2,1)}, bf16[2,256,256]{2,1,0:T(8,128)(2,1)S(1)}, u32[]{:S(2)}, u32[]{:S(2)}) collective-permute-start(bf16[2,256,256]{2,1,0:T(8,128)(2,1)} %gate.7.refs_1_), channel_id=1, source_target_pairs={{1,0},{0,1},{3,2},{2,3},{5,4},{4,5},{7,6},{6,7},{9,8},{8,9},{11,10... | collective-permute-start | bytes 786440 | tf_op jit(solution)/shard_map/ppermute | solution.py:291
  198.2 25.2 %collective-permute-start.13 = (bf16[256,2048]{1,0:T(8,128)(2,1)}, bf16[256,2048]{1,0:T(8,128)(2,1)S(1)}, u32[]{:S(2)}, u32[]{:S(2)}) collective-permute-start(bf16[256,2048]{1,0:T(8,128)(2,1)} %project.3), channel_id=1, source_target_pairs={{8,0},{10,2},{12,4},{14,6},{0,8},{2,10},{4,12},{6,14},{24,16},{26,... | collective-permute-start | bytes 3145736 | tf_op jit(solution)/shard_map/ppermute | solution.py:291
  201.4 9.4 %collective-permute-start.2 = (bf16[2,256,256]{2,1,0:T(8,128)(2,1)}, bf16[2,256,256]{2,1,0:T(8,128)(2,1)S(1)}, u32[]{:S(2)}, u32[]{:S(2)}) collective-permute-start(bf16[2,256,256]{2,1,0:T(8,128)(2,1)} %gate.5.refs_1_), channel_id=1, source_target_pairs={{1,0},{0,1},{3,2},{2,3},{5,4},{4,5},{7,6},{6,7},{9,8},{8,9},{11,10... | collective-permute-start | bytes 786440 | tf_op jit(solution)/shard_map/ppermute | solution.py:291
  205.6 9.1 %collective-permute-start.1 = (bf16[2,256,256]{2,1,0:T(8,128)(2,1)}, bf16[2,256,256]{2,1,0:T(8,128)(2,1)S(1)}, u32[]{:S(2)}, u32[]{:S(2)}) collective-permute-start(bf16[2,256,256]{2,1,0:T(8,128)(2,1)} %gate.4.refs_0_), channel_id=1, source_target_pairs={{1,0},{0,1},{3,2},{2,3},{5,4},{4,5},{7,6},{6,7},{9,8},{8,9},{11,10... | collective-permute-start | bytes 786440 | tf_op jit(solution)/shard_map/ppermute | solution.py:291
  (8 other events, 18.7 us)
where the time goes:
time: 227 us; the launch traced here: 226 us
  waiting for transfers between devices  75.9 us (33%)
  Pallas kernels  71 us (31%)
  starting transfers between devices  63.6 us (28%)
  local copies, waits for them, and re-layouts  9.14 us (4%)
  other arithmetic  6.37 us (3%)
    ppermute x13, waiting for transfers between devices, swap(): lax.ppermute(block, axis, [(i ^ mask, i) for i in range(lax.axis_size(axi...  59.2 us
    pallas_call x2, Pallas kernels, convolve(): pl.pallas_call(functools.partial(conv_kernel, n, tok, width, place), grid...  39.1 us
    all_to_all x2, starting transfers between devices, layer(): lax.all_to_all(turned, 'seq', split_axis=0, concat_axis=0, tiled=True)  33.9 us
    pallas_call x2, Pallas kernels, project(): pl.pallas_call(functools.partial(project_kernel, count, parts), grid_spec...  15.7 us
    ppermute x13, starting transfers between devices, swap(): lax.ppermute(block, axis, [(i ^ mask, i) for i in range(lax.axis_size(axi...  11.4 us
    pallas_call x4, Pallas kernels, gate(): pl.pallas_call(lambda spot_ref, *refs: gate_kernel(*refs), grid_spec=pltp...  10.7 us
    all_to_all x2, waiting for transfers between devices, layer(): lax.all_to_all(turned, 'seq', split_axis=0, concat_axis=0, tiled=True)  9.17 us
    all_to_all x2, starting transfers between devices, layer(): lax.all_to_all(conv, 'seq', split_axis=0, concat_axis=0, tiled=True, axis...  8.45 us
  transfers between devices with their start and end apart: 19, of which 9 were waited for; matrix products, arithmetic and copies ran while one was open for 3% of the time, Pallas kernels for 28%

commit v1 on v0

--- a/solution.py
+++ b/solution.py
@@ -10,6 +10,7 @@
 
 TAPS = 3
 PARTS = 2
+CUTS = 2
 LANES = 128
 PACK = 16
 
@@ -250,11 +251,15 @@
     out_ref[...] = total.astype(out_ref.dtype)
 
 
-def project(spots, gated, pieces, parts, kind):
+def project(spots, gated, pieces, parts, kind, columns, first):
     blocks, tokens, wide = gated[0].shape
     count = len(pieces)
-    columns = pieces[0].shape[1]
     step = min(512, columns)
+
+    def held(piece):
+        skip = first // step if piece.shape[1] > columns else 0
+        return pl.BlockSpec((wide, step), lambda j, spots: (0, j + skip))
+
     whole = pl.BlockSpec((blocks, tokens, wide), lambda j, spots: (0, 0, 0))
     return pl.pallas_call(
         functools.partial(project_kernel, count, parts),
@@ -262,7 +267,7 @@
             num_scalar_prefetch=1,
             grid=(columns // step,),
             in_specs=[whole] * len(gated)
-            + [pl.BlockSpec((wide, step), lambda j, spots: (0, j))] * count,
+            + [held(piece) for piece in pieces],
             out_specs=pl.BlockSpec((tokens, step), lambda j, spots: (0, j)),
             scratch_shapes=[pltpu.VMEM((tokens, count * wide), jnp.bfloat16)],
         ),
@@ -277,7 +282,7 @@
     sides = lax.axis_size("ch")
     here = lax.axis_index("seq")
     place = lax.axis_index("ch")
-    depth, _ = out_weight.shape
+    depth, columns = out_weight.shape
     pairs = long_filter.shape[0] // devices
     inner, outer = 4, devices // 8
     small = sides == 2 and outer == 2 and depth % 256 == 0
@@ -293,14 +298,19 @@
     last = slice(tokens - (TAPS - 1), None)
     edges = shifted(jnp.stack([query_feat[last], key_feat[last], value_feat[last]]), "seq", 1)
 
-    far = swap(out_weight, "seq", 2 * inner)
     near = swap(out_weight, "seq", 2)
     mate = swap(out_weight, "seq", 1)
-    far_near = swap(far, "seq", 2)
-    far_mate = swap(far, "seq", 1)
     near_mate = swap(near, "seq", 1)
-    far_near_mate = swap(far_near, "seq", 1)
-    pieces = [out_weight, mate, near, near_mate, far, far_mate, far_near, far_near_mate]
+    span = columns // CUTS
+    pieces = []
+    for cut in range(CUTS):
+        far = swap(out_weight[:, cut * span : (cut + 1) * span], "seq", 2 * inner)
+        far_near = swap(far, "seq", 2)
+        far_mate = swap(far, "seq", 1)
+        far_near_mate = swap(far_near, "seq", 1)
+        pieces.append(
+            [out_weight, mate, near, near_mate, far, far_mate, far_near, far_near_mate]
+        )
     masks = [0, 1, 2, 3, 2 * inner, 2 * inner + 1, 2 * inner + 2, 2 * inner + 3]
     spots = []
     for mask in masks:
@@ -351,10 +361,14 @@
     for part in range(parts):
         given_far.append(swap(given[part], "ch", 1))
         kept_far.append(swap(kept[part], "ch", 1))
-    sums = project(spots, given + given_far, pieces, parts, jnp.bfloat16)
-    taken = swap(sums, "seq", inner)
-    sums = project(spots, kept + kept_far, pieces, parts, jnp.float32)
-    return (sums + taken.astype(jnp.float32)).astype(jnp.bfloat16)
+    outs = []
+    for cut in range(CUTS):
+        sums = project(spots, given + given_far, pieces[cut], parts, jnp.bfloat16, span, cut * span)
+        outs.append(swap(sums, "seq", inner))
+    for cut in range(CUTS):
+        sums = project(spots, kept + kept_far, pieces[cut], parts, jnp.float32, span, cut * span)
+        outs[cut] = (sums + outs[cut].astype(jnp.float32)).astype(jnp.bfloat16)
+    return jnp.concatenate(outs, axis=1)
 
 
 def solution(mesh):

time: 227 us -> 225 us (level)
  starting transfers between devices: 63.6 us -> 46.4 us
  Pallas kernels: 71 us -> 76.8 us
  local copies, waits for them, and re-layouts: 9.14 us -> 14.7 us
  waiting for transfers between devices: 75.9 us -> 79 us
    all_to_all x2, starting transfers between devices: 33.9 us -> 11.5 us  [layer(): lax.all_to_all(turned, 'seq', split_axis=0, concat_axis=0, tiled=True)]
    all_to_all x2, waiting for transfers between devices: 0.01 us -> 6.51 us  [layer(): lax.all_to_all(conv, 'seq', split_axis=0, concat_axis=0, tiled=True, axis...]
    ppermute x13 -> x18, waiting for transfers between devices: 59.2 us -> 53.3 us  [swap(): lax.ppermute(block, axis, [(i ^ mask, i) for i in range(lax.axis_size(axi...]
    pallas_call x2 -> x4, Pallas kernels: 15.7 us -> 21.4 us  [project(): pl.pallas_call(functools.partial(project_kernel, count, parts), grid_spec...]
    ppermute x13 -> x18, starting transfers between devices: 11.4 us -> 16.7 us  [swap(): lax.ppermute(block, axis, [(i ^ mask, i) for i in range(lax.axis_size(axi...]
    unnamed x26 -> x32, local copies, waits for them, and re-layouts: 3 us -> 4.57 us
  transfers between devices with their start and end apart: 19 -> 24, of which waited for: 9 -> 8; matrix products, arithmetic and copies ran while one was open for 3% -> 6% of each run, Pallas kernels for 28% -> 34%
where the time goes in v1:
time: 225 us; the launch traced here: 224 us
  waiting for transfers between devices  79 us (35%)
  Pallas kernels  76.8 us (34%)
  starting transfers between devices  46.4 us (21%)
  local copies, waits for them, and re-layouts  14.7 us (7%)
  other arithmetic  7.01 us (3%)
    ppermute x18, waiting for transfers between devices, swap(): lax.ppermute(block, axis, [(i ^ mask, i) for i in range(lax.axis_size(axi...  53.3 us
    pallas_call x2, Pallas kernels, convolve(): pl.pallas_call(functools.partial(conv_kernel, n, tok, width, place), grid...  39.1 us
    pallas_call x4, Pallas kernels, project(): pl.pallas_call(functools.partial(project_kernel, count, parts), grid_spec...  21.4 us
    ppermute x18, starting transfers between devices, swap(): lax.ppermute(block, axis, [(i ^ mask, i) for i in range(lax.axis_size(axi...  16.7 us
    all_to_all x2, starting transfers between devices, layer(): lax.all_to_all(turned, 'seq', split_axis=0, concat_axis=0, tiled=True)  11.5 us
    all_to_all x2, waiting for transfers between devices, layer(): lax.all_to_all(turned, 'seq', split_axis=0, concat_axis=0, tiled=True)  11.4 us
    pallas_call x4, Pallas kernels, gate(): pl.pallas_call(lambda spot_ref, *refs: gate_kernel(*refs), grid_spec=pltp...  10.7 us
    all_to_all x2, starting transfers between devices, layer(): lax.all_to_all(conv, 'seq', split_axis=0, concat_axis=0, tiled=True, axis...  8.49 us
  transfers between devices with their start and end apart: 24, of which 8 were waited for; matrix products, arithmetic and copies ran while one was open for 6% of the time, Pallas kernels for 34%

profile of v1, /device:TPU:0, one launch (start us, length us, event | category | flops | bytes accessed | tf_op | source)
XLA Modules:
  0.0 224.1 jit_solution(8541579695992098230)
XLA Ops:
  2.1 7.4 %all-to-all-start.1 = ((bf16[16,64,256]{2,1,0:T(8,128)(2,1)}), bf16[16,64,256]{2,1,0:T(8,128)(2,1)S(1)}, u32[]{:S(2)}, u32[]{:S(2)}) async-start(bf16[16,64,256]{2,1,0:T(8,128)(2,1)} %bitcast.17), calls=%async_computation.1 | async-start | bytes 1048576 | tf_op jit(solution)/shard_map/all_to_all | solution.py:323
  14.2 2.8 %mix.3 = bf16[2,2,4,64,256]{4,3,2,1,0:T(8,128)(2,1)} custom-call(bf16[256,2048]{1,0:T(8,128)(2,1)} %key_ref.3, bf16[256,2048]{1,0:T(8,128)(2,1)} %value_ref.3, bf16[3,2,2048]{2,1,0:T(2,128)(2,1)} %copy-done.13, f32[3,3,2048]{2,1,0:T(4,128)} %refs_2_.7), custom_call_target="tpu_custom_call" | custom-call | tf_op jit(solution)/shard_map/mix/pallas_call | solution.py:160
  16.9 6.9 %all-to-all-done.1 = bf16[16,64,256]{2,1,0:T(8,128)(2,1)S(1)} async-done(((bf16[16,64,256]{2,1,0:T(8,128)(2,1)}), bf16[16,64,256]{2,1,0:T(8,128)(2,1)S(1)}, u32[]{:S(2)}, u32[]{:S(2)}) %all-to-all-start.1) | async-done | bytes 524320 | tf_op jit(solution)/shard_map/all_to_all | solution.py:323
  23.8 7.3 %all-to-all-start.3 = ((bf16[16,64,256]{2,1,0:T(8,128)(2,1)}), bf16[16,64,256]{2,1,0:T(8,128)(2,1)S(1)}, u32[]{:S(2)}, u32[]{:S(2)}) async-start(bf16[16,64,256]{2,1,0:T(8,128)(2,1)} %bitcast.33), calls=%async_computation.3 | async-start | bytes 1048576 | tf_op jit(solution)/shard_map/all_to_all | solution.py:346
  31.1 2.8 %mix.2 = bf16[2,2,4,64,256]{4,3,2,1,0:T(8,128)(2,1)} custom-call(bf16[256,2048]{1,0:T(8,128)(2,1)} %key_ref.3, bf16[256,2048]{1,0:T(8,128)(2,1)} %value_ref.3, bf16[3,2,2048]{2,1,0:T(2,128)(2,1)} %copy-done.13, f32[3,3,2048]{2,1,0:T(4,128)} %refs_2_.7), custom_call_target="tpu_custom_call" | custom-call | tf_op jit(solution)/shard_map/mix/pallas_call | solution.py:160
  33.9 11.4 %all-to-all-done.3.x_ref = bf16[16,64,256]{2,1,0:T(8,128)(2,1)S(1)} async-done(((bf16[16,64,256]{2,1,0:T(8,128)(2,1)}), bf16[16,64,256]{2,1,0:T(8,128)(2,1)S(1)}, u32[]{:S(2)}, u32[]{:S(2)}) %all-to-all-start.3) | async-done | bytes 524320 | tf_op jit(solution)/shard_map/all_to_all | solution.py:346
  46.2 4.2 %all-to-all-start = ((bf16[16,64,256]{2,1,0:T(8,128)(2,1)}), bf16[16,64,256]{2,1,0:T(8,128)(2,1)}, u32[]{:S(2)}, u32[]{:S(2)}) async-start(bf16[16,64,256]{2,1,0:T(8,128)(2,1)} %bitcast.30), calls=%async_computation | async-start | bytes 1048576 | tf_op jit(solution)/shard_map/all_to_all | solution.py:346
  58.2 19.6 %convolve.3 = bf16[16,64,256]{2,1,0:T(8,128)(2,1)} custom-call(bf16[16,64,256]{2,1,0:T(8,128)(2,1)} %copy-done.10, f32[64,32,128]{2,1,0:T(8,128)} %reshape.41.f_ref, f32[128,128]{1,0:T(8,128)} %broadcast_in_dim.8.gain_ref), custom_call_target="tpu_custom_call" | custom-call | tf_op jit(solution)/shard_map/convolve/pallas_call | solution.py:136
  77.8 4.1 %all-to-all-start.4 = ((bf16[8,2,64,256]{3,2,1,0:T(8,128)(2,1)}), bf16[8,2,64,256]{3,2,1,0:T(8,128)(2,1)}, u32[]{:S(2)}, u32[]{:S(2)}) async-start(bf16[8,2,64,256]{3,2,1,0:T(8,128)(2,1)} %bitcast.31), calls=%async_computation.4 | async-start | bytes 1048576 | tf_op jit(solution)/shard_map/all_to_all | solution.py:351
  83.0 2.8 %collective-permute-start.6 = (bf16[256,1024]{1,0:T(8,128)(2,1)}, bf16[256,1024]{1,0:T(8,128)(2,1)}, u32[]{:S(2)}, u32[]{:S(2)}) collective-permute-start(bf16[256,1024]{1,0:T(8,128)(2,1)} %get-tuple-element.5), channel_id=1, source_target_pairs={{16,0},{18,2},{20,4},{22,6},{24,8},{26,10},{28,12},{30,14},{0,16},... | collective-permute-start | bytes 1572872 | tf_op jit(solution)/shard_map/ppermute | solution.py:296
  89.0 42.6 %collective-permute-done.6.refs_8_ = bf16[256,1024]{1,0:T(8,128)(2,1)} collective-permute-done((bf16[256,1024]{1,0:T(8,128)(2,1)}, bf16[256,1024]{1,0:T(8,128)(2,1)}, u32[]{:S(2)}, u32[]{:S(2)}) %collective-permute-start.6) | collective-permute-done | bytes 524320 | tf_op jit(solution)/shard_map/ppermute | solution.py:296
  133.1 19.6 %convolve.2 = bf16[16,64,256]{2,1,0:T(8,128)(2,1)} custom-call(bf16[16,64,256]{2,1,0:T(8,128)(2,1)} %all-to-all-done.x_ref, f32[64,32,128]{2,1,0:T(8,128)} %reshape.41.f_ref, f32[128,128]{1,0:T(8,128)} %broadcast_in_dim.8.gain_ref), custom_call_target="tpu_custom_call" | custom-call | tf_op jit(solution)/shard_map/convolve/pallas_call | solution.py:136
  152.6 4.3 %all-to-all-start.2 = ((bf16[8,2,64,256]{3,2,1,0:T(8,128)(2,1)}), bf16[8,2,64,256]{3,2,1,0:T(8,128)(2,1)}, u32[]{:S(2)}, u32[]{:S(2)}) async-start(bf16[8,2,64,256]{3,2,1,0:T(8,128)(2,1)} %bitcast.32), calls=%async_computation.2 | async-start | bytes 1048576 | tf_op jit(solution)/shard_map/all_to_all | solution.py:351
  161.2 2.7 %gate.7.refs_1_ = bf16[2,256,256]{2,1,0:T(8,128)(2,1)} custom-call(s32[3]{0:T(128)} %pad_add_fusion.1.spot_ref, bf16[272,1024]{1,0:T(8,128)(2,1)} %collective-permute-done.10.refs_0_, bf16[2,1024]{1,0:T(2,128)(2,1)} %slice.31.refs_1_, f32[3,3,2048]{2,1,0:T(4,128)} %refs_2_.7, bf16[8,2,64,256]{3,2,1,0:T(8,128)(2,1)} %all-to-all-done.4.refs_3_), custom_call_target="tpu_custom_call" | custom-call | tf_op jit(solution)/shard_map/gate/pallas_call | solution.py:183
  163.9 6.5 %all-to-all-done.2.refs_3_ = bf16[8,2,64,256]{3,2,1,0:T(8,128)(2,1)} async-done(((bf16[8,2,64,256]{3,2,1,0:T(8,128)(2,1)}), bf16[8,2,64,256]{3,2,1,0:T(8,128)(2,1)}, u32[]{:S(2)}, u32[]{:S(2)}) %all-to-all-start.2) | async-done | bytes 524320 | tf_op jit(solution)/shard_map/all_to_all | solution.py:351
  170.4 2.7 %gate.6.refs_0_ = bf16[2,256,256]{2,1,0:T(8,128)(2,1)} custom-call(s32[3]{0:T(128)} %pad_add_fusion.1.spot_ref, bf16[272,1024]{1,0:T(8,128)(2,1)} %collective-permute-done.10.refs_0_, bf16[2,1024]{1,0:T(2,128)(2,1)} %slice.31.refs_1_, f32[3,3,2048]{2,1,0:T(4,128)} %refs_2_.7, bf16[8,2,64,256]{3,2,1,0:T(8,128)(2,1)} %all-to-all-done.2.refs_3_), custom_call_target="tpu_custom_call" | custom-call | tf_op jit(solution)/shard_map/gate/pallas_call | solution.py:183
  178.0 4.4 %collective-permute-done.12.refs_3_ = bf16[2,256,256]{2,1,0:T(8,128)(2,1)} collective-permute-done((bf16[2,256,256]{2,1,0:T(8,128)(2,1)S(1)}, bf16[2,256,256]{2,1,0:T(8,128)(2,1)}, u32[]{:S(2)}, u32[]{:S(2)}) %collective-permute-start.12) | collective-permute-done | bytes 262176 | tf_op jit(solution)/shard_map/ppermute | solution.py:296
  182.4 4.6 %collective-permute-done.11.refs_2_ = bf16[2,256,256]{2,1,0:T(8,128)(2,1)} collective-permute-done((bf16[2,256,256]{2,1,0:T(8,128)(2,1)}, bf16[2,256,256]{2,1,0:T(8,128)(2,1)}, u32[]{:S(2)}, u32[]{:S(2)}) %collective-permute-start.11) | collective-permute-done | bytes 262176 | tf_op jit(solution)/shard_map/ppermute | solution.py:296
  187.0 5.3 %project.5 = bf16[256,1024]{1,0:T(8,128)(2,1)} custom-call(s32[8]{0:T(128)} %stack.64.spots, bf16[2,256,256]{2,1,0:T(8,128)(2,1)} %gate.6.refs_0_, bf16[2,256,256]{2,1,0:T(8,128)(2,1)} %gate.7.refs_1_, bf16[2,256,256]{2,1,0:T(8,128)(2,1)} %collective-permute-done.11.refs_2_, bf16[2,256,256]{2,1,0:T(8,128)(2,1)} %collective-permute-done.12.refs_3_, ...), custom_call_target="tpu_custom_call" | custom-call | tf_op jit(solution)/shard_map/project/pallas_call | solution.py:264
  192.9 2.7 %gate.5.refs_1_ = bf16[2,256,256]{2,1,0:T(8,128)(2,1)} custom-call(s32[3]{0:T(128)} %pad_add_fusion.spot_ref, bf16[256,2048]{1,0:T(8,128)(2,1)} %refs_0_.3, bf16[2,2048]{1,0:T(2,128)(2,1)} %copy-done.14, f32[3,3,2048]{2,1,0:T(4,128)} %refs_2_.7, bf16[8,2,64,256]{3,2,1,0:T(8,128)(2,1)} %all-to-all-done.4.refs_3_), custom_call_target="tpu_custom_call" | custom-call | tf_op jit(solution)/shard_map/gate/pallas_call | solution.py:183
  197.1 2.7 %gate.4.refs_0_ = bf16[2,256,256]{2,1,0:T(8,128)(2,1)} custom-call(s32[3]{0:T(128)} %pad_add_fusion.spot_ref, bf16[256,2048]{1,0:T(8,128)(2,1)} %refs_0_.3, bf16[2,2048]{1,0:T(2,128)(2,1)} %copy-done.14, f32[3,3,2048]{2,1,0:T(4,128)} %refs_2_.7, bf16[8,2,64,256]{3,2,1,0:T(8,128)(2,1)} %all-to-all-done.2.refs_3_), custom_call_target="tpu_custom_call" | custom-call | tf_op jit(solution)/shard_map/gate/pallas_call | solution.py:183
  201.9 5.3 %project.7 = bf16[256,1024]{1,0:T(8,128)(2,1)} custom-call(s32[8]{0:T(128)} %stack.64.spots, bf16[2,256,256]{2,1,0:T(8,128)(2,1)} %gate.6.refs_0_, bf16[2,256,256]{2,1,0:T(8,128)(2,1)} %gate.7.refs_1_, bf16[2,256,256]{2,1,0:T(8,128)(2,1)} %collective-permute-done.11.refs_2_, bf16[2,256,256]{2,1,0:T(8,128)(2,1)} %collective-permute-done.12.refs_3_, ...), custom_call_target="tpu_custom_call" | custom-call | tf_op jit(solution)/shard_map/project/pallas_call | solution.py:264
  210.6 5.3 %project.4 = f32[256,1024]{1,0:T(8,128)} custom-call(s32[8]{0:T(128)} %stack.64.spots, bf16[2,256,256]{2,1,0:T(8,128)(2,1)} %gate.4.refs_0_, bf16[2,256,256]{2,1,0:T(8,128)(2,1)} %gate.5.refs_1_, bf16[2,256,256]{2,1,0:T(8,128)(2,1)} %copy-done.12, bf16[2,256,256]{2,1,0:T(8,128)(2,1)} %copy-done.11, bf16[256,2048]{1,0:T(8,128)(2,1)} %refs_4_.7, ...), custom_call_target="tpu_custom_call" | custom-call | tf_op jit(solution)/shard_map/project/pallas_call | solution.py:264
  215.9 5.5 %project.6 = f32[256,1024]{1,0:T(8,128)} custom-call(s32[8]{0:T(128)} %stack.64.spots, bf16[2,256,256]{2,1,0:T(8,128)(2,1)} %gate.4.refs_0_, bf16[2,256,256]{2,1,0:T(8,128)(2,1)} %gate.5.refs_1_, bf16[2,256,256]{2,1,0:T(8,128)(2,1)} %copy-done.12, bf16[2,256,256]{2,1,0:T(8,128)(2,1)} %copy-done.11, bf16[256,2048]{1,0:T(8,128)(2,1)} %refs_4_.7, ...), custom_call_target="tpu_custom_call" | custom-call | tf_op jit(solution)/shard_map/project/pallas_call | solution.py:264
  (90 shorter events, 40.4 us)
Async XLA Ops:
  2.1 21.7 %all-to-all-start.1 = ((bf16[16,64,256]{2,1,0:T(8,128)(2,1)}), bf16[16,64,256]{2,1,0:T(8,128)(2,1)S(1)}, u32[]{:S(2)}, u32[]{:S(2)}) async-start(bf16[16,64,256]{2,1,0:T(8,128)(2,1)} %bitcast.17), calls=%async_computation.1 | async-start | bytes 1048576 | tf_op jit(solution)/shard_map/all_to_all | solution.py:323
  10.4 3.1 %collective-permute-start = (bf16[3,2,2048]{2,1,0:T(2,128)(2,1)S(1)}, bf16[3,2,2048]{2,1,0:T(2,128)(2,1)S(1)}, u32[]{:S(2)}, u32[]{:S(2)}) collective-permute-start(bf16[3,2,2048]{2,1,0:T(2,128)(2,1)S(1)} %pad_maximum_fusion.1), channel_id=1, source_target_pairs={{0,2},{2,4},{4,6},{6,8},{8,10},{10,12},{12,14},{14,16},{16,18},{18... | collective-permute-start | bytes 73736 | tf_op jit(solution)/shard_map/ppermute | solution.py:21
  23.8 21.6 %all-to-all-start.3 = ((bf16[16,64,256]{2,1,0:T(8,128)(2,1)}), bf16[16,64,256]{2,1,0:T(8,128)(2,1)S(1)}, u32[]{:S(2)}, u32[]{:S(2)}) async-start(bf16[16,64,256]{2,1,0:T(8,128)(2,1)} %bitcast.33), calls=%async_computation.3 | async-start | bytes 1048576 | tf_op jit(solution)/shard_map/all_to_all | solution.py:346
  46.2 31.7 %all-to-all-start = ((bf16[16,64,256]{2,1,0:T(8,128)(2,1)}), bf16[16,64,256]{2,1,0:T(8,128)(2,1)}, u32[]{:S(2)}, u32[]{:S(2)}) async-start(bf16[16,64,256]{2,1,0:T(8,128)(2,1)} %bitcast.30), calls=%async_computation | async-start | bytes 1048576 | tf_op jit(solution)/shard_map/all_to_all | solution.py:346
  50.4 106.5 %collective-permute-start.4 = (bf16[256,2048]{1,0:T(8,128)(2,1)S(1)}, bf16[256,2048]{1,0:T(8,128)(2,1)S(1)}, u32[]{:S(2)}, u32[]{:S(2)}) collective-permute-start(bf16[256,2048]{1,0:T(8,128)(2,1)S(1)} %copy-done), channel_id=1, source_target_pairs={{4,0},{6,2},{0,4},{2,6},{12,8},{14,10},{8,12},{10,14},{20,16},{22,... | collective-permute-start | bytes 3145736 | tf_op jit(solution)/shard_map/ppermute | solution.py:296
  77.8 74.8 %all-to-all-start.4 = ((bf16[8,2,64,256]{3,2,1,0:T(8,128)(2,1)}), bf16[8,2,64,256]{3,2,1,0:T(8,128)(2,1)}, u32[]{:S(2)}, u32[]{:S(2)}) async-start(bf16[8,2,64,256]{3,2,1,0:T(8,128)(2,1)} %bitcast.31), calls=%async_computation.4 | async-start | bytes 1048576 | tf_op jit(solution)/shard_map/all_to_all | solution.py:351
  83.0 48.5 %collective-permute-start.6 = (bf16[256,1024]{1,0:T(8,128)(2,1)}, bf16[256,1024]{1,0:T(8,128)(2,1)}, u32[]{:S(2)}, u32[]{:S(2)}) collective-permute-start(bf16[256,1024]{1,0:T(8,128)(2,1)} %get-tuple-element.5), channel_id=1, source_target_pairs={{16,0},{18,2},{20,4},{22,6},{24,8},{26,10},{28,12},{30,14},{0,16},... | collective-permute-start | bytes 1572872 | tf_op jit(solution)/shard_map/ppermute | solution.py:296
  87.4 70.2 %collective-permute-start.10 = (bf16[272,1024]{1,0:T(8,128)(2,1)}, bf16[272,1024]{1,0:T(8,128)(2,1)}, u32[]{:S(2)}, u32[]{:S(2)}) collective-permute-start(bf16[272,1024]{1,0:T(8,128)(2,1)} %fusion.1), channel_id=1, source_target_pairs={{8,0},{10,2},{12,4},{14,6},{0,8},{2,10},{4,12},{6,14},{24,16},{26,... | collective-permute-start | bytes 1671176 | tf_op jit(solution)/shard_map/ppermute | solution.py:296
  88.9 68.4 %collective-permute-start.14 = (bf16[256,1024]{1,0:T(8,128)(2,1)}, bf16[256,1024]{1,0:T(8,128)(2,1)}, u32[]{:S(2)}, u32[]{:S(2)}) collective-permute-start(bf16[256,1024]{1,0:T(8,128)(2,1)} %get-tuple-element.6), channel_id=1, source_target_pairs={{16,0},{18,2},{20,4},{22,6},{24,8},{26,10},{28,12},{30,14},{0,16},... | collective-permute-start | bytes 1572872 | tf_op jit(solution)/shard_map/ppermute | solution.py:296
  89.0 85.6 %collective-permute-start.3 = (bf16[256,2048]{1,0:T(8,128)(2,1)S(1)}, bf16[256,2048]{1,0:T(8,128)(2,1)S(1)}, u32[]{:S(2)}, u32[]{:S(2)}) collective-permute-start(bf16[256,2048]{1,0:T(8,128)(2,1)S(1)} %copy-done), channel_id=1, source_target_pairs={{2,0},{0,2},{6,4},{4,6},{10,8},{8,10},{14,12},{12,14},{18,16},{16,... | collective-permute-start | bytes 3145736 | tf_op jit(solution)/shard_map/ppermute | solution.py:296
  131.6 27.7 %collective-permute-start.8 = (bf16[256,1024]{1,0:T(8,128)(2,1)}, bf16[256,1024]{1,0:T(8,128)(2,1)}, u32[]{:S(2)}, u32[]{:S(2)}) collective-permute-start(bf16[256,1024]{1,0:T(8,128)(2,1)} %collective-permute-done.6.refs_8_), channel_id=1, source_target_pairs={{4,0},{6,2},{0,4},{2,6},{12,8},{14,10},{8,12},{10,14},{20,16},{22,... | collective-permute-start | bytes 1572872 | tf_op jit(solution)/shard_map/ppermute | solution.py:296
  152.6 17.8 %all-to-all-start.2 = ((bf16[8,2,64,256]{3,2,1,0:T(8,128)(2,1)}), bf16[8,2,64,256]{3,2,1,0:T(8,128)(2,1)}, u32[]{:S(2)}, u32[]{:S(2)}) async-start(bf16[8,2,64,256]{3,2,1,0:T(8,128)(2,1)} %bitcast.32), calls=%async_computation.2 | async-start | bytes 1048576 | tf_op jit(solution)/shard_map/all_to_all | solution.py:351
  157.0 21.0 %collective-permute-start.5 = (bf16[256,2048]{1,0:T(8,128)(2,1)S(1)}, bf16[256,2048]{1,0:T(8,128)(2,1)}, u32[]{:S(2)}, u32[]{:S(2)}) collective-permute-start(bf16[256,2048]{1,0:T(8,128)(2,1)S(1)} %collective-permute-done.4.refs_6_), channel_id=1, source_target_pairs={{2,0},{0,2},{6,4},{4,6},{10,8},{8,10},{14,12},{12,14},{18,16},{16,... | collective-permute-start | bytes 3145736 | tf_op jit(solution)/shard_map/ppermute | solution.py:296
  157.2 15.8 %collective-permute-start.7 = (bf16[256,1024]{1,0:T(8,128)(2,1)}, bf16[256,1024]{1,0:T(8,128)(2,1)}, u32[]{:S(2)}, u32[]{:S(2)}) collective-permute-start(bf16[256,1024]{1,0:T(8,128)(2,1)} %collective-permute-done.6.refs_8_), channel_id=1, source_target_pairs={{2,0},{0,2},{6,4},{4,6},{10,8},{8,10},{14,12},{12,14},{18,16},{16,... | collective-permute-start | bytes 1572872 | tf_op jit(solution)/shard_map/ppermute | solution.py:296
  157.6 19.3 %collective-permute-start.16 = (bf16[256,1024]{1,0:T(8,128)(2,1)}, bf16[256,1024]{1,0:T(8,128)(2,1)}, u32[]{:S(2)}, u32[]{:S(2)}) collective-permute-start(bf16[256,1024]{1,0:T(8,128)(2,1)} %collective-permute-done.14.refs_8_), channel_id=1, source_target_pairs={{4,0},{6,2},{0,4},{2,6},{12,8},{14,10},{8,12},{10,14},{20,16},{22,... | collective-permute-start | bytes 1572872 | tf_op jit(solution)/shard_map/ppermute | solution.py:296
  159.3 17.5 %collective-permute-start.9 = (bf16[256,1024]{1,0:T(8,128)(2,1)}, bf16[256,1024]{1,0:T(8,128)(2,1)}, u32[]{:S(2)}, u32[]{:S(2)}) collective-permute-start(bf16[256,1024]{1,0:T(8,128)(2,1)} %collective-permute-done.8.refs_10_), channel_id=1, source_target_pairs={{2,0},{0,2},{6,4},{4,6},{10,8},{8,10},{14,12},{12,14},{18,16},{16,... | collective-permute-start | bytes 1572872 | tf_op jit(solution)/shard_map/ppermute | solution.py:296
  173.1 9.3 %collective-permute-start.12 = (bf16[2,256,256]{2,1,0:T(8,128)(2,1)S(1)}, bf16[2,256,256]{2,1,0:T(8,128)(2,1)}, u32[]{:S(2)}, u32[]{:S(2)}) collective-permute-start(bf16[2,256,256]{2,1,0:T(8,128)(2,1)S(1)} %copy-done.6), channel_id=1, source_target_pairs={{1,0},{0,1},{3,2},{2,3},{5,4},{4,5},{7,6},{6,7},{9,8},{8,9},{11,10... | collective-permute-start | bytes 786440 | tf_op jit(solution)/shard_map/ppermute | solution.py:296
  174.6 12.4 %collective-permute-start.11 = (bf16[2,256,256]{2,1,0:T(8,128)(2,1)}, bf16[2,256,256]{2,1,0:T(8,128)(2,1)}, u32[]{:S(2)}, u32[]{:S(2)}) collective-permute-start(bf16[2,256,256]{2,1,0:T(8,128)(2,1)} %gate.6.refs_0_), channel_id=1, source_target_pairs={{1,0},{0,1},{3,2},{2,3},{5,4},{4,5},{7,6},{6,7},{9,8},{8,9},{11,10... | collective-permute-start | bytes 786440 | tf_op jit(solution)/shard_map/ppermute | solution.py:296
  176.8 23.4 %collective-permute-start.15 = (bf16[256,1024]{1,0:T(8,128)(2,1)}, bf16[256,1024]{1,0:T(8,128)(2,1)S(1)}, u32[]{:S(2)}, u32[]{:S(2)}) collective-permute-start(bf16[256,1024]{1,0:T(8,128)(2,1)} %collective-permute-done.14.refs_8_), channel_id=1, source_target_pairs={{2,0},{0,2},{6,4},{4,6},{10,8},{8,10},{14,12},{12,14},{18,16},{16,... | collective-permute-start | bytes 1572872 | tf_op jit(solution)/shard_map/ppermute | solution.py:296
  176.8 23.4 %collective-permute-start.17 = (bf16[256,1024]{1,0:T(8,128)(2,1)}, bf16[256,1024]{1,0:T(8,128)(2,1)S(1)}, u32[]{:S(2)}, u32[]{:S(2)}) collective-permute-start(bf16[256,1024]{1,0:T(8,128)(2,1)} %collective-permute-done.16.refs_10_), channel_id=1, source_target_pairs={{2,0},{0,2},{6,4},{4,6},{10,8},{8,10},{14,12},{12,14},{18,16},{16,... | collective-permute-start | bytes 1572872 | tf_op jit(solution)/shard_map/ppermute | solution.py:296
  192.3 29.2 %collective-permute-start.13 = (bf16[256,1024]{1,0:T(8,128)(2,1)}, bf16[256,1024]{1,0:T(8,128)(2,1)}, u32[]{:S(2)}, u32[]{:S(2)}) collective-permute-start(bf16[256,1024]{1,0:T(8,128)(2,1)} %project.5), channel_id=1, source_target_pairs={{8,0},{10,2},{12,4},{14,6},{0,8},{2,10},{4,12},{6,14},{24,16},{26,... | collective-permute-start | bytes 1572872 | tf_op jit(solution)/shard_map/ppermute | solution.py:296
  195.6 13.6 %collective-permute-start.2 = (bf16[2,256,256]{2,1,0:T(8,128)(2,1)}, bf16[2,256,256]{2,1,0:T(8,128)(2,1)S(1)}, u32[]{:S(2)}, u32[]{:S(2)}) collective-permute-start(bf16[2,256,256]{2,1,0:T(8,128)(2,1)} %gate.5.refs_1_), channel_id=1, source_target_pairs={{1,0},{0,1},{3,2},{2,3},{5,4},{4,5},{7,6},{6,7},{9,8},{8,9},{11,10... | collective-permute-start | bytes 786440 | tf_op jit(solution)/shard_map/ppermute | solution.py:296
  199.8 9.4 %collective-permute-start.1 = (bf16[2,256,256]{2,1,0:T(8,128)(2,1)}, bf16[2,256,256]{2,1,0:T(8,128)(2,1)S(1)}, u32[]{:S(2)}, u32[]{:S(2)}) collective-permute-start(bf16[2,256,256]{2,1,0:T(8,128)(2,1)} %gate.4.refs_0_), channel_id=1, source_target_pairs={{1,0},{0,1},{3,2},{2,3},{5,4},{4,5},{7,6},{6,7},{9,8},{8,9},{11,10... | collective-permute-start | bytes 786440 | tf_op jit(solution)/shard_map/ppermute | solution.py:296
  207.2 15.6 %collective-permute-start.18 = (bf16[256,1024]{1,0:T(8,128)(2,1)}, bf16[256,1024]{1,0:T(8,128)(2,1)S(1)}, u32[]{:S(2)}, u32[]{:S(2)}) collective-permute-start(bf16[256,1024]{1,0:T(8,128)(2,1)} %project.7), channel_id=1, source_target_pairs={{8,0},{10,2},{12,4},{14,6},{0,8},{2,10},{4,12},{6,14},{24,16},{26,... | collective-permute-start | bytes 1572872 | tf_op jit(solution)/shard_map/ppermute | solution.py:296
  (16 other events, 168.4 us)

commit v2 on v1

--- a/solution.py
+++ b/solution.py
@@ -34,26 +34,39 @@
     return total
 
 
-def mix_kernel(key_ref, value_ref, edge_ref, short_ref, turned_ref):
+def mix_kernel(key_ref, value_ref, edge_ref, short_ref, *refs):
+    sent_ref = refs[-1]
+    outer, _, inner, _, tokens = sent_ref.shape
     edge = edge_ref[...].astype(jnp.float32)
     mixed = featurized(key_ref[...], edge[1], short_ref[1]) * featurized(
         value_ref[...], edge[2], short_ref[2]
     )
-    turned_ref[...] = mixed.T.astype(jnp.bfloat16).reshape(turned_ref.shape)
-
-
-def gate_kernel(query_ref, edge_ref, short_ref, conv_ref, gated_ref):
-    edge = edge_ref[...].astype(jnp.float32)
-    query_short = featurized(query_ref[...], edge, short_ref[0])
-    summed = conv_ref[...].astype(jnp.float32).reshape(query_short.shape[1], query_short.shape[0]).T
-    gated_ref[0] = (query_short * summed).astype(jnp.bfloat16)
-
-
-def conv_kernel(n, tok, width, place, x_ref, f_ref, gain_ref, y_ref, xi, xs, ys):
+    each = mixed.shape[1] // (outer * inner)
+    turned = mixed.T.astype(jnp.bfloat16)
+    sent_ref[:, 0, :, 0:each, :] = turned.reshape(outer, inner, each, tokens)
+    for taps_ref in refs[:-1]:
+        taps = taps_ref[...].astype(jnp.bfloat16)
+        sent_ref[:, 0, :, each:, :] = taps.reshape(outer, inner, each // 2, tokens)
+
+
+def gate_kernel(count, *refs):
+    short_ref = refs[0]
+    for own in range(count):
+        query_ref, edge_ref, conv_ref = refs[1 + 3 * own : 4 + 3 * own]
+        gated_ref = refs[1 + 3 * count + own]
+        edge = edge_ref[...].astype(jnp.float32)
+        query_short = featurized(query_ref[...], edge, short_ref[0])
+        wide, tokens = query_short.shape[1], query_short.shape[0]
+        summed = conv_ref[...].astype(jnp.float32).reshape(wide, tokens).T
+        gated_ref[0] = (query_short * summed).astype(jnp.bfloat16)
+
+
+def conv_kernel(n, tok, width, place, x_ref, f_ref, gain_ref, y_ref, xi, xs, ys, fs):
     halves = tok // LANES
     groups = LANES // PACK
     for e in range(halves):
         for i in range(n):
+            fs[:, i * halves + e, :] = f_ref[i, :, e * LANES : (e + 1) * LANES].astype(jnp.float32)
             xi[e, i * width : (i + 1) * width, :] = x_ref[
                 i, :, e * LANES : (e + 1) * LANES
             ].astype(jnp.float32)
@@ -67,7 +80,7 @@
         def skewed(m):
             if m == 0:
                 return jnp.zeros((PACK, LANES), jnp.float32)
-            row = f_ref[p, m - 1 : m, :]
+            row = fs[p, m - 1 : m, :]
             return pltpu.roll(
                 jnp.broadcast_to(row, (PACK, LANES)), 0, 1, stride=1, stride_axis=0
             )
@@ -128,8 +141,8 @@
             y_ref[place(i), :, e * LANES : (e + 1) * LANES] = total.astype(jnp.bfloat16)
 
 
-def convolve(x, f, gain, part, place):
-    n, chans, tok = x.shape
+def convolve(x, f, skip, chans, gain, part, place):
+    n, _, tok = x.shape
     width = min(16, chans)
     halves = tok // LANES
     assert halves == 2
@@ -138,64 +151,68 @@
         grid=(chans // width,),
         in_specs=[
             pl.BlockSpec((n, width, tok), lambda g: (0, g, 0)),
-            pl.BlockSpec(
-                (width // 2, n * halves, LANES), lambda g: (g + part * (chans // width), 0, 0)
-            ),
+            pl.BlockSpec((n, width // 2, tok), lambda g: (0, g + skip // (width // 2), 0)),
             pl.BlockSpec((width, LANES), lambda g: (g + part * (chans // width), 0)),
         ],
         out_specs=pl.BlockSpec((n, width, tok), lambda g: (0, g, 0)),
-        out_shape=jax.ShapeDtypeStruct(x.shape, jnp.bfloat16),
+        out_shape=jax.ShapeDtypeStruct((n, chans, tok), jnp.bfloat16),
         scratch_shapes=[
             pltpu.VMEM((halves, n * width, LANES), jnp.float32),
             pltpu.VMEM((halves, width, 2 * n, LANES), jnp.float32),
             pltpu.VMEM((halves, n * width, LANES), jnp.float32),
+            pltpu.VMEM((width // 2, n * halves, LANES), jnp.float32),
         ],
         name="convolve",
     )(x, f, gain)
 
 
-def mix(key_feat, value_feat, edges, short_filter, part, parts, outer, inner):
+def mix(key_feat, value_feat, edges, short_filter, part, parts, outer, inner, *taps):
     tokens, channels = key_feat.shape
     wide = channels // (2 * parts)
+    each = wide // (outer * inner)
+    each += each // 2 * len(taps)
+    rows = pl.BlockSpec((tokens, wide), lambda g: (0, g * parts + part))
     return pl.pallas_call(
         mix_kernel,
         grid=(2,),
         in_specs=[
-            pl.BlockSpec((tokens, wide), lambda g: (0, g * parts + part)),
-            pl.BlockSpec((tokens, wide), lambda g: (0, g * parts + part)),
+            rows,
+            rows,
             pl.BlockSpec((3, TAPS - 1, wide), lambda g: (0, 0, g * parts + part)),
             pl.BlockSpec((3, TAPS, wide), lambda g: (0, 0, g * parts + part)),
-        ],
-        out_specs=pl.BlockSpec(
-            (outer, 1, inner, wide // (outer * inner), tokens), lambda g: (0, g, 0, 0, 0)
-        ),
-        out_shape=jax.ShapeDtypeStruct(
-            (outer, 2, inner, wide // (outer * inner), tokens), jnp.bfloat16
-        ),
+        ]
+        + [pl.BlockSpec((wide // 2, tokens), lambda g: (g * parts + part, 0))] * len(taps),
+        out_specs=pl.BlockSpec((outer, 1, inner, each, tokens), lambda g: (0, g, 0, 0, 0)),
+        out_shape=jax.ShapeDtypeStruct((outer, 2, inner, each, tokens), jnp.bfloat16),
         name="mix",
-    )(key_feat, value_feat, edges, short_filter)
-
-
-def gate(spot, query, edge, short_filter, conv, first, wide):
-    sources, _, each, tokens = conv.shape
-    blocks = sources * each // wide
+    )(key_feat, value_feat, edges, short_filter, *taps)
+
+
+def gate(spot, short_filter, conv, first, wide, *sources):
+    count = len(sources)
+    origins, _, each, tokens = conv.shape
+    blocks = origins * each // wide
     per = wide // each
+    specs, operands = [], []
+    for own, (query, edge) in enumerate(sources):
+        column = lambda g, spot, own=own: (0, spot[1 + 2 * own] + g + first * blocks)
+        specs += [
+            pl.BlockSpec((tokens, wide), column),
+            pl.BlockSpec((TAPS - 1, wide), column),
+            pl.BlockSpec((per, 1, each, tokens), lambda g, spot, own=own: (g, spot[2 + 2 * own], 0, 0)),
+        ]
+        operands += [query, edge, conv]
     return pl.pallas_call(
-        lambda spot_ref, *refs: gate_kernel(*refs),
+        lambda spot_ref, *refs: gate_kernel(count, *refs),
         grid_spec=pltpu.PrefetchScalarGridSpec(
             num_scalar_prefetch=1,
             grid=(blocks,),
-            in_specs=[
-                pl.BlockSpec((tokens, wide), lambda g, spot: (0, spot[0] + g + first * blocks)),
-                pl.BlockSpec((TAPS - 1, wide), lambda g, spot: (0, spot[0] + g + first * blocks)),
-                pl.BlockSpec((3, TAPS, wide), lambda g, spot: (0, 0, spot[1] + g + first * blocks)),
-                pl.BlockSpec((per, 1, each, tokens), lambda g, spot: (g, spot[2], 0, 0)),
-            ],
-            out_specs=pl.BlockSpec((1, tokens, wide), lambda g, spot: (g, 0, 0)),
+            in_specs=[pl.BlockSpec((3, TAPS, wide), lambda g, spot: (0, 0, spot[0] + g + first * blocks))] + specs,
+            out_specs=[pl.BlockSpec((1, tokens, wide), lambda g, spot: (g, 0, 0))] * count,
         ),
-        out_shape=jax.ShapeDtypeStruct((blocks, tokens, wide), jnp.bfloat16),
+        out_shape=[jax.ShapeDtypeStruct((blocks, tokens, wide), jnp.bfloat16)] * count,
         name="gate",
-    )(spot, query, edge, short_filter, conv)
+    )(spot, short_filter, *operands)
 
 
 def plain(query_feat, key_feat, value_feat, short_filter, long_filter, direct_gain, out_weight):
@@ -208,33 +225,31 @@
     edges = shifted(jnp.stack([query_feat[last], key_feat[last], value_feat[last]]), "seq", 1)
     sent = long_filter.astype(jnp.bfloat16).reshape(devices, pairs, tokens)
     taps = lax.all_to_all(sent, "seq", split_axis=0, concat_axis=0, tiled=True)
-    taps = taps.astype(jnp.float32).transpose(1, 0, 2)
-    taps = taps.reshape(pairs, devices * tokens // LANES, LANES)
     gain = lax.dynamic_index_in_dim(direct_gain.reshape(devices, 2 * pairs, 1), here, 0, False)
     gain = jnp.broadcast_to(gain, (2 * pairs, LANES))
     turned = mix(key_feat, value_feat, edges, short_filter, 0, 1, 1, devices // 2)
     turned = turned.reshape(devices, 2 * pairs, tokens)
     spread = lax.all_to_all(turned, "seq", split_axis=0, concat_axis=0, tiled=True)
-    conv = convolve(spread, taps, gain, 0, lambda i: i)
+    conv = convolve(spread, taps, 0, 2 * pairs, gain, 0, lambda i: i)
     conv = lax.all_to_all(conv, "seq", split_axis=0, concat_axis=0, tiled=True)
     wide = min(256, channels)
     spot = jnp.zeros((3,), jnp.int32)
-    gated = gate(spot, query_feat, edges[0], short_filter, conv[:, None], 0, wide)
+    (gated,) = gate(spot, short_filter, conv[:, None], 0, wide, (query_feat, edges[0]))
     gated = gated.transpose(1, 0, 2).reshape(tokens, channels)
     features = lax.all_gather(gated, "ch", axis=1, tiled=True)
     return jnp.dot(features, weights, preferred_element_type=jnp.float32).astype(jnp.bfloat16)
 
 
-def project_kernel(count, parts, spots, *refs):
-    gated, pieces = refs[: 2 * parts], refs[2 * parts : 2 * parts + count]
-    out_ref, rows = refs[2 * parts + count :]
+def project_kernel(count, per, spots, *refs):
+    gated, pieces = refs[:per], refs[per : per + count]
+    out_ref, rows = refs[per + count :]
     blocks, _, wide = gated[0].shape
 
     @pl.when(pl.program_id(0) == 0)
     def _():
         for piece in range(count):
             spot = spots[piece]
-            for source in range(2 * parts):
+            for source in range(per):
 
                 @pl.when(spot // blocks == source)
                 def _():
@@ -251,10 +266,10 @@
     out_ref[...] = total.astype(out_ref.dtype)
 
 
-def project(spots, gated, pieces, parts, kind, columns, first):
+def project(spots, gated, pieces, kind, columns, first):
     blocks, tokens, wide = gated[0].shape
     count = len(pieces)
-    step = min(512, columns)
+    step = min(256, columns)
 
     def held(piece):
         skip = first // step if piece.shape[1] > columns else 0
@@ -262,12 +277,11 @@
 
     whole = pl.BlockSpec((blocks, tokens, wide), lambda j, spots: (0, 0, 0))
     return pl.pallas_call(
-        functools.partial(project_kernel, count, parts),
+        functools.partial(project_kernel, count, len(gated)),
         grid_spec=pltpu.PrefetchScalarGridSpec(
             num_scalar_prefetch=1,
             grid=(columns // step,),
-            in_specs=[whole] * len(gated)
-            + [held(piece) for piece in pieces],
+            in_specs=[whole] * len(gated) + [held(piece) for piece in pieces],
             out_specs=pl.BlockSpec((tokens, step), lambda j, spots: (0, j)),
             scratch_shapes=[pltpu.VMEM((tokens, count * wide), jnp.bfloat16)],
         ),
@@ -318,11 +332,6 @@
         spots.append((owner // (2 * inner) != place) * inner + owner % inner)
     spots = jnp.stack(spots).astype(jnp.int32)
 
-    sent = long_filter.astype(jnp.bfloat16)
-    sent = sent.reshape(2, parts, outer, inner, pairs // parts, tokens).transpose(2, 0, 3, 1, 4, 5)
-    taps = lax.all_to_all(sent.reshape(devices, pairs, tokens), "seq", split_axis=0, concat_axis=0, tiled=True)
-    taps = taps.astype(jnp.float32).transpose(1, 0, 2)
-    taps = taps.reshape(pairs, devices * tokens // LANES, LANES)
     gain = direct_gain.reshape(2, parts, devices // 2, 2 * pairs // parts)
     gain = lax.dynamic_index_in_dim(lax.dynamic_index_in_dim(gain, twin, 0, False), rank, 1, False)
     gain = jnp.broadcast_to(gain.reshape(2 * pairs, 1), (2 * pairs, LANES))
@@ -341,33 +350,38 @@
     groups = [[o * 2 * inner + t * inner + i for o in range(outer) for i in range(inner)] for t in range(2)]
     spreads, backs = [], []
     for part in range(parts):
-        turned = mix(key_feat, value_feat, edges, short_filter, part, parts, outer, inner)
-        turned = turned.reshape(devices, 2 * pairs // parts, tokens)
+        turned = mix(
+            key_feat, value_feat, edges, short_filter, part, parts, outer, inner, long_filter
+        )
+        turned = turned.reshape(devices, 3 * pairs // parts, tokens)
         spreads.append(lax.all_to_all(turned, "seq", split_axis=0, concat_axis=0, tiled=True))
     for part in range(parts):
-        conv = convolve(spreads[part], taps, gain, part, at)
+        chans = 2 * pairs // parts
+        conv = convolve(spreads[part], spreads[part], chans, chans, gain, part, at)
         conv = conv.reshape(devices // 2, 2, 2 * pairs // parts, tokens)
         backs.append(
             lax.all_to_all(conv, "seq", split_axis=0, concat_axis=0, tiled=True, axis_index_groups=groups)
         )
     blocks = half // wide
-    kept_spot = jnp.stack([twin * blocks, twin * blocks, twin]).astype(jnp.int32)
-    given_spot = jnp.stack([0 * twin, twin * blocks, 1 - twin]).astype(jnp.int32)
+    spot = jnp.stack([twin * blocks, twin * blocks, twin, 0 * twin, 1 - twin]).astype(jnp.int32)
     kept, given = [], []
     for part in range(parts):
-        given.append(gate(given_spot, asked, asked_edge, short_filter, backs[part], part, wide))
-        kept.append(gate(kept_spot, query_feat, edges[0], short_filter, backs[part], part, wide))
-    given_far, kept_far = [], []
+        own, passed = gate(
+            spot, short_filter, backs[part], part, wide, (query_feat, edges[0]), (asked, asked_edge)
+        )
+        kept.append(own)
+        given.append(passed)
+    kept_far, given_far = [], []
     for part in range(parts):
         given_far.append(swap(given[part], "ch", 1))
         kept_far.append(swap(kept[part], "ch", 1))
-    outs = []
+    sums, taken = [], []
     for cut in range(CUTS):
-        sums = project(spots, given + given_far, pieces[cut], parts, jnp.bfloat16, span, cut * span)
-        outs.append(swap(sums, "seq", inner))
+        passed = project(spots, given + given_far, pieces[cut], jnp.bfloat16, span, cut * span)
+        taken.append(swap(passed, "seq", inner))
     for cut in range(CUTS):
-        sums = project(spots, kept + kept_far, pieces[cut], parts, jnp.float32, span, cut * span)
-        outs[cut] = (sums + outs[cut].astype(jnp.float32)).astype(jnp.bfloat16)
+        sums.append(project(spots, kept + kept_far, pieces[cut], jnp.float32, span, cut * span))
+    outs = [(a + b.astype(jnp.float32)).astype(jnp.bfloat16) for a, b in zip(sums, taken)]
     return jnp.concatenate(outs, axis=1)
 
 

time: 225 us -> 214 us (0.951)
  starting transfers between devices: 46.4 us -> 42.3 us
  local copies, waits for them, and re-layouts: 14.7 us -> 11.6 us
  other arithmetic: 7.01 us -> 4.4 us
    all_to_all x1 -> x0, starting transfers between devices: 7.39 us -> none  [layer(): lax.all_to_all(sent.reshape(devices, pairs, tokens), 'seq', split_axis=0,...]
    all_to_all x1 -> x0, waiting for transfers between devices: 6.86 us -> none  [layer(): lax.all_to_all(sent.reshape(devices, pairs, tokens), 'seq', split_axis=0,...]
    reshape x3 -> x0, local copies, waits for them, and re-layouts: 4.7 us -> none  [the longest x2 3.86 us: layer(): taps = taps.reshape(pairs, devices * tokens // LANES, LANES)]
    all_to_all x2, waiting for transfers between devices: 11.4 us -> 15.7 us  [layer(): lax.all_to_all(turned, 'seq', split_axis=0, concat_axis=0, tiled=True)]
    all_to_all x2, starting transfers between devices: 11.5 us -> 14.7 us  [layer(): lax.all_to_all(turned, 'seq', split_axis=0, concat_axis=0, tiled=True)]
    unnamed x32 -> x34, local copies, waits for them, and re-layouts: 4.57 us -> 4.8 us
    pallas_call x10 -> x8, Pallas kernels: 37.6 us -> 37.6 us  [the longest x4 25.4 us: project(): pl.pallas_call(functools.partial(project_kernel, count, len(gated)), grid...]
  transfers between devices with their start and end apart: 24 -> 23, of which waited for: 8 -> 8; matrix products, arithmetic and copies ran while one was open for 6% -> 3% of each run, Pallas kernels for 34% -> 35%
where the time goes in v2:
time: 214 us; the launch traced here: 213 us
  Pallas kernels  77.3 us (36%)
  waiting for transfers between devices  77.2 us (36%)
  starting transfers between devices  42.3 us (20%)
  local copies, waits for them, and re-layouts  11.6 us (5%)
  other arithmetic  4.4 us (2%)
    ppermute x18, waiting for transfers between devices, swap(): lax.ppermute(block, axis, [(i ^ mask, i) for i in range(lax.axis_size(axi...  54.7 us
    pallas_call x2, Pallas kernels, convolve(): pl.pallas_call(functools.partial(conv_kernel, n, tok, width, place), grid...  39.6 us
    pallas_call x4, Pallas kernels, project(): pl.pallas_call(functools.partial(project_kernel, count, len(gated)), grid...  25.4 us
    ppermute x18, starting transfers between devices, swap(): lax.ppermute(block, axis, [(i ^ mask, i) for i in range(lax.axis_size(axi...  16.8 us
    all_to_all x2, waiting for transfers between devices, layer(): lax.all_to_all(turned, 'seq', split_axis=0, concat_axis=0, tiled=True)  15.7 us
    all_to_all x2, starting transfers between devices, layer(): lax.all_to_all(turned, 'seq', split_axis=0, concat_axis=0, tiled=True)  14.7 us
    all_to_all x2, starting transfers between devices, layer(): lax.all_to_all(conv, 'seq', split_axis=0, concat_axis=0, tiled=True, axis...  8.47 us
    pallas_call x2, Pallas kernels, gate(): pl.pallas_call(lambda spot_ref, *refs: gate_kernel(count, *refs), grid_sp...  6.22 us
  transfers between devices with their start and end apart: 23, of which 8 were waited for; matrix products, arithmetic and copies ran while one was open for 3% of the time, Pallas kernels for 35%

profile of v2, /device:TPU:0, one launch (start us, length us, event | category | flops | bytes accessed | tf_op | source)
XLA Modules:
  0.0 213.0 jit_solution(5708744901713478858)
XLA Ops:
  1.6 2.4 %collective-permute-start = (bf16[3,2,2048]{2,1,0:T(2,128)(2,1)S(1)}, bf16[3,2,2048]{2,1,0:T(2,128)(2,1)S(1)}, u32[]{:S(2)}, u32[]{:S(2)}) collective-permute-start(bf16[3,2,2048]{2,1,0:T(2,128)(2,1)S(1)} %pad_maximum_fusion.1), channel_id=1, source_target_pairs={{0,2},{2,4},{4,6},{6,8},{8,10},{10,12},{12,14},{14,16},{16,18},{18... | collective-permute-start | bytes 73736 | tf_op jit(solution)/shard_map/ppermute | solution.py:21
  5.5 3.0 %mix.3 = bf16[2,2,4,96,256]{4,3,2,1,0:T(8,128)(2,1)} custom-call(bf16[256,2048]{1,0:T(8,128)(2,1)} %key_ref.3, bf16[256,2048]{1,0:T(8,128)(2,1)} %value_ref.3, bf16[3,2,2048]{2,1,0:T(2,128)(2,1)} %copy-done.14, f32[3,3,2048]{2,1,0:T(4,128)} %refs_0_.7, f32[1024,256]{1,0:T(8,128)} %refs_0_.6), custom_call_target="tpu_custom_call" | custom-call | tf_op jit(solution)/shard_map/mix/pallas_call | solution.py:175
  8.4 9.3 %all-to-all-start.2 = ((bf16[16,96,256]{2,1,0:T(8,128)(2,1)}), bf16[16,96,256]{2,1,0:T(8,128)(2,1)S(1)}, u32[]{:S(2)}, u32[]{:S(2)}) async-start(bf16[16,96,256]{2,1,0:T(8,128)(2,1)} %bitcast.24), calls=%async_computation.2 | async-start | bytes 1572864 | tf_op jit(solution)/shard_map/all_to_all | solution.py:357
  17.7 3.0 %mix.2 = bf16[2,2,4,96,256]{4,3,2,1,0:T(8,128)(2,1)} custom-call(bf16[256,2048]{1,0:T(8,128)(2,1)} %key_ref.3, bf16[256,2048]{1,0:T(8,128)(2,1)} %value_ref.3, bf16[3,2,2048]{2,1,0:T(2,128)(2,1)} %copy-done.14, f32[3,3,2048]{2,1,0:T(4,128)} %refs_0_.7, f32[1024,256]{1,0:T(8,128)} %refs_0_.6), custom_call_target="tpu_custom_call" | custom-call | tf_op jit(solution)/shard_map/mix/pallas_call | solution.py:175
  20.7 15.7 %all-to-all-done.2.x_ref.f_ref = bf16[16,96,256]{2,1,0:T(8,128)(2,1)S(1)} async-done(((bf16[16,96,256]{2,1,0:T(8,128)(2,1)}), bf16[16,96,256]{2,1,0:T(8,128)(2,1)S(1)}, u32[]{:S(2)}, u32[]{:S(2)}) %all-to-all-start.2) | async-done | bytes 786464 | tf_op jit(solution)/shard_map/all_to_all | solution.py:357
  37.3 5.4 %all-to-all-start = ((bf16[16,96,256]{2,1,0:T(8,128)(2,1)}), bf16[16,96,256]{2,1,0:T(8,128)(2,1)S(1)}, u32[]{:S(2)}, u32[]{:S(2)}) async-start(bf16[16,96,256]{2,1,0:T(8,128)(2,1)} %bitcast.23), calls=%async_computation | async-start | bytes 1572864 | tf_op jit(solution)/shard_map/all_to_all | solution.py:357
  42.7 2.0 collective-permute-start.5
  45.6 19.8 %convolve.3 = bf16[16,64,256]{2,1,0:T(8,128)(2,1)} custom-call(bf16[16,96,256]{2,1,0:T(8,128)(2,1)} %copy-done.5, bf16[16,96,256]{2,1,0:T(8,128)(2,1)} %copy-done.5, f32[128,128]{1,0:T(8,128)} %broadcast_in_dim.8.gain_ref), custom_call_target="tpu_custom_call" | custom-call | tf_op jit(solution)/shard_map/convolve/pallas_call | solution.py:149
  66.3 4.1 %all-to-all-start.3 = ((bf16[8,2,64,256]{3,2,1,0:T(8,128)(2,1)}), bf16[8,2,64,256]{3,2,1,0:T(8,128)(2,1)}, u32[]{:S(2)}, u32[]{:S(2)}) async-start(bf16[8,2,64,256]{3,2,1,0:T(8,128)(2,1)} %bitcast.25), calls=%async_computation.3 | async-start | bytes 1048576 | tf_op jit(solution)/shard_map/all_to_all | solution.py:363
  71.5 2.8 %collective-permute-start.7 = (bf16[256,1024]{1,0:T(8,128)(2,1)}, bf16[256,1024]{1,0:T(8,128)(2,1)}, u32[]{:S(2)}, u32[]{:S(2)}) collective-permute-start(bf16[256,1024]{1,0:T(8,128)(2,1)} %get-tuple-element.13), channel_id=1, source_target_pairs={{16,0},{18,2},{20,4},{22,6},{24,8},{26,10},{28,12},{30,14},{0,16},... | collective-permute-start | bytes 1572872 | tf_op jit(solution)/shard_map/ppermute | solution.py:310
  77.5 42.5 %collective-permute-done.7.refs_8_ = bf16[256,1024]{1,0:T(8,128)(2,1)} collective-permute-done((bf16[256,1024]{1,0:T(8,128)(2,1)}, bf16[256,1024]{1,0:T(8,128)(2,1)}, u32[]{:S(2)}, u32[]{:S(2)}) %collective-permute-start.7) | collective-permute-done | bytes 524320 | tf_op jit(solution)/shard_map/ppermute | solution.py:310
  121.5 19.8 %convolve.2 = bf16[16,64,256]{2,1,0:T(8,128)(2,1)} custom-call(bf16[16,96,256]{2,1,0:T(8,128)(2,1)} %copy-done.4, bf16[16,96,256]{2,1,0:T(8,128)(2,1)} %copy-done.4, f32[128,128]{1,0:T(8,128)} %broadcast_in_dim.8.gain_ref), custom_call_target="tpu_custom_call" | custom-call | tf_op jit(solution)/shard_map/convolve/pallas_call | solution.py:149
  141.4 4.3 %all-to-all-start.1 = ((bf16[8,2,64,256]{3,2,1,0:T(8,128)(2,1)}), bf16[8,2,64,256]{3,2,1,0:T(8,128)(2,1)}, u32[]{:S(2)}, u32[]{:S(2)}) async-start(bf16[8,2,64,256]{3,2,1,0:T(8,128)(2,1)} %bitcast.26), calls=%async_computation.1 | async-start | bytes 1048576 | tf_op jit(solution)/shard_map/all_to_all | solution.py:363
  146.3 1.7 collective-permute-start.16
  149.9 3.1 %gate.3 = (bf16[2,256,256]{2,1,0:T(8,128)(2,1)}, bf16[2,256,256]{2,1,0:T(8,128)(2,1)}) custom-call(s32[5]{0:T(128)} %stack.64.spot_ref, f32[3,3,2048]{2,1,0:T(4,128)} %refs_0_.7, bf16[256,2048]{1,0:T(8,128)(2,1)} %refs_1_.3, bf16[2,2048]{1,0:T(2,128)(2,1)} %copy-done.15, bf16[8,2,64,256]{3,2,1,0:T(8,128)(2,1)} %all-to-all-done.3.refs_3_.refs_6_, ...), custom_call_target="tpu_custom_call" | custom-call | tf_op jit(solution)/shard_map/gate/pallas_call | solution.py:205
  153.0 6.0 %all-to-all-done.1.refs_3_.refs_6_ = bf16[8,2,64,256]{3,2,1,0:T(8,128)(2,1)} async-done(((bf16[8,2,64,256]{3,2,1,0:T(8,128)(2,1)}), bf16[8,2,64,256]{3,2,1,0:T(8,128)(2,1)}, u32[]{:S(2)}, u32[]{:S(2)}) %all-to-all-start.1) | async-done | bytes 524320 | tf_op jit(solution)/shard_map/all_to_all | solution.py:363
  159.1 3.1 %gate.2 = (bf16[2,256,256]{2,1,0:T(8,128)(2,1)}, bf16[2,256,256]{2,1,0:T(8,128)(2,1)}) custom-call(s32[5]{0:T(128)} %stack.64.spot_ref, f32[3,3,2048]{2,1,0:T(4,128)} %refs_0_.7, bf16[256,2048]{1,0:T(8,128)(2,1)} %refs_1_.3, bf16[2,2048]{1,0:T(2,128)(2,1)} %copy-done.15, bf16[8,2,64,256]{3,2,1,0:T(8,128)(2,1)} %all-to-all-done.1.refs_3_.refs_6_, ...), custom_call_target="tpu_custom_call" | custom-call | tf_op jit(solution)/shard_map/gate/pallas_call | solution.py:205
  166.7 5.0 %collective-permute-done.12.refs_3_ = bf16[2,256,256]{2,1,0:T(8,128)(2,1)} collective-permute-done((bf16[2,256,256]{2,1,0:T(8,128)(2,1)}, bf16[2,256,256]{2,1,0:T(8,128)(2,1)}, u32[]{:S(2)}, u32[]{:S(2)}) %collective-permute-start.12) | collective-permute-done | bytes 262176 | tf_op jit(solution)/shard_map/ppermute | solution.py:310
  171.8 4.7 %collective-permute-done.11.refs_2_ = bf16[2,256,256]{2,1,0:T(8,128)(2,1)} collective-permute-done((bf16[2,256,256]{2,1,0:T(8,128)(2,1)}, bf16[2,256,256]{2,1,0:T(8,128)(2,1)}, u32[]{:S(2)}, u32[]{:S(2)}) %collective-permute-start.11) | collective-permute-done | bytes 262176 | tf_op jit(solution)/shard_map/ppermute | solution.py:310
  176.4 6.3 %project.5 = bf16[256,1024]{1,0:T(8,128)(2,1)} custom-call(s32[8]{0:T(128)} %stack.60.spots, bf16[2,256,256]{2,1,0:T(8,128)(2,1)} %get-tuple-element.11.refs_0_, bf16[2,256,256]{2,1,0:T(8,128)(2,1)} %get-tuple-element.12.refs_1_, bf16[2,256,256]{2,1,0:T(8,128)(2,1)} %collective-permute-done.11.refs_2_, bf16[2,256,256]{2,1,0:T(8,128)(2,1)} %collective-permute-done.12.refs_3_, ...), custom_call_target="tpu_custom_call" | custom-call | tf_op jit(solution)/shard_map/project/pallas_call | solution.py:279
  186.4 6.2 %project.7 = bf16[256,1024]{1,0:T(8,128)(2,1)} custom-call(s32[8]{0:T(128)} %stack.60.spots, bf16[2,256,256]{2,1,0:T(8,128)(2,1)} %get-tuple-element.11.refs_0_, bf16[2,256,256]{2,1,0:T(8,128)(2,1)} %get-tuple-element.12.refs_1_, bf16[2,256,256]{2,1,0:T(8,128)(2,1)} %collective-permute-done.11.refs_2_, bf16[2,256,256]{2,1,0:T(8,128)(2,1)} %collective-permute-done.12.refs_3_, ...), custom_call_target="tpu_custom_call" | custom-call | tf_op jit(solution)/shard_map/project/pallas_call | solution.py:279
  192.7 1.9 collective-permute-start.18
  196.5 6.4 %project.4 = f32[256,1024]{1,0:T(8,128)} custom-call(s32[8]{0:T(128)} %stack.60.spots, bf16[2,256,256]{2,1,0:T(8,128)(2,1)} %get-tuple-element.9.refs_0_, bf16[2,256,256]{2,1,0:T(8,128)(2,1)} %get-tuple-element.10.refs_1_, bf16[2,256,256]{2,1,0:T(8,128)(2,1)} %copy-done.13, bf16[2,256,256]{2,1,0:T(8,128)(2,1)} %copy-done.12, bf16[256,2048]{1,0:T(8,128)(2,1)} %refs_4_.7, ...), custom_call_target="tpu_custom_call" | custom-call | tf_op jit(solution)/shard_map/project/pallas_call | solution.py:279
  202.9 6.5 %project.6 = f32[256,1024]{1,0:T(8,128)} custom-call(s32[8]{0:T(128)} %stack.60.spots, bf16[2,256,256]{2,1,0:T(8,128)(2,1)} %get-tuple-element.9.refs_0_, bf16[2,256,256]{2,1,0:T(8,128)(2,1)} %get-tuple-element.10.refs_1_, bf16[2,256,256]{2,1,0:T(8,128)(2,1)} %copy-done.13, bf16[2,256,256]{2,1,0:T(8,128)(2,1)} %copy-done.12, bf16[256,2048]{1,0:T(8,128)(2,1)} %refs_4_.7, ...), custom_call_target="tpu_custom_call" | custom-call | tf_op jit(solution)/shard_map/project/pallas_call | solution.py:279
  (82 shorter events, 27.6 us)
Async XLA Ops:
  1.6 3.2 %collective-permute-start = (bf16[3,2,2048]{2,1,0:T(2,128)(2,1)S(1)}, bf16[3,2,2048]{2,1,0:T(2,128)(2,1)S(1)}, u32[]{:S(2)}, u32[]{:S(2)}) collective-permute-start(bf16[3,2,2048]{2,1,0:T(2,128)(2,1)S(1)} %pad_maximum_fusion.1), channel_id=1, source_target_pairs={{0,2},{2,4},{4,6},{6,8},{8,10},{10,12},{12,14},{14,16},{16,18},{18... | collective-permute-start | bytes 73736 | tf_op jit(solution)/shard_map/ppermute | solution.py:21
  8.4 28.0 %all-to-all-start.2 = ((bf16[16,96,256]{2,1,0:T(8,128)(2,1)}), bf16[16,96,256]{2,1,0:T(8,128)(2,1)S(1)}, u32[]{:S(2)}, u32[]{:S(2)}) async-start(bf16[16,96,256]{2,1,0:T(8,128)(2,1)} %bitcast.24), calls=%async_computation.2 | async-start | bytes 1572864 | tf_op jit(solution)/shard_map/all_to_all | solution.py:357
  37.3 28.1 %all-to-all-start = ((bf16[16,96,256]{2,1,0:T(8,128)(2,1)}), bf16[16,96,256]{2,1,0:T(8,128)(2,1)S(1)}, u32[]{:S(2)}, u32[]{:S(2)}) async-start(bf16[16,96,256]{2,1,0:T(8,128)(2,1)} %bitcast.23), calls=%async_computation | async-start | bytes 1572864 | tf_op jit(solution)/shard_map/all_to_all | solution.py:357
  42.7 103.0 %collective-permute-start.5 = (bf16[256,2048]{1,0:T(8,128)(2,1)S(1)}, bf16[256,2048]{1,0:T(8,128)(2,1)S(1)}, u32[]{:S(2)}, u32[]{:S(2)}) collective-permute-start(bf16[256,2048]{1,0:T(8,128)(2,1)S(1)} %copy-done), channel_id=1, source_target_pairs={{4,0},{6,2},{0,4},{2,6},{12,8},{14,10},{8,12},{10,14},{20,16},{22,... | collective-permute-start | bytes 3145736 | tf_op jit(solution)/shard_map/ppermute | solution.py:310
  66.3 75.1 %all-to-all-start.3 = ((bf16[8,2,64,256]{3,2,1,0:T(8,128)(2,1)}), bf16[8,2,64,256]{3,2,1,0:T(8,128)(2,1)}, u32[]{:S(2)}, u32[]{:S(2)}) async-start(bf16[8,2,64,256]{3,2,1,0:T(8,128)(2,1)} %bitcast.25), calls=%async_computation.3 | async-start | bytes 1048576 | tf_op jit(solution)/shard_map/all_to_all | solution.py:363
  71.5 48.5 %collective-permute-start.7 = (bf16[256,1024]{1,0:T(8,128)(2,1)}, bf16[256,1024]{1,0:T(8,128)(2,1)}, u32[]{:S(2)}, u32[]{:S(2)}) collective-permute-start(bf16[256,1024]{1,0:T(8,128)(2,1)} %get-tuple-element.13), channel_id=1, source_target_pairs={{16,0},{18,2},{20,4},{22,6},{24,8},{26,10},{28,12},{30,14},{0,16},... | collective-permute-start | bytes 1572872 | tf_op jit(solution)/shard_map/ppermute | solution.py:310
  75.0 66.3 %copy-start.15 = (bf16[2,2048]{1,0:T(2,128)(2,1)}, bf16[2,2048]{1,0:T(2,128)(2,1)S(1)}, u32[]{:S(2)}) copy-start(bf16[2,2048]{1,0:T(2,128)(2,1)S(1)} %slice_bitcast_fusion.refs_2_) | copy-start | bytes 24580
  75.9 70.4 %collective-permute-start.1 = (bf16[272,1024]{1,0:T(8,128)(2,1)}, bf16[272,1024]{1,0:T(8,128)(2,1)}, u32[]{:S(2)}, u32[]{:S(2)}) collective-permute-start(bf16[272,1024]{1,0:T(8,128)(2,1)} %fusion.1), channel_id=1, source_target_pairs={{8,0},{10,2},{12,4},{14,6},{0,8},{2,10},{4,12},{6,14},{24,16},{26,... | collective-permute-start | bytes 1671176 | tf_op jit(solution)/shard_map/ppermute | solution.py:310
  77.4 68.6 %collective-permute-start.14 = (bf16[256,1024]{1,0:T(8,128)(2,1)}, bf16[256,1024]{1,0:T(8,128)(2,1)}, u32[]{:S(2)}, u32[]{:S(2)}) collective-permute-start(bf16[256,1024]{1,0:T(8,128)(2,1)} %get-tuple-element.14), channel_id=1, source_target_pairs={{16,0},{18,2},{20,4},{22,6},{24,8},{26,10},{28,12},{30,14},{0,16},... | collective-permute-start | bytes 1572872 | tf_op jit(solution)/shard_map/ppermute | solution.py:310
  77.5 86.3 %collective-permute-start.4 = (bf16[256,2048]{1,0:T(8,128)(2,1)S(1)}, bf16[256,2048]{1,0:T(8,128)(2,1)S(1)}, u32[]{:S(2)}, u32[]{:S(2)}) collective-permute-start(bf16[256,2048]{1,0:T(8,128)(2,1)S(1)} %copy-done), channel_id=1, source_target_pairs={{2,0},{0,2},{6,4},{4,6},{10,8},{8,10},{14,12},{12,14},{18,16},{16,... | collective-permute-start | bytes 3145736 | tf_op jit(solution)/shard_map/ppermute | solution.py:310
  120.0 28.0 %collective-permute-start.9 = (bf16[256,1024]{1,0:T(8,128)(2,1)}, bf16[256,1024]{1,0:T(8,128)(2,1)}, u32[]{:S(2)}, u32[]{:S(2)}) collective-permute-start(bf16[256,1024]{1,0:T(8,128)(2,1)} %collective-permute-done.7.refs_8_), channel_id=1, source_target_pairs={{4,0},{6,2},{0,4},{2,6},{12,8},{14,10},{8,12},{10,14},{20,16},{22,... | collective-permute-start | bytes 1572872 | tf_op jit(solution)/shard_map/ppermute | solution.py:310
  141.4 17.7 %all-to-all-start.1 = ((bf16[8,2,64,256]{3,2,1,0:T(8,128)(2,1)}), bf16[8,2,64,256]{3,2,1,0:T(8,128)(2,1)}, u32[]{:S(2)}, u32[]{:S(2)}) async-start(bf16[8,2,64,256]{3,2,1,0:T(8,128)(2,1)} %bitcast.26), calls=%async_computation.1 | async-start | bytes 1048576 | tf_op jit(solution)/shard_map/all_to_all | solution.py:363
  145.7 21.0 %collective-permute-start.6 = (bf16[256,2048]{1,0:T(8,128)(2,1)S(1)}, bf16[256,2048]{1,0:T(8,128)(2,1)}, u32[]{:S(2)}, u32[]{:S(2)}) collective-permute-start(bf16[256,2048]{1,0:T(8,128)(2,1)S(1)} %collective-permute-done.5.refs_6_), channel_id=1, source_target_pairs={{2,0},{0,2},{6,4},{4,6},{10,8},{8,10},{14,12},{12,14},{18,16},{16,... | collective-permute-start | bytes 3145736 | tf_op jit(solution)/shard_map/ppermute | solution.py:310
  146.0 16.2 %collective-permute-start.8 = (bf16[256,1024]{1,0:T(8,128)(2,1)}, bf16[256,1024]{1,0:T(8,128)(2,1)}, u32[]{:S(2)}, u32[]{:S(2)}) collective-permute-start(bf16[256,1024]{1,0:T(8,128)(2,1)} %collective-permute-done.7.refs_8_), channel_id=1, source_target_pairs={{2,0},{0,2},{6,4},{4,6},{10,8},{8,10},{14,12},{12,14},{18,16},{16,... | collective-permute-start | bytes 1572872 | tf_op jit(solution)/shard_map/ppermute | solution.py:310
  146.3 19.3 %collective-permute-start.16 = (bf16[256,1024]{1,0:T(8,128)(2,1)}, bf16[256,1024]{1,0:T(8,128)(2,1)}, u32[]{:S(2)}, u32[]{:S(2)}) collective-permute-start(bf16[256,1024]{1,0:T(8,128)(2,1)} %collective-permute-done.14.refs_8_), channel_id=1, source_target_pairs={{4,0},{6,2},{0,4},{2,6},{12,8},{14,10},{8,12},{10,14},{20,16},{22,... | collective-permute-start | bytes 1572872 | tf_op jit(solution)/shard_map/ppermute | solution.py:310
  148.0 17.5 %collective-permute-start.10 = (bf16[256,1024]{1,0:T(8,128)(2,1)}, bf16[256,1024]{1,0:T(8,128)(2,1)}, u32[]{:S(2)}, u32[]{:S(2)}) collective-permute-start(bf16[256,1024]{1,0:T(8,128)(2,1)} %collective-permute-done.9.refs_10_), channel_id=1, source_target_pairs={{2,0},{0,2},{6,4},{4,6},{10,8},{8,10},{14,12},{12,14},{18,16},{16,... | collective-permute-start | bytes 1572872 | tf_op jit(solution)/shard_map/ppermute | solution.py:310
  162.2 9.6 %collective-permute-start.12 = (bf16[2,256,256]{2,1,0:T(8,128)(2,1)}, bf16[2,256,256]{2,1,0:T(8,128)(2,1)}, u32[]{:S(2)}, u32[]{:S(2)}) collective-permute-start(bf16[2,256,256]{2,1,0:T(8,128)(2,1)} %get-tuple-element.12.refs_1_), channel_id=1, source_target_pairs={{1,0},{0,1},{3,2},{2,3},{5,4},{4,5},{7,6},{6,7},{9,8},{8,9},{11,10... | collective-permute-start | bytes 786440 | tf_op jit(solution)/shard_map/ppermute | solution.py:310
  163.8 12.6 %collective-permute-start.11 = (bf16[2,256,256]{2,1,0:T(8,128)(2,1)}, bf16[2,256,256]{2,1,0:T(8,128)(2,1)}, u32[]{:S(2)}, u32[]{:S(2)}) collective-permute-start(bf16[2,256,256]{2,1,0:T(8,128)(2,1)} %get-tuple-element.11.refs_0_), channel_id=1, source_target_pairs={{1,0},{0,1},{3,2},{2,3},{5,4},{4,5},{7,6},{6,7},{9,8},{8,9},{11,10... | collective-permute-start | bytes 786440 | tf_op jit(solution)/shard_map/ppermute | solution.py:310
  165.6 19.3 %collective-permute-start.15 = (bf16[256,1024]{1,0:T(8,128)(2,1)}, bf16[256,1024]{1,0:T(8,128)(2,1)S(1)}, u32[]{:S(2)}, u32[]{:S(2)}) collective-permute-start(bf16[256,1024]{1,0:T(8,128)(2,1)} %collective-permute-done.14.refs_8_), channel_id=1, source_target_pairs={{2,0},{0,2},{6,4},{4,6},{10,8},{8,10},{14,12},{12,14},{18,16},{16,... | collective-permute-start | bytes 1572872 | tf_op jit(solution)/shard_map/ppermute | solution.py:310
  165.6 19.3 %collective-permute-start.17 = (bf16[256,1024]{1,0:T(8,128)(2,1)}, bf16[256,1024]{1,0:T(8,128)(2,1)S(1)}, u32[]{:S(2)}, u32[]{:S(2)}) collective-permute-start(bf16[256,1024]{1,0:T(8,128)(2,1)} %collective-permute-done.16.refs_10_), channel_id=1, source_target_pairs={{2,0},{0,2},{6,4},{4,6},{10,8},{8,10},{14,12},{12,14},{18,16},{16,... | collective-permute-start | bytes 1572872 | tf_op jit(solution)/shard_map/ppermute | solution.py:310
  182.7 26.7 %collective-permute-start.13 = (bf16[256,1024]{1,0:T(8,128)(2,1)}, bf16[256,1024]{1,0:T(8,128)(2,1)}, u32[]{:S(2)}, u32[]{:S(2)}) collective-permute-start(bf16[256,1024]{1,0:T(8,128)(2,1)} %project.5), channel_id=1, source_target_pairs={{8,0},{10,2},{12,4},{14,6},{0,8},{2,10},{4,12},{6,14},{24,16},{26,... | collective-permute-start | bytes 1572872 | tf_op jit(solution)/shard_map/ppermute | solution.py:310
  182.7 11.9 %collective-permute-start.3 = (bf16[2,256,256]{2,1,0:T(8,128)(2,1)S(1)}, bf16[2,256,256]{2,1,0:T(8,128)(2,1)S(1)}, u32[]{:S(2)}, u32[]{:S(2)}) collective-permute-start(bf16[2,256,256]{2,1,0:T(8,128)(2,1)S(1)} %copy-done.10), channel_id=1, source_target_pairs={{1,0},{0,1},{3,2},{2,3},{5,4},{4,5},{7,6},{6,7},{9,8},{8,9},{11,10... | collective-permute-start | bytes 786440 | tf_op jit(solution)/shard_map/ppermute | solution.py:310
  184.3 11.5 %collective-permute-start.2 = (bf16[2,256,256]{2,1,0:T(8,128)(2,1)S(1)}, bf16[2,256,256]{2,1,0:T(8,128)(2,1)S(1)}, u32[]{:S(2)}, u32[]{:S(2)}) collective-permute-start(bf16[2,256,256]{2,1,0:T(8,128)(2,1)S(1)} %copy-done.11), channel_id=1, source_target_pairs={{1,0},{0,1},{3,2},{2,3},{5,4},{4,5},{7,6},{6,7},{9,8},{8,9},{11,10... | collective-permute-start | bytes 786440 | tf_op jit(solution)/shard_map/ppermute | solution.py:310
  192.7 18.0 %collective-permute-start.18 = (bf16[256,1024]{1,0:T(8,128)(2,1)}, bf16[256,1024]{1,0:T(8,128)(2,1)}, u32[]{:S(2)}, u32[]{:S(2)}) collective-permute-start(bf16[256,1024]{1,0:T(8,128)(2,1)} %project.7), channel_id=1, source_target_pairs={{8,0},{10,2},{12,4},{14,6},{0,8},{2,10},{4,12},{6,14},{24,16},{26,... | collective-permute-start | bytes 1572872 | tf_op jit(solution)/shard_map/ppermute | solution.py:310
  (16 other events, 117.9 us)

commit v3 on v2

--- a/solution.py
+++ b/solution.py
@@ -240,35 +240,51 @@
     return jnp.dot(features, weights, preferred_element_type=jnp.float32).astype(jnp.bfloat16)
 
 
-def project_kernel(count, per, spots, *refs):
-    gated, pieces = refs[:per], refs[per : per + count]
-    out_ref, rows = refs[per + count :]
-    blocks, _, wide = gated[0].shape
-
-    @pl.when(pl.program_id(0) == 0)
+def project_kernel(per, spots, *refs):
+    gated, pieces = refs[: 2 * per], refs[2 * per : -3]
+    more, pieces = pieces[: len(pieces) % 8], pieces[len(pieces) % 8 :]
+    kept_ref, given_ref, rows = refs[-3:]
+    blocks, tokens, wide = gated[0].shape
+    count = len(pieces) // 2
+
+    def run(first):
+        @pl.when(pl.program_id(0) == 0)
+        def _():
+            for piece in range(count):
+                spot = spots[first + piece]
+                columns = slice(piece * wide, (piece + 1) * wide)
+                for source in range(per):
+
+                    @pl.when(spot // blocks == source)
+                    def _():
+                        rows[:tokens, columns] = gated[source][lax.rem(spot, blocks)]
+                        rows[tokens:, columns] = gated[per + source][lax.rem(spot, blocks)]
+
+        total = None
+        for piece in range(count):
+            out = jnp.dot(
+                rows[:, piece * wide : (piece + 1) * wide],
+                pieces[first + piece][...],
+                preferred_element_type=jnp.float32,
+            )
+            total = out if total is None else total + out
+        kept, given = total[:tokens], total[tokens:]
+        if more:
+            kept, given = kept + more[0][...], given + more[1][...]
+        kept_ref[...] = kept
+        given_ref[...] = given.astype(given_ref.dtype)
+
+    @pl.when(spots[2 * count] == 0)
     def _():
-        for piece in range(count):
-            spot = spots[piece]
-            for source in range(per):
-
-                @pl.when(spot // blocks == source)
-                def _():
-                    rows[:, piece * wide : (piece + 1) * wide] = gated[source][lax.rem(spot, blocks)]
-
-    total = None
-    for piece in range(count):
-        out = jnp.dot(
-            rows[:, piece * wide : (piece + 1) * wide],
-            pieces[piece][...],
-            preferred_element_type=jnp.float32,
-        )
-        total = out if total is None else total + out
-    out_ref[...] = total.astype(out_ref.dtype)
-
-
-def project(spots, gated, pieces, kind, columns, first):
-    blocks, tokens, wide = gated[0].shape
-    count = len(pieces)
+        run(0)
+
+    @pl.when(spots[2 * count] != 0)
+    def _():
+        run(count)
+
+
+def project(spots, kept, given, pieces, columns, first, more=()):
+    blocks, tokens, wide = kept[0].shape
     step = min(256, columns)
 
     def held(piece):
@@ -276,18 +292,22 @@
         return pl.BlockSpec((wide, step), lambda j, spots: (0, j + skip))
 
     whole = pl.BlockSpec((blocks, tokens, wide), lambda j, spots: (0, 0, 0))
+    out = pl.BlockSpec((tokens, step), lambda j, spots: (0, j))
     return pl.pallas_call(
-        functools.partial(project_kernel, count, len(gated)),
+        functools.partial(project_kernel, len(kept)),
         grid_spec=pltpu.PrefetchScalarGridSpec(
             num_scalar_prefetch=1,
             grid=(columns // step,),
-            in_specs=[whole] * len(gated) + [held(piece) for piece in pieces],
-            out_specs=pl.BlockSpec((tokens, step), lambda j, spots: (0, j)),
-            scratch_shapes=[pltpu.VMEM((tokens, count * wide), jnp.bfloat16)],
+            in_specs=[whole] * (2 * len(kept)) + [out] * len(more) + [held(piece) for piece in pieces],
+            out_specs=[out, out],
+            scratch_shapes=[pltpu.VMEM((2 * tokens, len(pieces) // 2 * wide), jnp.bfloat16)],
         ),
-        out_shape=jax.ShapeDtypeStruct((tokens, columns), kind),
+        out_shape=[
+            jax.ShapeDtypeStruct((tokens, columns), jnp.float32),
+            jax.ShapeDtypeStruct((tokens, columns), jnp.bfloat16 if more else jnp.float32),
+        ],
         name="project",
-    )(spots, *gated, *pieces)
+    )(spots, *kept, *given, *more, *pieces)
 
 
 def layer(query_feat, key_feat, value_feat, short_filter, long_filter, direct_gain, out_weight):
@@ -318,7 +338,11 @@
     span = columns // CUTS
     pieces = []
     for cut in range(CUTS):
-        far = swap(out_weight[:, cut * span : (cut + 1) * span], "seq", 2 * inner)
+        share = span // 2 if cut == 0 else span
+        far = []
+        for start in range(cut * span, (cut + 1) * span, share):
+            far.append(swap(out_weight[:, start : start + share], "seq", 2 * inner))
+        far = far[0] if len(far) == 1 else jnp.concatenate(far, axis=1)
         far_near = swap(far, "seq", 2)
         far_mate = swap(far, "seq", 1)
         far_near_mate = swap(far_near, "seq", 1)
@@ -326,11 +350,10 @@
             [out_weight, mate, near, near_mate, far, far_mate, far_near, far_near_mate]
         )
     masks = [0, 1, 2, 3, 2 * inner, 2 * inner + 1, 2 * inner + 2, 2 * inner + 3]
-    spots = []
-    for mask in masks:
-        owner = here ^ mask
-        spots.append((owner // (2 * inner) != place) * inner + owner % inner)
-    spots = jnp.stack(spots).astype(jnp.int32)
+    spots = [(here ^ mask) % inner for mask in masks]
+    apart = (here // (2 * inner) + place) % 2
+    near_spots = jnp.stack(spots + [apart]).astype(jnp.int32)
+    far_spots = jnp.stack(spots + [1 - apart]).astype(jnp.int32)
 
     gain = direct_gain.reshape(2, parts, devices // 2, 2 * pairs // parts)
     gain = lax.dynamic_index_in_dim(lax.dynamic_index_in_dim(gain, twin, 0, False), rank, 1, False)
@@ -376,11 +399,15 @@
         given_far.append(swap(given[part], "ch", 1))
         kept_far.append(swap(kept[part], "ch", 1))
     sums, taken = [], []
+    halves = []
     for cut in range(CUTS):
-        passed = project(spots, given + given_far, pieces[cut], jnp.bfloat16, span, cut * span)
+        halves.append(project(near_spots, kept, given, pieces[cut], span, cut * span))
+    for cut in range(CUTS):
+        held, passed = project(
+            far_spots, kept_far, given_far, pieces[cut], span, cut * span, halves[cut]
+        )
+        sums.append(held)
         taken.append(swap(passed, "seq", inner))
-    for cut in range(CUTS):
-        sums.append(project(spots, kept + kept_far, pieces[cut], jnp.float32, span, cut * span))
     outs = [(a + b.astype(jnp.float32)).astype(jnp.bfloat16) for a, b in zip(sums, taken)]
     return jnp.concatenate(outs, axis=1)
 

time: 214 us -> 205 us (0.958)
  waiting for transfers between devices: 77.2 us -> 50 us
  starting transfers between devices: 42.3 us -> 57.6 us
    ppermute x18 -> x19, waiting for transfers between devices: 54.7 us -> 28 us  [swap(): lax.ppermute(block, axis, [(i ^ mask, i) for i in range(lax.axis_size(axi...]
    all_to_all x2, starting transfers between devices: 8.47 us -> 21.3 us  [layer(): lax.all_to_all(conv, 'seq', split_axis=0, concat_axis=0, tiled=True, axis...]
    ppermute x18 -> x19, starting transfers between devices: 16.8 us -> 19.1 us  [swap(): lax.ppermute(block, axis, [(i ^ mask, i) for i in range(lax.axis_size(axi...]
    convert_element_type x2, other arithmetic: 2.45 us -> 0.28 us  [layer(): (a + b.astype(jnp.float32)).astype(jnp.bfloat16)]
    unnamed x34 -> x31, local copies, waits for them, and re-layouts: 4.8 us -> 4.68 us
  transfers between devices with their start and end apart: 23 -> 24, of which waited for: 8 -> 9; matrix products, arithmetic and copies ran while one was open for 3% -> 5% of each run, Pallas kernels for 35% -> 37%
where the time goes in v3:
time: 205 us; the launch traced here: 203 us
  Pallas kernels  78.9 us (38%)
  starting transfers between devices  57.6 us (28%)
  waiting for transfers between devices  50 us (24%)
  local copies, waits for them, and re-layouts  13.4 us (7%)
  other arithmetic  3.27 us (2%)
    pallas_call x2, Pallas kernels, convolve(): pl.pallas_call(functools.partial(conv_kernel, n, tok, width, place), grid...  39.9 us
    ppermute x19, waiting for transfers between devices, swap(): lax.ppermute(block, axis, [(i ^ mask, i) for i in range(lax.axis_size(axi...  28 us
    pallas_call x4, Pallas kernels, project(): pl.pallas_call(functools.partial(project_kernel, len(kept)), grid_spec=pl...  26.8 us
    all_to_all x2, starting transfers between devices, layer(): lax.all_to_all(conv, 'seq', split_axis=0, concat_axis=0, tiled=True, axis...  21.3 us
    ppermute x19, starting transfers between devices, swap(): lax.ppermute(block, axis, [(i ^ mask, i) for i in range(lax.axis_size(axi...  19.1 us
    all_to_all x2, waiting for transfers between devices, layer(): lax.all_to_all(turned, 'seq', split_axis=0, concat_axis=0, tiled=True)  15.7 us
    all_to_all x2, starting transfers between devices, layer(): lax.all_to_all(turned, 'seq', split_axis=0, concat_axis=0, tiled=True)  14.7 us
    pallas_call x2, Pallas kernels, gate(): pl.pallas_call(lambda spot_ref, *refs: gate_kernel(count, *refs), grid_sp...  6.23 us
  transfers between devices with their start and end apart: 24, of which 9 were waited for; matrix products, arithmetic and copies ran while one was open for 5% of the time, Pallas kernels for 37%

profile of v3, /device:TPU:0, one launch (start us, length us, event | category | flops | bytes accessed | tf_op | source)
XLA Modules:
  0.0 203.4 jit_solution(7045106457701381828)
XLA Ops:
  1.6 2.4 %collective-permute-start = (bf16[3,2,2048]{2,1,0:T(2,128)(2,1)S(1)}, bf16[3,2,2048]{2,1,0:T(2,128)(2,1)S(1)}, u32[]{:S(2)}, u32[]{:S(2)}) collective-permute-start(bf16[3,2,2048]{2,1,0:T(2,128)(2,1)S(1)} %pad_maximum_fusion.1), channel_id=1, source_target_pairs={{0,2},{2,4},{4,6},{6,8},{8,10},{10,12},{12,14},{14,16},{16,18},{18... | collective-permute-start | bytes 73736 | tf_op jit(solution)/shard_map/ppermute | solution.py:21
  5.5 3.0 %mix.3 = bf16[2,2,4,96,256]{4,3,2,1,0:T(8,128)(2,1)} custom-call(bf16[256,2048]{1,0:T(8,128)(2,1)} %key_ref.3, bf16[256,2048]{1,0:T(8,128)(2,1)} %value_ref.3, bf16[3,2,2048]{2,1,0:T(2,128)(2,1)} %copy-done.12, f32[3,3,2048]{2,1,0:T(4,128)} %refs_0_.7, f32[1024,256]{1,0:T(8,128)} %refs_0_.6), custom_call_target="tpu_custom_call" | custom-call | tf_op jit(solution)/shard_map/mix/pallas_call | solution.py:175
  8.4 9.3 %all-to-all-start.2 = ((bf16[16,96,256]{2,1,0:T(8,128)(2,1)}), bf16[16,96,256]{2,1,0:T(8,128)(2,1)S(1)}, u32[]{:S(2)}, u32[]{:S(2)}) async-start(bf16[16,96,256]{2,1,0:T(8,128)(2,1)} %bitcast.26), calls=%async_computation.2 | async-start | bytes 1572864 | tf_op jit(solution)/shard_map/all_to_all | solution.py:380
  17.7 3.0 %mix.2 = bf16[2,2,4,96,256]{4,3,2,1,0:T(8,128)(2,1)} custom-call(bf16[256,2048]{1,0:T(8,128)(2,1)} %key_ref.3, bf16[256,2048]{1,0:T(8,128)(2,1)} %value_ref.3, bf16[3,2,2048]{2,1,0:T(2,128)(2,1)} %copy-done.12, f32[3,3,2048]{2,1,0:T(4,128)} %refs_0_.7, f32[1024,256]{1,0:T(8,128)} %refs_0_.6), custom_call_target="tpu_custom_call" | custom-call | tf_op jit(solution)/shard_map/mix/pallas_call | solution.py:175
  20.7 15.7 %all-to-all-done.2.x_ref.f_ref = bf16[16,96,256]{2,1,0:T(8,128)(2,1)S(1)} async-done(((bf16[16,96,256]{2,1,0:T(8,128)(2,1)}), bf16[16,96,256]{2,1,0:T(8,128)(2,1)S(1)}, u32[]{:S(2)}, u32[]{:S(2)}) %all-to-all-start.2) | async-done | bytes 786464 | tf_op jit(solution)/shard_map/all_to_all | solution.py:380
  36.4 5.4 %all-to-all-start = ((bf16[16,96,256]{2,1,0:T(8,128)(2,1)}), bf16[16,96,256]{2,1,0:T(8,128)(2,1)}, u32[]{:S(2)}, u32[]{:S(2)}) async-start(bf16[16,96,256]{2,1,0:T(8,128)(2,1)} %bitcast.25), calls=%async_computation | async-start | bytes 1572864 | tf_op jit(solution)/shard_map/all_to_all | solution.py:380
  44.7 2.4 %collective-permute-start.9 = (bf16[256,512]{1,0:T(8,128)(2,1)}, bf16[256,512]{1,0:T(8,128)(2,1)}, u32[]{:S(2)}, u32[]{:S(2)}) collective-permute-start(bf16[256,512]{1,0:T(8,128)(2,1)} %get-tuple-element.30), channel_id=1, source_target_pairs={{16,0},{18,2},{20,4},{22,6},{24,8},{26,10},{28,12},{30,14},{0,16},... | collective-permute-start | bytes 786440 | tf_op jit(solution)/shard_map/ppermute | solution.py:330
  48.4 2.4 %collective-permute-start.15 = (bf16[256,1024]{1,0:T(8,128)(2,1)}, bf16[256,1024]{1,0:T(8,128)(2,1)}, u32[]{:S(2)}, u32[]{:S(2)}) collective-permute-start(bf16[256,1024]{1,0:T(8,128)(2,1)} %slice.33), channel_id=1, source_target_pairs={{16,0},{18,2},{20,4},{22,6},{24,8},{26,10},{28,12},{30,14},{0,16},... | collective-permute-start | bytes 1572872 | tf_op jit(solution)/shard_map/ppermute | solution.py:330
  51.7 19.8 %convolve.3 = bf16[16,64,256]{2,1,0:T(8,128)(2,1)} custom-call(bf16[16,96,256]{2,1,0:T(8,128)(2,1)} %copy-done.3, bf16[16,96,256]{2,1,0:T(8,128)(2,1)} %copy-done.3, f32[128,128]{1,0:T(8,128)} %broadcast_in_dim.8.gain_ref), custom_call_target="tpu_custom_call" | custom-call | tf_op jit(solution)/shard_map/convolve/pallas_call | solution.py:149
  71.6 17.0 %all-to-all-start.3 = ((bf16[8,2,64,256]{3,2,1,0:T(8,128)(2,1)}), bf16[8,2,64,256]{3,2,1,0:T(8,128)(2,1)}, u32[]{:S(2)}, u32[]{:S(2)}) async-start(bf16[8,2,64,256]{3,2,1,0:T(8,128)(2,1)} %bitcast.28), calls=%async_computation.3 | async-start | bytes 1048576 | tf_op jit(solution)/shard_map/all_to_all | solution.py:386
  93.8 8.9 %collective-permute-done.10 = bf16[256,512]{1,0:T(8,128)(2,1)S(1)} collective-permute-done((bf16[256,512]{1,0:T(8,128)(2,1)}, bf16[256,512]{1,0:T(8,128)(2,1)S(1)}, u32[]{:S(2)}, u32[]{:S(2)}) %collective-permute-start.10) | collective-permute-done | bytes 262176 | tf_op jit(solution)/shard_map/ppermute | solution.py:330
  104.9 20.1 %convolve.2 = bf16[16,64,256]{2,1,0:T(8,128)(2,1)} custom-call(bf16[16,96,256]{2,1,0:T(8,128)(2,1)} %all-to-all-done.x_ref.f_ref, bf16[16,96,256]{2,1,0:T(8,128)(2,1)} %all-to-all-done.x_ref.f_ref, f32[128,128]{1,0:T(8,128)} %broadcast_in_dim.8.gain_ref), custom_call_target="tpu_custom_call" | custom-call | tf_op jit(solution)/shard_map/convolve/pallas_call | solution.py:149
  125.0 4.3 %all-to-all-start.1 = ((bf16[8,2,64,256]{3,2,1,0:T(8,128)(2,1)}), bf16[8,2,64,256]{3,2,1,0:T(8,128)(2,1)}, u32[]{:S(2)}, u32[]{:S(2)}) async-start(bf16[8,2,64,256]{3,2,1,0:T(8,128)(2,1)} %bitcast.27), calls=%async_computation.1 | async-start | bytes 1048576 | tf_op jit(solution)/shard_map/all_to_all | solution.py:386
  133.2 3.1 %gate.3 = (bf16[2,256,256]{2,1,0:T(8,128)(2,1)}, bf16[2,256,256]{2,1,0:T(8,128)(2,1)}) custom-call(s32[5]{0:T(128)} %stack.82.spot_ref, f32[3,3,2048]{2,1,0:T(4,128)} %refs_0_.7, bf16[256,2048]{1,0:T(8,128)(2,1)} %refs_1_.3, bf16[2,2048]{1,0:T(2,128)(2,1)} %copy-done.13, bf16[8,2,64,256]{3,2,1,0:T(8,128)(2,1)} %all-to-all-done.3.refs_3_.refs_6_, ...), custom_call_target="tpu_custom_call" | custom-call | tf_op jit(solution)/shard_map/gate/pallas_call | solution.py:205
  137.9 5.4 %all-to-all-done.1.refs_3_.refs_6_ = bf16[8,2,64,256]{3,2,1,0:T(8,128)(2,1)} async-done(((bf16[8,2,64,256]{3,2,1,0:T(8,128)(2,1)}), bf16[8,2,64,256]{3,2,1,0:T(8,128)(2,1)}, u32[]{:S(2)}, u32[]{:S(2)}) %all-to-all-start.1) | async-done | bytes 524320 | tf_op jit(solution)/shard_map/all_to_all | solution.py:386
  143.3 3.1 %gate.2 = (bf16[2,256,256]{2,1,0:T(8,128)(2,1)}, bf16[2,256,256]{2,1,0:T(8,128)(2,1)}) custom-call(s32[5]{0:T(128)} %stack.82.spot_ref, f32[3,3,2048]{2,1,0:T(4,128)} %refs_0_.7, bf16[256,2048]{1,0:T(8,128)(2,1)} %refs_1_.3, bf16[2,2048]{1,0:T(2,128)(2,1)} %copy-done.13, bf16[8,2,64,256]{3,2,1,0:T(8,128)(2,1)} %all-to-all-done.1.refs_3_.refs_6_, ...), custom_call_target="tpu_custom_call" | custom-call | tf_op jit(solution)/shard_map/gate/pallas_call | solution.py:205
  153.0 6.6 %project.4 = (f32[256,1024]{1,0:T(8,128)}, f32[256,1024]{1,0:T(8,128)}) custom-call(s32[9]{0:T(128)} %stack.88.spots, bf16[2,256,256]{2,1,0:T(8,128)(2,1)} %get-tuple-element.17.refs_0_, bf16[2,256,256]{2,1,0:T(8,128)(2,1)} %get-tuple-element.18.refs_1_, bf16[2,256,256]{2,1,0:T(8,128)(2,1)} %get-tuple-element.19.refs_2_, ...), custom_call_target="tpu_custom_call" | custom-call | tf_op jit(solution)/shard_map/project/pallas_call | solution.py:296
  159.6 2.0 collective-permute-done.2.refs_0_
  161.6 4.7 %collective-permute-done.4.refs_2_ = bf16[2,256,256]{2,1,0:T(8,128)(2,1)S(1)} collective-permute-done((bf16[2,256,256]{2,1,0:T(8,128)(2,1)}, bf16[2,256,256]{2,1,0:T(8,128)(2,1)S(1)}, u32[]{:S(2)}, u32[]{:S(2)}) %collective-permute-start.4) | collective-permute-done | bytes 262176 | tf_op jit(solution)/shard_map/ppermute | solution.py:330
  166.9 6.8 %project.5 = (f32[256,1024]{1,0:T(8,128)}, bf16[256,1024]{1,0:T(8,128)(2,1)}) custom-call(s32[9]{0:T(128)} %stack.78.spots, bf16[2,256,256]{2,1,0:T(8,128)(2,1)} %copy-done.8, bf16[2,256,256]{2,1,0:T(8,128)(2,1)} %copy-done.6, bf16[2,256,256]{2,1,0:T(8,128)(2,1)} %copy-done.9, bf16[2,256,256]{2,1,0:T(8,128)(2,1)} %copy-done.7, ...), custom_call_target="tpu_custom_call" | custom-call | tf_op jit(solution)/shard_map/project/pallas_call | solution.py:296
  175.4 6.6 %project.6 = (f32[256,1024]{1,0:T(8,128)}, f32[256,1024]{1,0:T(8,128)}) custom-call(s32[9]{0:T(128)} %stack.88.spots, bf16[2,256,256]{2,1,0:T(8,128)(2,1)} %get-tuple-element.17.refs_0_, bf16[2,256,256]{2,1,0:T(8,128)(2,1)} %get-tuple-element.18.refs_1_, bf16[2,256,256]{2,1,0:T(8,128)(2,1)} %get-tuple-element.19.refs_2_, ...), custom_call_target="tpu_custom_call" | custom-call | tf_op jit(solution)/shard_map/project/pallas_call | solution.py:296
  182.0 6.9 %project.7 = (f32[256,1024]{1,0:T(8,128)}, bf16[256,1024]{1,0:T(8,128)(2,1)}) custom-call(s32[9]{0:T(128)} %stack.78.spots, bf16[2,256,256]{2,1,0:T(8,128)(2,1)} %copy-done.8, bf16[2,256,256]{2,1,0:T(8,128)(2,1)} %copy-done.6, bf16[2,256,256]{2,1,0:T(8,128)(2,1)} %copy-done.9, bf16[2,256,256]{2,1,0:T(8,128)(2,1)} %copy-done.7, ...), custom_call_target="tpu_custom_call" | custom-call | tf_op jit(solution)/shard_map/project/pallas_call | solution.py:296
  189.0 2.1 %collective-permute-start.19 = (bf16[256,1024]{1,0:T(8,128)(2,1)}, bf16[256,1024]{1,0:T(8,128)(2,1)S(1)}, u32[]{:S(2)}, u32[]{:S(2)}) collective-permute-start(bf16[256,1024]{1,0:T(8,128)(2,1)} %get-tuple-element.28), channel_id=1, source_target_pairs={{8,0},{10,2},{12,4},{14,6},{0,8},{2,10},{4,12},{6,14},{24,16},{26,... | collective-permute-start | bytes 1572872 | tf_op jit(solution)/shard_map/ppermute | solution.py:330
  191.2 11.0 %collective-permute-done.19 = bf16[256,1024]{1,0:T(8,128)(2,1)S(1)} collective-permute-done((bf16[256,1024]{1,0:T(8,128)(2,1)}, bf16[256,1024]{1,0:T(8,128)(2,1)S(1)}, u32[]{:S(2)}, u32[]{:S(2)}) %collective-permute-start.19) | collective-permute-done | bytes 524320 | tf_op jit(solution)/shard_map/ppermute | solution.py:330
  (84 shorter events, 31.3 us)
Async XLA Ops:
  1.6 3.2 %collective-permute-start = (bf16[3,2,2048]{2,1,0:T(2,128)(2,1)S(1)}, bf16[3,2,2048]{2,1,0:T(2,128)(2,1)S(1)}, u32[]{:S(2)}, u32[]{:S(2)}) collective-permute-start(bf16[3,2,2048]{2,1,0:T(2,128)(2,1)S(1)} %pad_maximum_fusion.1), channel_id=1, source_target_pairs={{0,2},{2,4},{4,6},{6,8},{8,10},{10,12},{12,14},{14,16},{16,18},{18... | collective-permute-start | bytes 73736 | tf_op jit(solution)/shard_map/ppermute | solution.py:21
  8.4 28.0 %all-to-all-start.2 = ((bf16[16,96,256]{2,1,0:T(8,128)(2,1)}), bf16[16,96,256]{2,1,0:T(8,128)(2,1)S(1)}, u32[]{:S(2)}, u32[]{:S(2)}) async-start(bf16[16,96,256]{2,1,0:T(8,128)(2,1)} %bitcast.26), calls=%async_computation.2 | async-start | bytes 1572864 | tf_op jit(solution)/shard_map/all_to_all | solution.py:380
  36.4 35.1 %all-to-all-start = ((bf16[16,96,256]{2,1,0:T(8,128)(2,1)}), bf16[16,96,256]{2,1,0:T(8,128)(2,1)}, u32[]{:S(2)}, u32[]{:S(2)}) async-start(bf16[16,96,256]{2,1,0:T(8,128)(2,1)} %bitcast.25), calls=%async_computation | async-start | bytes 1572864 | tf_op jit(solution)/shard_map/all_to_all | solution.py:380
  41.9 63.0 %collective-permute-start.7 = (bf16[256,2048]{1,0:T(8,128)(2,1)S(1)}, bf16[256,2048]{1,0:T(8,128)(2,1)S(1)}, u32[]{:S(2)}, u32[]{:S(2)}) collective-permute-start(bf16[256,2048]{1,0:T(8,128)(2,1)S(1)} %copy-done), channel_id=1, source_target_pairs={{4,0},{6,2},{0,4},{2,6},{12,8},{14,10},{8,12},{10,14},{20,16},{22,... | collective-permute-start | bytes 3145736 | tf_op jit(solution)/shard_map/ppermute | solution.py:330
  43.8 102.6 %collective-permute-start.6 = (bf16[256,2048]{1,0:T(8,128)(2,1)S(1)}, bf16[256,2048]{1,0:T(8,128)(2,1)S(1)}, u32[]{:S(2)}, u32[]{:S(2)}) collective-permute-start(bf16[256,2048]{1,0:T(8,128)(2,1)S(1)} %copy-done), channel_id=1, source_target_pairs={{2,0},{0,2},{6,4},{4,6},{10,8},{8,10},{14,12},{12,14},{18,16},{16,... | collective-permute-start | bytes 3145736 | tf_op jit(solution)/shard_map/ppermute | solution.py:330
  44.7 46.8 %collective-permute-start.9 = (bf16[256,512]{1,0:T(8,128)(2,1)}, bf16[256,512]{1,0:T(8,128)(2,1)}, u32[]{:S(2)}, u32[]{:S(2)}) collective-permute-start(bf16[256,512]{1,0:T(8,128)(2,1)} %get-tuple-element.30), channel_id=1, source_target_pairs={{16,0},{18,2},{20,4},{22,6},{24,8},{26,10},{28,12},{30,14},{0,16},... | collective-permute-start | bytes 786440 | tf_op jit(solution)/shard_map/ppermute | solution.py:330
  47.0 55.7 %collective-permute-start.10 = (bf16[256,512]{1,0:T(8,128)(2,1)}, bf16[256,512]{1,0:T(8,128)(2,1)S(1)}, u32[]{:S(2)}, u32[]{:S(2)}) collective-permute-start(bf16[256,512]{1,0:T(8,128)(2,1)} %get-tuple-element.29), channel_id=1, source_target_pairs={{16,0},{18,2},{20,4},{22,6},{24,8},{26,10},{28,12},{30,14},{0,16},... | collective-permute-start | bytes 786440 | tf_op jit(solution)/shard_map/ppermute | solution.py:330
  48.4 80.9 %collective-permute-start.15 = (bf16[256,1024]{1,0:T(8,128)(2,1)}, bf16[256,1024]{1,0:T(8,128)(2,1)}, u32[]{:S(2)}, u32[]{:S(2)}) collective-permute-start(bf16[256,1024]{1,0:T(8,128)(2,1)} %slice.33), channel_id=1, source_target_pairs={{16,0},{18,2},{20,4},{22,6},{24,8},{26,10},{28,12},{30,14},{0,16},... | collective-permute-start | bytes 1572872 | tf_op jit(solution)/shard_map/ppermute | solution.py:330
  71.6 53.4 %all-to-all-start.3 = ((bf16[8,2,64,256]{3,2,1,0:T(8,128)(2,1)}), bf16[8,2,64,256]{3,2,1,0:T(8,128)(2,1)}, u32[]{:S(2)}, u32[]{:S(2)}) async-start(bf16[8,2,64,256]{3,2,1,0:T(8,128)(2,1)} %bitcast.28), calls=%async_computation.3 | async-start | bytes 1048576 | tf_op jit(solution)/shard_map/all_to_all | solution.py:386
  91.5 38.1 %collective-permute-start.1 = (bf16[272,1024]{1,0:T(8,128)(2,1)}, bf16[272,1024]{1,0:T(8,128)(2,1)}, u32[]{:S(2)}, u32[]{:S(2)}) collective-permute-start(bf16[272,1024]{1,0:T(8,128)(2,1)} %fusion.1), channel_id=1, source_target_pairs={{8,0},{10,2},{12,4},{14,6},{0,8},{2,10},{4,12},{6,14},{24,16},{26,... | collective-permute-start | bytes 1671176 | tf_op jit(solution)/shard_map/ppermute | solution.py:330
  103.4 27.7 %collective-permute-start.12 = (bf16[256,1024]{1,0:T(8,128)(2,1)}, bf16[256,1024]{1,0:T(8,128)(2,1)}, u32[]{:S(2)}, u32[]{:S(2)}) collective-permute-start(bf16[256,1024]{1,0:T(8,128)(2,1)} %constant_dynamic-update-slice_fusion.refs_8_.refs_10_), channel_id=1, source_target_pairs={{4,0},{6,2},{0,4},{2,6},{12,8},{14,10},{8,12},{10,14},{20,16},{22,... | collective-permute-start | bytes 1572872 | tf_op jit(solution)/shard_map/ppermute | solution.py:330
  104.9 46.3 %collective-permute-start.8 = (bf16[256,2048]{1,0:T(8,128)(2,1)S(1)}, bf16[256,2048]{1,0:T(8,128)(2,1)}, u32[]{:S(2)}, u32[]{:S(2)}) collective-permute-start(bf16[256,2048]{1,0:T(8,128)(2,1)S(1)} %collective-permute-done.7.refs_6_.refs_8_), channel_id=1, source_target_pairs={{2,0},{0,2},{6,4},{4,6},{10,8},{8,10},{14,12},{12,14},{18,16},{16,... | collective-permute-start | bytes 3145736 | tf_op jit(solution)/shard_map/ppermute | solution.py:330
  125.0 18.4 %all-to-all-start.1 = ((bf16[8,2,64,256]{3,2,1,0:T(8,128)(2,1)}), bf16[8,2,64,256]{3,2,1,0:T(8,128)(2,1)}, u32[]{:S(2)}, u32[]{:S(2)}) async-start(bf16[8,2,64,256]{3,2,1,0:T(8,128)(2,1)} %bitcast.27), calls=%async_computation.1 | async-start | bytes 1048576 | tf_op jit(solution)/shard_map/all_to_all | solution.py:386
  129.3 7.0 %collective-permute-start.11 = (bf16[256,1024]{1,0:T(8,128)(2,1)}, bf16[256,1024]{1,0:T(8,128)(2,1)}, u32[]{:S(2)}, u32[]{:S(2)}) collective-permute-start(bf16[256,1024]{1,0:T(8,128)(2,1)} %constant_dynamic-update-slice_fusion.refs_8_.refs_10_), channel_id=1, source_target_pairs={{2,0},{0,2},{6,4},{4,6},{10,8},{8,10},{14,12},{12,14},{18,16},{16,... | collective-permute-start | bytes 1572872 | tf_op jit(solution)/shard_map/ppermute | solution.py:330
  129.6 19.6 %collective-permute-start.17 = (bf16[256,1024]{1,0:T(8,128)(2,1)}, bf16[256,1024]{1,0:T(8,128)(2,1)}, u32[]{:S(2)}, u32[]{:S(2)}) collective-permute-start(bf16[256,1024]{1,0:T(8,128)(2,1)} %collective-permute-done.15.refs_8_.refs_10_), channel_id=1, source_target_pairs={{4,0},{6,2},{0,4},{2,6},{12,8},{14,10},{8,12},{10,14},{20,16},{22,... | collective-permute-start | bytes 1572872 | tf_op jit(solution)/shard_map/ppermute | solution.py:330
  131.2 19.5 %collective-permute-start.13 = (bf16[256,1024]{1,0:T(8,128)(2,1)}, bf16[256,1024]{1,0:T(8,128)(2,1)}, u32[]{:S(2)}, u32[]{:S(2)}) collective-permute-start(bf16[256,1024]{1,0:T(8,128)(2,1)} %collective-permute-done.12.refs_10_.refs_12_), channel_id=1, source_target_pairs={{2,0},{0,2},{6,4},{4,6},{10,8},{8,10},{14,12},{12,14},{18,16},{16,... | collective-permute-start | bytes 1572872 | tf_op jit(solution)/shard_map/ppermute | solution.py:330
  136.3 14.9 %collective-permute-start.3 = (bf16[2,256,256]{2,1,0:T(8,128)(2,1)}, bf16[2,256,256]{2,1,0:T(8,128)(2,1)S(1)}, u32[]{:S(2)}, u32[]{:S(2)}) collective-permute-start(bf16[2,256,256]{2,1,0:T(8,128)(2,1)} %get-tuple-element.18.refs_1_), channel_id=1, source_target_pairs={{1,0},{0,1},{3,2},{2,3},{5,4},{4,5},{7,6},{6,7},{9,8},{8,9},{11,10... | collective-permute-start | bytes 786440 | tf_op jit(solution)/shard_map/ppermute | solution.py:330
  146.5 13.1 %collective-permute-start.5 = (bf16[2,256,256]{2,1,0:T(8,128)(2,1)}, bf16[2,256,256]{2,1,0:T(8,128)(2,1)S(1)}, u32[]{:S(2)}, u32[]{:S(2)}) collective-permute-start(bf16[2,256,256]{2,1,0:T(8,128)(2,1)} %get-tuple-element.20.refs_3_), channel_id=1, source_target_pairs={{1,0},{0,1},{3,2},{2,3},{5,4},{4,5},{7,6},{6,7},{9,8},{8,9},{11,10... | collective-permute-start | bytes 786440 | tf_op jit(solution)/shard_map/ppermute | solution.py:330
  149.2 12.4 %collective-permute-start.2 = (bf16[2,256,256]{2,1,0:T(8,128)(2,1)}, bf16[2,256,256]{2,1,0:T(8,128)(2,1)S(1)}, u32[]{:S(2)}, u32[]{:S(2)}) collective-permute-start(bf16[2,256,256]{2,1,0:T(8,128)(2,1)} %get-tuple-element.17.refs_0_), channel_id=1, source_target_pairs={{1,0},{0,1},{3,2},{2,3},{5,4},{4,5},{7,6},{6,7},{9,8},{8,9},{11,10... | collective-permute-start | bytes 786440 | tf_op jit(solution)/shard_map/ppermute | solution.py:330
  150.7 15.5 %collective-permute-start.4 = (bf16[2,256,256]{2,1,0:T(8,128)(2,1)}, bf16[2,256,256]{2,1,0:T(8,128)(2,1)S(1)}, u32[]{:S(2)}, u32[]{:S(2)}) collective-permute-start(bf16[2,256,256]{2,1,0:T(8,128)(2,1)} %get-tuple-element.19.refs_2_), channel_id=1, source_target_pairs={{1,0},{0,1},{3,2},{2,3},{5,4},{4,5},{7,6},{6,7},{9,8},{8,9},{11,10... | collective-permute-start | bytes 786440 | tf_op jit(solution)/shard_map/ppermute | solution.py:330
  151.2 22.6 %collective-permute-start.16 = (bf16[256,1024]{1,0:T(8,128)(2,1)}, bf16[256,1024]{1,0:T(8,128)(2,1)S(1)}, u32[]{:S(2)}, u32[]{:S(2)}) collective-permute-start(bf16[256,1024]{1,0:T(8,128)(2,1)} %collective-permute-done.15.refs_8_.refs_10_), channel_id=1, source_target_pairs={{2,0},{0,2},{6,4},{4,6},{10,8},{8,10},{14,12},{12,14},{18,16},{16,... | collective-permute-start | bytes 1572872 | tf_op jit(solution)/shard_map/ppermute | solution.py:330
  151.2 22.6 %collective-permute-start.18 = (bf16[256,1024]{1,0:T(8,128)(2,1)}, bf16[256,1024]{1,0:T(8,128)(2,1)S(1)}, u32[]{:S(2)}, u32[]{:S(2)}) collective-permute-start(bf16[256,1024]{1,0:T(8,128)(2,1)} %collective-permute-done.17.refs_10_.refs_12_), channel_id=1, source_target_pairs={{2,0},{0,2},{6,4},{4,6},{10,8},{8,10},{14,12},{12,14},{18,16},{16,... | collective-permute-start | bytes 1572872 | tf_op jit(solution)/shard_map/ppermute | solution.py:330
  173.7 17.4 %collective-permute-start.14 = (bf16[256,1024]{1,0:T(8,128)(2,1)}, bf16[256,1024]{1,0:T(8,128)(2,1)S(1)}, u32[]{:S(2)}, u32[]{:S(2)}) collective-permute-start(bf16[256,1024]{1,0:T(8,128)(2,1)} %get-tuple-element.24), channel_id=1, source_target_pairs={{8,0},{10,2},{12,4},{14,6},{0,8},{2,10},{4,12},{6,14},{24,16},{26,... | collective-permute-start | bytes 1572872 | tf_op jit(solution)/shard_map/ppermute | solution.py:330
  189.0 13.3 %collective-permute-start.19 = (bf16[256,1024]{1,0:T(8,128)(2,1)}, bf16[256,1024]{1,0:T(8,128)(2,1)S(1)}, u32[]{:S(2)}, u32[]{:S(2)}) collective-permute-start(bf16[256,1024]{1,0:T(8,128)(2,1)} %get-tuple-element.28), channel_id=1, source_target_pairs={{8,0},{10,2},{12,4},{14,6},{0,8},{2,10},{4,12},{6,14},{24,16},{26,... | collective-permute-start | bytes 1572872 | tf_op jit(solution)/shard_map/ppermute | solution.py:330
  (15 other events, 109.4 us)

commit v4 on v2

--- a/solution.py
+++ b/solution.py
@@ -241,19 +241,21 @@
 
 
 def project_kernel(count, per, spots, *refs):
-    gated, pieces = refs[:per], refs[per : per + count]
-    out_ref, rows = refs[per + count :]
-    blocks, _, wide = gated[0].shape
+    gated, pieces = refs[: 2 * per], refs[2 * per : 2 * per + count]
+    kept_ref, given_ref, rows = refs[2 * per + count :]
+    blocks, tokens, wide = gated[0].shape
 
     @pl.when(pl.program_id(0) == 0)
     def _():
         for piece in range(count):
             spot = spots[piece]
+            columns = slice(piece * wide, (piece + 1) * wide)
             for source in range(per):
 
                 @pl.when(spot // blocks == source)
                 def _():
-                    rows[:, piece * wide : (piece + 1) * wide] = gated[source][lax.rem(spot, blocks)]
+                    rows[:tokens, columns] = gated[source][lax.rem(spot, blocks)]
+                    rows[tokens:, columns] = gated[per + source][lax.rem(spot, blocks)]
 
     total = None
     for piece in range(count):
@@ -263,31 +265,36 @@
             preferred_element_type=jnp.float32,
         )
         total = out if total is None else total + out
-    out_ref[...] = total.astype(out_ref.dtype)
-
-
-def project(spots, gated, pieces, kind, columns, first):
-    blocks, tokens, wide = gated[0].shape
+    kept_ref[...] = total[:tokens]
+    given_ref[...] = total[tokens:].astype(jnp.bfloat16)
+
+
+def project(spots, kept, given, pieces, columns, first):
+    blocks, tokens, wide = kept[0].shape
     count = len(pieces)
-    step = min(256, columns)
+    step = min(512, columns)
 
     def held(piece):
         skip = first // step if piece.shape[1] > columns else 0
         return pl.BlockSpec((wide, step), lambda j, spots: (0, j + skip))
 
     whole = pl.BlockSpec((blocks, tokens, wide), lambda j, spots: (0, 0, 0))
+    out = pl.BlockSpec((tokens, step), lambda j, spots: (0, j))
     return pl.pallas_call(
-        functools.partial(project_kernel, count, len(gated)),
+        functools.partial(project_kernel, count, len(kept)),
         grid_spec=pltpu.PrefetchScalarGridSpec(
             num_scalar_prefetch=1,
             grid=(columns // step,),
-            in_specs=[whole] * len(gated) + [held(piece) for piece in pieces],
-            out_specs=pl.BlockSpec((tokens, step), lambda j, spots: (0, j)),
-            scratch_shapes=[pltpu.VMEM((tokens, count * wide), jnp.bfloat16)],
+            in_specs=[whole] * (2 * len(kept)) + [held(piece) for piece in pieces],
+            out_specs=[out, out],
+            scratch_shapes=[pltpu.VMEM((2 * tokens, count * wide), jnp.bfloat16)],
         ),
-        out_shape=jax.ShapeDtypeStruct((tokens, columns), kind),
+        out_shape=[
+            jax.ShapeDtypeStruct((tokens, columns), jnp.float32),
+            jax.ShapeDtypeStruct((tokens, columns), jnp.bfloat16),
+        ],
         name="project",
-    )(spots, *gated, *pieces)
+    )(spots, *kept, *given, *pieces)
 
 
 def layer(query_feat, key_feat, value_feat, short_filter, long_filter, direct_gain, out_weight):
@@ -318,7 +325,11 @@
     span = columns // CUTS
     pieces = []
     for cut in range(CUTS):
-        far = swap(out_weight[:, cut * span : (cut + 1) * span], "seq", 2 * inner)
+        share = span // 2 if cut == 0 else span
+        far = []
+        for start in range(cut * span, (cut + 1) * span, share):
+            far.append(swap(out_weight[:, start : start + share], "seq", 2 * inner))
+        far = far[0] if len(far) == 1 else jnp.concatenate(far, axis=1)
         far_near = swap(far, "seq", 2)
         far_mate = swap(far, "seq", 1)
         far_near_mate = swap(far_near, "seq", 1)
@@ -377,10 +388,11 @@
         kept_far.append(swap(kept[part], "ch", 1))
     sums, taken = [], []
     for cut in range(CUTS):
-        passed = project(spots, given + given_far, pieces[cut], jnp.bfloat16, span, cut * span)
+        held, passed = project(
+            spots, kept + kept_far, given + given_far, pieces[cut], span, cut * span
+        )
+        sums.append(held)
         taken.append(swap(passed, "seq", inner))
-    for cut in range(CUTS):
-        sums.append(project(spots, kept + kept_far, pieces[cut], jnp.float32, span, cut * span))
     outs = [(a + b.astype(jnp.float32)).astype(jnp.bfloat16) for a, b in zip(sums, taken)]
     return jnp.concatenate(outs, axis=1)
 

time: 214 us -> 202 us (0.944)
  waiting for transfers between devices: 77.2 us -> 62.8 us
  starting transfers between devices: 42.3 us -> 56.2 us
  Pallas kernels: 77.3 us -> 65.7 us
  other arithmetic: 4.4 us -> 2.25 us
    ppermute x18 -> x19, waiting for transfers between devices: 54.7 us -> 40.4 us  [swap(): lax.ppermute(block, axis, [(i ^ mask, i) for i in range(lax.axis_size(axi...]
    all_to_all x2, starting transfers between devices: 8.47 us -> 20.6 us  [layer(): lax.all_to_all(conv, 'seq', split_axis=0, concat_axis=0, tiled=True, axis...]
    pallas_call x4 -> x2, Pallas kernels: 25.4 us -> 13.8 us  [project(): pl.pallas_call(functools.partial(project_kernel, count, len(kept)), grid_...]
    convert_element_type x2, other arithmetic: 2.45 us -> 0.29 us  [layer(): (a + b.astype(jnp.float32)).astype(jnp.bfloat16)]
    ppermute x18 -> x19, starting transfers between devices: 16.8 us -> 18.6 us  [swap(): lax.ppermute(block, axis, [(i ^ mask, i) for i in range(lax.axis_size(axi...]
    unnamed x34 -> x37, local copies, waits for them, and re-layouts: 4.8 us -> 4.61 us
  transfers between devices with their start and end apart: 23 -> 24, of which waited for: 8 -> 10; matrix products, arithmetic and copies ran while one was open for 3% -> 5% of each run, Pallas kernels for 35% -> 31%
where the time goes in v4:
time: 202 us; the launch traced here: 201 us
  Pallas kernels  65.7 us (33%)
  waiting for transfers between devices  62.8 us (31%)
  starting transfers between devices  56.2 us (28%)
  local copies, waits for them, and re-layouts  13.6 us (7%)
  other arithmetic  2.25 us (1%)
    ppermute x19, waiting for transfers between devices, swap(): lax.ppermute(block, axis, [(i ^ mask, i) for i in range(lax.axis_size(axi...  40.4 us
    pallas_call x2, Pallas kernels, convolve(): pl.pallas_call(functools.partial(conv_kernel, n, tok, width, place), grid...  39.7 us
    all_to_all x2, starting transfers between devices, layer(): lax.all_to_all(conv, 'seq', split_axis=0, concat_axis=0, tiled=True, axis...  20.6 us
    ppermute x19, starting transfers between devices, swap(): lax.ppermute(block, axis, [(i ^ mask, i) for i in range(lax.axis_size(axi...  18.6 us
    all_to_all x2, waiting for transfers between devices, layer(): lax.all_to_all(turned, 'seq', split_axis=0, concat_axis=0, tiled=True)  15.7 us
    all_to_all x2, starting transfers between devices, layer(): lax.all_to_all(turned, 'seq', split_axis=0, concat_axis=0, tiled=True)  14.7 us
    pallas_call x2, Pallas kernels, project(): pl.pallas_call(functools.partial(project_kernel, count, len(kept)), grid_...  13.8 us
    pallas_call x2, Pallas kernels, gate(): pl.pallas_call(lambda spot_ref, *refs: gate_kernel(count, *refs), grid_sp...  6.19 us
  transfers between devices with their start and end apart: 24, of which 10 were waited for; matrix products, arithmetic and copies ran while one was open for 5% of the time, Pallas kernels for 31%

profile of v4, /device:TPU:0, one launch (start us, length us, event | category | flops | bytes accessed | tf_op | source)
XLA Modules:
  0.0 200.8 jit_solution(18047094018214319300)
XLA Ops:
  1.6 2.4 %collective-permute-start = (bf16[3,2,2048]{2,1,0:T(2,128)(2,1)S(1)}, bf16[3,2,2048]{2,1,0:T(2,128)(2,1)S(1)}, u32[]{:S(2)}, u32[]{:S(2)}) collective-permute-start(bf16[3,2,2048]{2,1,0:T(2,128)(2,1)S(1)} %pad_maximum_fusion.1), channel_id=1, source_target_pairs={{0,2},{2,4},{4,6},{6,8},{8,10},{10,12},{12,14},{14,16},{16,18},{18... | collective-permute-start | bytes 73736 | tf_op jit(solution)/shard_map/ppermute | solution.py:21
  5.5 3.0 %mix.3 = bf16[2,2,4,96,256]{4,3,2,1,0:T(8,128)(2,1)} custom-call(bf16[256,2048]{1,0:T(8,128)(2,1)} %key_ref.3, bf16[256,2048]{1,0:T(8,128)(2,1)} %value_ref.3, bf16[3,2,2048]{2,1,0:T(2,128)(2,1)} %copy-done.15, f32[3,3,2048]{2,1,0:T(4,128)} %refs_0_.7, f32[1024,256]{1,0:T(8,128)} %refs_0_.6), custom_call_target="tpu_custom_call" | custom-call | tf_op jit(solution)/shard_map/mix/pallas_call | solution.py:175
  8.4 9.3 %all-to-all-start.2 = ((bf16[16,96,256]{2,1,0:T(8,128)(2,1)}), bf16[16,96,256]{2,1,0:T(8,128)(2,1)S(1)}, u32[]{:S(2)}, u32[]{:S(2)}) async-start(bf16[16,96,256]{2,1,0:T(8,128)(2,1)} %bitcast.24), calls=%async_computation.2 | async-start | bytes 1572864 | tf_op jit(solution)/shard_map/all_to_all | solution.py:368
  17.7 3.0 %mix.2 = bf16[2,2,4,96,256]{4,3,2,1,0:T(8,128)(2,1)} custom-call(bf16[256,2048]{1,0:T(8,128)(2,1)} %key_ref.3, bf16[256,2048]{1,0:T(8,128)(2,1)} %value_ref.3, bf16[3,2,2048]{2,1,0:T(2,128)(2,1)} %copy-done.15, f32[3,3,2048]{2,1,0:T(4,128)} %refs_0_.7, f32[1024,256]{1,0:T(8,128)} %refs_0_.6), custom_call_target="tpu_custom_call" | custom-call | tf_op jit(solution)/shard_map/mix/pallas_call | solution.py:175
  20.7 15.7 %all-to-all-done.2.x_ref.f_ref = bf16[16,96,256]{2,1,0:T(8,128)(2,1)S(1)} async-done(((bf16[16,96,256]{2,1,0:T(8,128)(2,1)}), bf16[16,96,256]{2,1,0:T(8,128)(2,1)S(1)}, u32[]{:S(2)}, u32[]{:S(2)}) %all-to-all-start.2) | async-done | bytes 786464 | tf_op jit(solution)/shard_map/all_to_all | solution.py:368
  36.4 5.4 %all-to-all-start = ((bf16[16,96,256]{2,1,0:T(8,128)(2,1)}), bf16[16,96,256]{2,1,0:T(8,128)(2,1)S(1)}, u32[]{:S(2)}, u32[]{:S(2)}) async-start(bf16[16,96,256]{2,1,0:T(8,128)(2,1)} %bitcast.23), calls=%async_computation | async-start | bytes 1572864 | tf_op jit(solution)/shard_map/all_to_all | solution.py:368
  44.6 2.4 %collective-permute-start.9 = (bf16[256,512]{1,0:T(8,128)(2,1)}, bf16[256,512]{1,0:T(8,128)(2,1)}, u32[]{:S(2)}, u32[]{:S(2)}) collective-permute-start(bf16[256,512]{1,0:T(8,128)(2,1)} %get-tuple-element.22), channel_id=1, source_target_pairs={{16,0},{18,2},{20,4},{22,6},{24,8},{26,10},{28,12},{30,14},{0,16},... | collective-permute-start | bytes 786440 | tf_op jit(solution)/shard_map/ppermute | solution.py:317
  48.4 2.4 %collective-permute-start.15 = (bf16[256,1024]{1,0:T(8,128)(2,1)}, bf16[256,1024]{1,0:T(8,128)(2,1)}, u32[]{:S(2)}, u32[]{:S(2)}) collective-permute-start(bf16[256,1024]{1,0:T(8,128)(2,1)} %slice.33), channel_id=1, source_target_pairs={{16,0},{18,2},{20,4},{22,6},{24,8},{26,10},{28,12},{30,14},{0,16},... | collective-permute-start | bytes 1572872 | tf_op jit(solution)/shard_map/ppermute | solution.py:317
  51.7 19.8 %convolve.3 = bf16[16,64,256]{2,1,0:T(8,128)(2,1)} custom-call(bf16[16,96,256]{2,1,0:T(8,128)(2,1)} %copy-done.3, bf16[16,96,256]{2,1,0:T(8,128)(2,1)} %copy-done.3, f32[128,128]{1,0:T(8,128)} %broadcast_in_dim.8.gain_ref), custom_call_target="tpu_custom_call" | custom-call | tf_op jit(solution)/shard_map/convolve/pallas_call | solution.py:149
  71.5 16.9 %all-to-all-start.3 = ((bf16[8,2,64,256]{3,2,1,0:T(8,128)(2,1)}), bf16[8,2,64,256]{3,2,1,0:T(8,128)(2,1)S(1)}, u32[]{:S(2)}, u32[]{:S(2)}) async-start(bf16[8,2,64,256]{3,2,1,0:T(8,128)(2,1)} %bitcast.26), calls=%async_computation.3 | async-start | bytes 1048576 | tf_op jit(solution)/shard_map/all_to_all | solution.py:374
  93.1 9.7 %collective-permute-done.10 = bf16[256,512]{1,0:T(8,128)(2,1)} collective-permute-done((bf16[256,512]{1,0:T(8,128)(2,1)}, bf16[256,512]{1,0:T(8,128)(2,1)}, u32[]{:S(2)}, u32[]{:S(2)}) %collective-permute-start.10) | collective-permute-done | bytes 262176 | tf_op jit(solution)/shard_map/ppermute | solution.py:317
  106.0 19.9 %convolve.2 = bf16[16,64,256]{2,1,0:T(8,128)(2,1)} custom-call(bf16[16,96,256]{2,1,0:T(8,128)(2,1)} %copy-done.2, bf16[16,96,256]{2,1,0:T(8,128)(2,1)} %copy-done.2, f32[128,128]{1,0:T(8,128)} %broadcast_in_dim.8.gain_ref), custom_call_target="tpu_custom_call" | custom-call | tf_op jit(solution)/shard_map/convolve/pallas_call | solution.py:149
  125.8 3.7 %all-to-all-start.1 = ((bf16[8,2,64,256]{3,2,1,0:T(8,128)(2,1)}), bf16[8,2,64,256]{3,2,1,0:T(8,128)(2,1)S(1)}, u32[]{:S(2)}, u32[]{:S(2)}) async-start(bf16[8,2,64,256]{3,2,1,0:T(8,128)(2,1)} %bitcast.25), calls=%async_computation.1 | async-start | bytes 1048576 | tf_op jit(solution)/shard_map/all_to_all | solution.py:374
  133.4 3.1 %gate.3 = (bf16[2,256,256]{2,1,0:T(8,128)(2,1)}, bf16[2,256,256]{2,1,0:T(8,128)(2,1)}) custom-call(s32[5]{0:T(128)} %stack.64.spot_ref, f32[3,3,2048]{2,1,0:T(4,128)} %refs_0_.7, bf16[256,2048]{1,0:T(8,128)(2,1)} %refs_1_.3, bf16[2,2048]{1,0:T(2,128)(2,1)} %copy-done.16, bf16[8,2,64,256]{3,2,1,0:T(8,128)(2,1)} %copy-done.4, ...), custom_call_target="tpu_custom_call" | custom-call | tf_op jit(solution)/shard_map/gate/pallas_call | solution.py:205
  138.1 5.9 %all-to-all-done.1.refs_3_.refs_6_ = bf16[8,2,64,256]{3,2,1,0:T(8,128)(2,1)S(1)} async-done(((bf16[8,2,64,256]{3,2,1,0:T(8,128)(2,1)}), bf16[8,2,64,256]{3,2,1,0:T(8,128)(2,1)S(1)}, u32[]{:S(2)}, u32[]{:S(2)}) %all-to-all-start.1) | async-done | bytes 524320 | tf_op jit(solution)/shard_map/all_to_all | solution.py:374
  144.8 3.1 %gate.2 = (bf16[2,256,256]{2,1,0:T(8,128)(2,1)}, bf16[2,256,256]{2,1,0:T(8,128)(2,1)}) custom-call(s32[5]{0:T(128)} %stack.64.spot_ref, f32[3,3,2048]{2,1,0:T(4,128)} %refs_0_.7, bf16[256,2048]{1,0:T(8,128)(2,1)} %refs_1_.3, bf16[2,2048]{1,0:T(2,128)(2,1)} %copy-done.16, bf16[8,2,64,256]{3,2,1,0:T(8,128)(2,1)} %copy-done.5, ...), custom_call_target="tpu_custom_call" | custom-call | tf_op jit(solution)/shard_map/gate/pallas_call | solution.py:205
  152.6 4.5 %collective-permute-done.5.refs_7_ = bf16[2,256,256]{2,1,0:T(8,128)(2,1)S(1)} collective-permute-done((bf16[2,256,256]{2,1,0:T(8,128)(2,1)S(1)}, bf16[2,256,256]{2,1,0:T(8,128)(2,1)S(1)}, u32[]{:S(2)}, u32[]{:S(2)}) %collective-permute-start.5) | collective-permute-done | bytes 262176 | tf_op jit(solution)/shard_map/ppermute | solution.py:317
  157.2 5.6 %collective-permute-done.2.refs_2_ = bf16[2,256,256]{2,1,0:T(8,128)(2,1)S(1)} collective-permute-done((bf16[2,256,256]{2,1,0:T(8,128)(2,1)}, bf16[2,256,256]{2,1,0:T(8,128)(2,1)S(1)}, u32[]{:S(2)}, u32[]{:S(2)}) %collective-permute-start.2) | collective-permute-done | bytes 262176 | tf_op jit(solution)/shard_map/ppermute | solution.py:317
  162.8 4.7 %collective-permute-done.4.refs_6_ = bf16[2,256,256]{2,1,0:T(8,128)(2,1)S(1)} collective-permute-done((bf16[2,256,256]{2,1,0:T(8,128)(2,1)}, bf16[2,256,256]{2,1,0:T(8,128)(2,1)S(1)}, u32[]{:S(2)}, u32[]{:S(2)}) %collective-permute-start.4) | collective-permute-done | bytes 262176 | tf_op jit(solution)/shard_map/ppermute | solution.py:317
  168.2 6.9 %project.2 = (f32[256,1024]{1,0:T(8,128)}, bf16[256,1024]{1,0:T(8,128)(2,1)}) custom-call(s32[8]{0:T(128)} %stack.60.spots, bf16[2,256,256]{2,1,0:T(8,128)(2,1)} %get-tuple-element.13.refs_0_, bf16[2,256,256]{2,1,0:T(8,128)(2,1)} %get-tuple-element.14.refs_1_, bf16[2,256,256]{2,1,0:T(8,128)(2,1)} %copy-done.10, bf16[2,256,256]{2,1,0:T(8,128)(2,1)} %copy-done.8, ...), custom_call_target="tpu_custom_call" | custom-call | tf_op jit(solution)/shard_map/project/pallas_call | solution.py:283
  176.0 6.9 %project.3 = (f32[256,1024]{1,0:T(8,128)}, bf16[256,1024]{1,0:T(8,128)(2,1)}) custom-call(s32[8]{0:T(128)} %stack.60.spots, bf16[2,256,256]{2,1,0:T(8,128)(2,1)} %get-tuple-element.13.refs_0_, bf16[2,256,256]{2,1,0:T(8,128)(2,1)} %get-tuple-element.14.refs_1_, bf16[2,256,256]{2,1,0:T(8,128)(2,1)} %copy-done.10, bf16[2,256,256]{2,1,0:T(8,128)(2,1)} %copy-done.8, ...), custom_call_target="tpu_custom_call" | custom-call | tf_op jit(solution)/shard_map/project/pallas_call | solution.py:283
  182.9 2.1 %collective-permute-start.19 = (bf16[256,1024]{1,0:T(8,128)(2,1)}, bf16[256,1024]{1,0:T(8,128)(2,1)S(1)}, u32[]{:S(2)}, u32[]{:S(2)}) collective-permute-start(bf16[256,1024]{1,0:T(8,128)(2,1)} %get-tuple-element.20), channel_id=1, source_target_pairs={{8,0},{10,2},{12,4},{14,6},{0,8},{2,10},{4,12},{6,14},{24,16},{26,... | collective-permute-start | bytes 1572872 | tf_op jit(solution)/shard_map/ppermute | solution.py:317
  185.0 5.2 %collective-permute-done.14 = bf16[256,1024]{1,0:T(8,128)(2,1)S(1)} collective-permute-done((bf16[256,1024]{1,0:T(8,128)(2,1)}, bf16[256,1024]{1,0:T(8,128)(2,1)S(1)}, u32[]{:S(2)}, u32[]{:S(2)}) %collective-permute-start.14) | collective-permute-done | bytes 524320 | tf_op jit(solution)/shard_map/ppermute | solution.py:317
  190.3 9.3 %collective-permute-done.19 = bf16[256,1024]{1,0:T(8,128)(2,1)S(1)} collective-permute-done((bf16[256,1024]{1,0:T(8,128)(2,1)}, bf16[256,1024]{1,0:T(8,128)(2,1)S(1)}, u32[]{:S(2)}, u32[]{:S(2)}) %collective-permute-start.19) | collective-permute-done | bytes 524320 | tf_op jit(solution)/shard_map/ppermute | solution.py:317
  (87 shorter events, 29.9 us)
Async XLA Ops:
  1.6 3.2 %collective-permute-start = (bf16[3,2,2048]{2,1,0:T(2,128)(2,1)S(1)}, bf16[3,2,2048]{2,1,0:T(2,128)(2,1)S(1)}, u32[]{:S(2)}, u32[]{:S(2)}) collective-permute-start(bf16[3,2,2048]{2,1,0:T(2,128)(2,1)S(1)} %pad_maximum_fusion.1), channel_id=1, source_target_pairs={{0,2},{2,4},{4,6},{6,8},{8,10},{10,12},{12,14},{14,16},{16,18},{18... | collective-permute-start | bytes 73736 | tf_op jit(solution)/shard_map/ppermute | solution.py:21
  8.4 28.0 %all-to-all-start.2 = ((bf16[16,96,256]{2,1,0:T(8,128)(2,1)}), bf16[16,96,256]{2,1,0:T(8,128)(2,1)S(1)}, u32[]{:S(2)}, u32[]{:S(2)}) async-start(bf16[16,96,256]{2,1,0:T(8,128)(2,1)} %bitcast.24), calls=%async_computation.2 | async-start | bytes 1572864 | tf_op jit(solution)/shard_map/all_to_all | solution.py:368
  36.4 35.1 %all-to-all-start = ((bf16[16,96,256]{2,1,0:T(8,128)(2,1)}), bf16[16,96,256]{2,1,0:T(8,128)(2,1)S(1)}, u32[]{:S(2)}, u32[]{:S(2)}) async-start(bf16[16,96,256]{2,1,0:T(8,128)(2,1)} %bitcast.23), calls=%async_computation | async-start | bytes 1572864 | tf_op jit(solution)/shard_map/all_to_all | solution.py:368
  41.8 64.1 %collective-permute-start.7 = (bf16[256,2048]{1,0:T(8,128)(2,1)S(1)}, bf16[256,2048]{1,0:T(8,128)(2,1)}, u32[]{:S(2)}, u32[]{:S(2)}) collective-permute-start(bf16[256,2048]{1,0:T(8,128)(2,1)S(1)} %copy-done.1), channel_id=1, source_target_pairs={{4,0},{6,2},{0,4},{2,6},{12,8},{14,10},{8,12},{10,14},{20,16},{22,... | collective-permute-start | bytes 3145736 | tf_op jit(solution)/shard_map/ppermute | solution.py:317
  43.8 104.1 %collective-permute-start.6 = (bf16[256,2048]{1,0:T(8,128)(2,1)S(1)}, bf16[256,2048]{1,0:T(8,128)(2,1)}, u32[]{:S(2)}, u32[]{:S(2)}) collective-permute-start(bf16[256,2048]{1,0:T(8,128)(2,1)S(1)} %copy-done.1), channel_id=1, source_target_pairs={{2,0},{0,2},{6,4},{4,6},{10,8},{8,10},{14,12},{12,14},{18,16},{16,... | collective-permute-start | bytes 3145736 | tf_op jit(solution)/shard_map/ppermute | solution.py:317
  44.6 46.8 %collective-permute-start.9 = (bf16[256,512]{1,0:T(8,128)(2,1)}, bf16[256,512]{1,0:T(8,128)(2,1)}, u32[]{:S(2)}, u32[]{:S(2)}) collective-permute-start(bf16[256,512]{1,0:T(8,128)(2,1)} %get-tuple-element.22), channel_id=1, source_target_pairs={{16,0},{18,2},{20,4},{22,6},{24,8},{26,10},{28,12},{30,14},{0,16},... | collective-permute-start | bytes 786440 | tf_op jit(solution)/shard_map/ppermute | solution.py:317
  47.0 55.8 %collective-permute-start.10 = (bf16[256,512]{1,0:T(8,128)(2,1)}, bf16[256,512]{1,0:T(8,128)(2,1)}, u32[]{:S(2)}, u32[]{:S(2)}) collective-permute-start(bf16[256,512]{1,0:T(8,128)(2,1)} %get-tuple-element.21), channel_id=1, source_target_pairs={{16,0},{18,2},{20,4},{22,6},{24,8},{26,10},{28,12},{30,14},{0,16},... | collective-permute-start | bytes 786440 | tf_op jit(solution)/shard_map/ppermute | solution.py:317
  48.4 81.1 %collective-permute-start.15 = (bf16[256,1024]{1,0:T(8,128)(2,1)}, bf16[256,1024]{1,0:T(8,128)(2,1)}, u32[]{:S(2)}, u32[]{:S(2)}) collective-permute-start(bf16[256,1024]{1,0:T(8,128)(2,1)} %slice.33), channel_id=1, source_target_pairs={{16,0},{18,2},{20,4},{22,6},{24,8},{26,10},{28,12},{30,14},{0,16},... | collective-permute-start | bytes 1572872 | tf_op jit(solution)/shard_map/ppermute | solution.py:317
  71.5 54.3 %all-to-all-start.3 = ((bf16[8,2,64,256]{3,2,1,0:T(8,128)(2,1)}), bf16[8,2,64,256]{3,2,1,0:T(8,128)(2,1)S(1)}, u32[]{:S(2)}, u32[]{:S(2)}) async-start(bf16[8,2,64,256]{3,2,1,0:T(8,128)(2,1)} %bitcast.26), calls=%async_computation.3 | async-start | bytes 1048576 | tf_op jit(solution)/shard_map/all_to_all | solution.py:374
  91.5 38.6 %collective-permute-start.1 = (bf16[272,1024]{1,0:T(8,128)(2,1)}, bf16[272,1024]{1,0:T(8,128)(2,1)}, u32[]{:S(2)}, u32[]{:S(2)}) collective-permute-start(bf16[272,1024]{1,0:T(8,128)(2,1)} %fusion.1), channel_id=1, source_target_pairs={{8,0},{10,2},{12,4},{14,6},{0,8},{2,10},{4,12},{6,14},{24,16},{26,... | collective-permute-start | bytes 1671176 | tf_op jit(solution)/shard_map/ppermute | solution.py:317
  104.5 26.9 %collective-permute-start.12 = (bf16[256,1024]{1,0:T(8,128)(2,1)}, bf16[256,1024]{1,0:T(8,128)(2,1)}, u32[]{:S(2)}, u32[]{:S(2)}) collective-permute-start(bf16[256,1024]{1,0:T(8,128)(2,1)} %constant_dynamic-update-slice_fusion.refs_12_), channel_id=1, source_target_pairs={{4,0},{6,2},{0,4},{2,6},{12,8},{14,10},{8,12},{10,14},{20,16},{22,... | collective-permute-start | bytes 1572872 | tf_op jit(solution)/shard_map/ppermute | solution.py:317
  106.0 45.6 %collective-permute-start.8 = (bf16[256,2048]{1,0:T(8,128)(2,1)}, bf16[256,2048]{1,0:T(8,128)(2,1)S(1)}, u32[]{:S(2)}, u32[]{:S(2)}) collective-permute-start(bf16[256,2048]{1,0:T(8,128)(2,1)} %collective-permute-done.7.refs_10_), channel_id=1, source_target_pairs={{2,0},{0,2},{6,4},{4,6},{10,8},{8,10},{14,12},{12,14},{18,16},{16,... | collective-permute-start | bytes 3145736 | tf_op jit(solution)/shard_map/ppermute | solution.py:317
  125.8 18.2 %all-to-all-start.1 = ((bf16[8,2,64,256]{3,2,1,0:T(8,128)(2,1)}), bf16[8,2,64,256]{3,2,1,0:T(8,128)(2,1)S(1)}, u32[]{:S(2)}, u32[]{:S(2)}) async-start(bf16[8,2,64,256]{3,2,1,0:T(8,128)(2,1)} %bitcast.25), calls=%async_computation.1 | async-start | bytes 1048576 | tf_op jit(solution)/shard_map/all_to_all | solution.py:374
  129.5 7.0 %collective-permute-start.11 = (bf16[256,1024]{1,0:T(8,128)(2,1)}, bf16[256,1024]{1,0:T(8,128)(2,1)}, u32[]{:S(2)}, u32[]{:S(2)}) collective-permute-start(bf16[256,1024]{1,0:T(8,128)(2,1)} %constant_dynamic-update-slice_fusion.refs_12_), channel_id=1, source_target_pairs={{2,0},{0,2},{6,4},{4,6},{10,8},{8,10},{14,12},{12,14},{18,16},{16,... | collective-permute-start | bytes 1572872 | tf_op jit(solution)/shard_map/ppermute | solution.py:317
  130.0 19.5 %collective-permute-start.17 = (bf16[256,1024]{1,0:T(8,128)(2,1)}, bf16[256,1024]{1,0:T(8,128)(2,1)}, u32[]{:S(2)}, u32[]{:S(2)}) collective-permute-start(bf16[256,1024]{1,0:T(8,128)(2,1)} %collective-permute-done.15.refs_12_), channel_id=1, source_target_pairs={{4,0},{6,2},{0,4},{2,6},{12,8},{14,10},{8,12},{10,14},{20,16},{22,... | collective-permute-start | bytes 1572872 | tf_op jit(solution)/shard_map/ppermute | solution.py:317
  131.4 19.5 %collective-permute-start.13 = (bf16[256,1024]{1,0:T(8,128)(2,1)}, bf16[256,1024]{1,0:T(8,128)(2,1)}, u32[]{:S(2)}, u32[]{:S(2)}) collective-permute-start(bf16[256,1024]{1,0:T(8,128)(2,1)} %collective-permute-done.12.refs_14_), channel_id=1, source_target_pairs={{2,0},{0,2},{6,4},{4,6},{10,8},{8,10},{14,12},{12,14},{18,16},{16,... | collective-permute-start | bytes 1572872 | tf_op jit(solution)/shard_map/ppermute | solution.py:317
  136.5 15.0 %collective-permute-start.3 = (bf16[2,256,256]{2,1,0:T(8,128)(2,1)}, bf16[2,256,256]{2,1,0:T(8,128)(2,1)S(1)}, u32[]{:S(2)}, u32[]{:S(2)}) collective-permute-start(bf16[2,256,256]{2,1,0:T(8,128)(2,1)} %get-tuple-element.14.refs_1_), channel_id=1, source_target_pairs={{1,0},{0,1},{3,2},{2,3},{5,4},{4,5},{7,6},{6,7},{9,8},{8,9},{11,10... | collective-permute-start | bytes 786440 | tf_op jit(solution)/shard_map/ppermute | solution.py:317
  147.9 9.2 %collective-permute-start.5 = (bf16[2,256,256]{2,1,0:T(8,128)(2,1)S(1)}, bf16[2,256,256]{2,1,0:T(8,128)(2,1)S(1)}, u32[]{:S(2)}, u32[]{:S(2)}) collective-permute-start(bf16[2,256,256]{2,1,0:T(8,128)(2,1)S(1)} %copy-done.7), channel_id=1, source_target_pairs={{1,0},{0,1},{3,2},{2,3},{5,4},{4,5},{7,6},{6,7},{9,8},{8,9},{11,10... | collective-permute-start | bytes 786440 | tf_op jit(solution)/shard_map/ppermute | solution.py:317
  149.5 13.3 %collective-permute-start.2 = (bf16[2,256,256]{2,1,0:T(8,128)(2,1)}, bf16[2,256,256]{2,1,0:T(8,128)(2,1)S(1)}, u32[]{:S(2)}, u32[]{:S(2)}) collective-permute-start(bf16[2,256,256]{2,1,0:T(8,128)(2,1)} %get-tuple-element.13.refs_0_), channel_id=1, source_target_pairs={{1,0},{0,1},{3,2},{2,3},{5,4},{4,5},{7,6},{6,7},{9,8},{8,9},{11,10... | collective-permute-start | bytes 786440 | tf_op jit(solution)/shard_map/ppermute | solution.py:317
  150.9 16.5 %collective-permute-start.4 = (bf16[2,256,256]{2,1,0:T(8,128)(2,1)}, bf16[2,256,256]{2,1,0:T(8,128)(2,1)S(1)}, u32[]{:S(2)}, u32[]{:S(2)}) collective-permute-start(bf16[2,256,256]{2,1,0:T(8,128)(2,1)} %get-tuple-element.15.refs_4_), channel_id=1, source_target_pairs={{1,0},{0,1},{3,2},{2,3},{5,4},{4,5},{7,6},{6,7},{9,8},{8,9},{11,10... | collective-permute-start | bytes 786440 | tf_op jit(solution)/shard_map/ppermute | solution.py:317
  151.6 23.6 %collective-permute-start.16 = (bf16[256,1024]{1,0:T(8,128)(2,1)}, bf16[256,1024]{1,0:T(8,128)(2,1)S(1)}, u32[]{:S(2)}, u32[]{:S(2)}) collective-permute-start(bf16[256,1024]{1,0:T(8,128)(2,1)} %collective-permute-done.15.refs_12_), channel_id=1, source_target_pairs={{2,0},{0,2},{6,4},{4,6},{10,8},{8,10},{14,12},{12,14},{18,16},{16,... | collective-permute-start | bytes 1572872 | tf_op jit(solution)/shard_map/ppermute | solution.py:317
  151.6 23.6 %collective-permute-start.18 = (bf16[256,1024]{1,0:T(8,128)(2,1)}, bf16[256,1024]{1,0:T(8,128)(2,1)}, u32[]{:S(2)}, u32[]{:S(2)}) collective-permute-start(bf16[256,1024]{1,0:T(8,128)(2,1)} %collective-permute-done.17.refs_14_), channel_id=1, source_target_pairs={{2,0},{0,2},{6,4},{4,6},{10,8},{8,10},{14,12},{12,14},{18,16},{16,... | collective-permute-start | bytes 1572872 | tf_op jit(solution)/shard_map/ppermute | solution.py:317
  175.1 15.1 %collective-permute-start.14 = (bf16[256,1024]{1,0:T(8,128)(2,1)}, bf16[256,1024]{1,0:T(8,128)(2,1)S(1)}, u32[]{:S(2)}, u32[]{:S(2)}) collective-permute-start(bf16[256,1024]{1,0:T(8,128)(2,1)} %get-tuple-element.18), channel_id=1, source_target_pairs={{8,0},{10,2},{12,4},{14,6},{0,8},{2,10},{4,12},{6,14},{24,16},{26,... | collective-permute-start | bytes 1572872 | tf_op jit(solution)/shard_map/ppermute | solution.py:317
  182.9 16.7 %collective-permute-start.19 = (bf16[256,1024]{1,0:T(8,128)(2,1)}, bf16[256,1024]{1,0:T(8,128)(2,1)S(1)}, u32[]{:S(2)}, u32[]{:S(2)}) collective-permute-start(bf16[256,1024]{1,0:T(8,128)(2,1)} %get-tuple-element.20), channel_id=1, source_target_pairs={{8,0},{10,2},{12,4},{14,6},{0,8},{2,10},{4,12},{6,14},{24,16},{26,... | collective-permute-start | bytes 1572872 | tf_op jit(solution)/shard_map/ppermute | solution.py:317
  (18 other events, 171.6 us)

commit v5 on v4

--- a/solution.py
+++ b/solution.py
@@ -9,7 +9,7 @@
 
 
 TAPS = 3
-PARTS = 2
+PARTS = (1, 1)
 CUTS = 2
 LANES = 128
 PACK = 16
@@ -141,7 +141,7 @@
             y_ref[place(i), :, e * LANES : (e + 1) * LANES] = total.astype(jnp.bfloat16)
 
 
-def convolve(x, f, skip, chans, gain, part, place):
+def convolve(x, f, chans, gain, place, x_at, f_at, gain_at):
     n, _, tok = x.shape
     width = min(16, chans)
     halves = tok // LANES
@@ -150,9 +150,9 @@
         functools.partial(conv_kernel, n, tok, width, place),
         grid=(chans // width,),
         in_specs=[
-            pl.BlockSpec((n, width, tok), lambda g: (0, g, 0)),
-            pl.BlockSpec((n, width // 2, tok), lambda g: (0, g + skip // (width // 2), 0)),
-            pl.BlockSpec((width, LANES), lambda g: (g + part * (chans // width), 0)),
+            pl.BlockSpec((n, width, tok), lambda g: (0, x_at(g), 0)),
+            pl.BlockSpec((n, width // 2, tok), lambda g: (0, f_at(g), 0)),
+            pl.BlockSpec((width, LANES), lambda g: (gain_at(g), 0)),
         ],
         out_specs=pl.BlockSpec((n, width, tok), lambda g: (0, g, 0)),
         out_shape=jax.ShapeDtypeStruct((n, chans, tok), jnp.bfloat16),
@@ -166,40 +166,46 @@
     )(x, f, gain)
 
 
-def mix(key_feat, value_feat, edges, short_filter, part, parts, outer, inner, *taps):
+def mix(key_feat, value_feat, edges, short_filter, start, blocks, wide, outer, inner, *taps):
     tokens, channels = key_feat.shape
-    wide = channels // (2 * parts)
     each = wide // (outer * inner)
     each += each // 2 * len(taps)
-    rows = pl.BlockSpec((tokens, wide), lambda g: (0, g * parts + part))
+    per = channels // (2 * wide)
+    rows = pl.BlockSpec((tokens, wide), lambda t, g: (0, t * per + start + g))
     return pl.pallas_call(
         mix_kernel,
-        grid=(2,),
+        grid=(2, blocks),
         in_specs=[
             rows,
             rows,
-            pl.BlockSpec((3, TAPS - 1, wide), lambda g: (0, 0, g * parts + part)),
-            pl.BlockSpec((3, TAPS, wide), lambda g: (0, 0, g * parts + part)),
+            pl.BlockSpec((3, TAPS - 1, wide), lambda t, g: (0, 0, t * per + start + g)),
+            pl.BlockSpec((3, TAPS, wide), lambda t, g: (0, 0, t * per + start + g)),
         ]
-        + [pl.BlockSpec((wide // 2, tokens), lambda g: (g * parts + part, 0))] * len(taps),
-        out_specs=pl.BlockSpec((outer, 1, inner, each, tokens), lambda g: (0, g, 0, 0, 0)),
-        out_shape=jax.ShapeDtypeStruct((outer, 2, inner, each, tokens), jnp.bfloat16),
+        + [pl.BlockSpec((wide // 2, tokens), lambda t, g: (t * per + start + g, 0))] * len(taps),
+        out_specs=pl.BlockSpec((outer, 1, inner, each, tokens), lambda t, g: (0, t, 0, g, 0)),
+        out_shape=jax.ShapeDtypeStruct((outer, 2, inner, blocks * each, tokens), jnp.bfloat16),
         name="mix",
     )(key_feat, value_feat, edges, short_filter, *taps)
 
 
 def gate(spot, short_filter, conv, first, wide, *sources):
     count = len(sources)
-    origins, _, each, tokens = conv.shape
-    blocks = origins * each // wide
+    origins, _, chans, tokens = conv.shape
+    blocks = origins * chans // wide
+    each = max(wide // origins, 1)
+    each = each if chans % each == 0 and each % 8 == 0 else chans
     per = wide // each
     specs, operands = [], []
     for own, (query, edge) in enumerate(sources):
-        column = lambda g, spot, own=own: (0, spot[1 + 2 * own] + g + first * blocks)
+        column = lambda g, spot, own=own: (0, spot[1 + 2 * own] + g + first)
+
+        def part(g, spot, own=own):
+            return (0, spot[2 + 2 * own], g, 0) if per == origins else (g, spot[2 + 2 * own], 0, 0)
+
         specs += [
             pl.BlockSpec((tokens, wide), column),
             pl.BlockSpec((TAPS - 1, wide), column),
-            pl.BlockSpec((per, 1, each, tokens), lambda g, spot, own=own: (g, spot[2 + 2 * own], 0, 0)),
+            pl.BlockSpec((per, 1, each, tokens), part),
         ]
         operands += [query, edge, conv]
     return pl.pallas_call(
@@ -207,7 +213,7 @@
         grid_spec=pltpu.PrefetchScalarGridSpec(
             num_scalar_prefetch=1,
             grid=(blocks,),
-            in_specs=[pl.BlockSpec((3, TAPS, wide), lambda g, spot: (0, 0, spot[0] + g + first * blocks))] + specs,
+            in_specs=[pl.BlockSpec((3, TAPS, wide), lambda g, spot: (0, 0, spot[0] + g + first))] + specs,
             out_specs=[pl.BlockSpec((1, tokens, wide), lambda g, spot: (g, 0, 0))] * count,
         ),
         out_shape=[jax.ShapeDtypeStruct((blocks, tokens, wide), jnp.bfloat16)] * count,
@@ -227,10 +233,11 @@
     taps = lax.all_to_all(sent, "seq", split_axis=0, concat_axis=0, tiled=True)
     gain = lax.dynamic_index_in_dim(direct_gain.reshape(devices, 2 * pairs, 1), here, 0, False)
     gain = jnp.broadcast_to(gain, (2 * pairs, LANES))
-    turned = mix(key_feat, value_feat, edges, short_filter, 0, 1, 1, devices // 2)
+    turned = mix(key_feat, value_feat, edges, short_filter, 0, 1, channels // 2, 1, devices // 2)
     turned = turned.reshape(devices, 2 * pairs, tokens)
     spread = lax.all_to_all(turned, "seq", split_axis=0, concat_axis=0, tiled=True)
-    conv = convolve(spread, taps, 0, 2 * pairs, gain, 0, lambda i: i)
+    same = lambda i: i
+    conv = convolve(spread, taps, 2 * pairs, gain, same, same, same, same)
     conv = lax.all_to_all(conv, "seq", split_axis=0, concat_axis=0, tiled=True)
     wide = min(256, channels)
     spot = jnp.zeros((3,), jnp.int32)
@@ -243,19 +250,20 @@
 def project_kernel(count, per, spots, *refs):
     gated, pieces = refs[: 2 * per], refs[2 * per : 2 * per + count]
     kept_ref, given_ref, rows = refs[2 * per + count :]
-    blocks, tokens, wide = gated[0].shape
+    tokens, wide = gated[0].shape[1:]
+    places = [(source, block) for source in range(per) for block in range(gated[source].shape[0])]
 
     @pl.when(pl.program_id(0) == 0)
     def _():
         for piece in range(count):
             spot = spots[piece]
             columns = slice(piece * wide, (piece + 1) * wide)
-            for source in range(per):
-
-                @pl.when(spot // blocks == source)
+            for value, (source, block) in enumerate(places):
+
+                @pl.when(spot == value)
                 def _():
-                    rows[:tokens, columns] = gated[source][lax.rem(spot, blocks)]
-                    rows[tokens:, columns] = gated[per + source][lax.rem(spot, blocks)]
+                    rows[:tokens, columns] = gated[source][block]
+                    rows[tokens:, columns] = gated[per + source][block]
 
     total = None
     for piece in range(count):
@@ -270,7 +278,7 @@
 
 
 def project(spots, kept, given, pieces, columns, first):
-    blocks, tokens, wide = kept[0].shape
+    tokens, wide = kept[0].shape[1:]
     count = len(pieces)
     step = min(512, columns)
 
@@ -278,14 +286,14 @@
         skip = first // step if piece.shape[1] > columns else 0
         return pl.BlockSpec((wide, step), lambda j, spots: (0, j + skip))
 
-    whole = pl.BlockSpec((blocks, tokens, wide), lambda j, spots: (0, 0, 0))
+    whole = [pl.BlockSpec(block.shape, lambda j, spots: (0, 0, 0)) for block in (*kept, *given)]
     out = pl.BlockSpec((tokens, step), lambda j, spots: (0, j))
     return pl.pallas_call(
         functools.partial(project_kernel, count, len(kept)),
         grid_spec=pltpu.PrefetchScalarGridSpec(
             num_scalar_prefetch=1,
             grid=(columns // step,),
-            in_specs=[whole] * (2 * len(kept)) + [held(piece) for piece in pieces],
+            in_specs=whole + [held(piece) for piece in pieces],
             out_specs=[out, out],
             scratch_shapes=[pltpu.VMEM((2 * tokens, count * wide), jnp.bfloat16)],
         ),
@@ -309,7 +317,11 @@
     small = sides == 2 and outer == 2 and depth % 256 == 0
     if not small:
         return plain(query_feat, key_feat, value_feat, short_filter, long_filter, direct_gain, out_weight)
-    parts = PARTS
+    half = channels // 2
+    wide = depth
+    parts = [half // wide * share // sum(PARTS) for share in PARTS]
+    starts = [sum(parts[:part]) for part in range(len(parts))]
+    each = wide // (devices // 2)
     twin = here // inner % 2
     rank = here // (2 * inner) * inner + here % inner
 
@@ -343,12 +355,10 @@
         spots.append((owner // (2 * inner) != place) * inner + owner % inner)
     spots = jnp.stack(spots).astype(jnp.int32)
 
-    gain = direct_gain.reshape(2, parts, devices // 2, 2 * pairs // parts)
+    gain = direct_gain.reshape(2, half // wide, devices // 2, each)
     gain = lax.dynamic_index_in_dim(lax.dynamic_index_in_dim(gain, twin, 0, False), rank, 1, False)
     gain = jnp.broadcast_to(gain.reshape(2 * pairs, 1), (2 * pairs, LANES))
 
-    half = channels // 2
-    wide = depth
     padded = jnp.pad(edges[0], ((0, PACK - (TAPS - 1)), (0, 0)))
     asked = jnp.concatenate([query_feat, padded], axis=0)
     asked = lax.dynamic_slice_in_dim(asked, (1 - twin) * half, half, 1)
@@ -359,31 +369,38 @@
         return (i // (2 * inner) * inner + i % inner) * 2 + i // inner % 2
 
     groups = [[o * 2 * inner + t * inner + i for o in range(outer) for i in range(inner)] for t in range(2)]
-    spreads, backs = [], []
-    for part in range(parts):
+    spreads, backs, kept, given = [], [], [], []
+    for start, blocks in zip(starts, parts):
         turned = mix(
-            key_feat, value_feat, edges, short_filter, part, parts, outer, inner, long_filter
-        )
-        turned = turned.reshape(devices, 3 * pairs // parts, tokens)
+            key_feat, value_feat, edges, short_filter, start, blocks, wide, outer, inner, long_filter
+        )
+        turned = turned.reshape(devices, blocks * (each + each // 2), tokens)
         spreads.append(lax.all_to_all(turned, "seq", split_axis=0, concat_axis=0, tiled=True))
-    for part in range(parts):
-        chans = 2 * pairs // parts
-        conv = convolve(spreads[part], spreads[part], chans, chans, gain, part, at)
-        conv = conv.reshape(devices // 2, 2, 2 * pairs // parts, tokens)
+    for part, (start, blocks) in enumerate(zip(starts, parts)):
+        width = min(16, each)
+        per = each // width
+        conv = convolve(
+            spreads[part],
+            spreads[part],
+            blocks * each,
+            gain,
+            at,
+            lambda g: g // per * (3 * per // 2) + g % per,
+            lambda g: g // per * (3 * per) + 2 * per + g % per,
+            lambda g: start * per + g,
+        )
+        conv = conv.reshape(devices // 2, 2, blocks * each, tokens)
         backs.append(
             lax.all_to_all(conv, "seq", split_axis=0, concat_axis=0, tiled=True, axis_index_groups=groups)
         )
     blocks = half // wide
     spot = jnp.stack([twin * blocks, twin * blocks, twin, 0 * twin, 1 - twin]).astype(jnp.int32)
-    kept, given = [], []
-    for part in range(parts):
-        own, passed = gate(
-            spot, short_filter, backs[part], part, wide, (query_feat, edges[0]), (asked, asked_edge)
-        )
+    for part, start in enumerate(starts):
+        own, passed = gate(spot, short_filter, backs[part], start, wide, (query_feat, edges[0]), (asked, asked_edge))
         kept.append(own)
         given.append(passed)
     kept_far, given_far = [], []
-    for part in range(parts):
+    for part in range(len(parts)):
         given_far.append(swap(given[part], "ch", 1))
         kept_far.append(swap(kept[part], "ch", 1))
     sums, taken = [], []

time: 202 us -> 203 us (level)
  Pallas kernels: 65.7 us -> 68.1 us
    pallas_call x2, Pallas kernels: 5.96 us -> 8.14 us  [mix(): pl.pallas_call(mix_kernel, grid=(2, blocks), in_specs=[rows, rows, pl.Blo...]
  transfers between devices with their start and end apart: 24 -> 24, of which waited for: 10 -> 10; matrix products, arithmetic and copies ran while one was open for 5% -> 5% of each run, Pallas kernels for 31% -> 32%
where the time goes in v5:
time: 203 us; the launch traced here: 202 us
  Pallas kernels  68.1 us (34%)
  waiting for transfers between devices  61.6 us (30%)
  starting transfers between devices  56.2 us (28%)
  local copies, waits for them, and re-layouts  13.6 us (7%)
  other arithmetic  2.25 us (1%)
    ppermute x19, waiting for transfers between devices, swap(): lax.ppermute(block, axis, [(i ^ mask, i) for i in range(lax.axis_size(axi...  40.3 us
    pallas_call x2, Pallas kernels, convolve(): pl.pallas_call(functools.partial(conv_kernel, n, tok, width, place), grid...  39.8 us
    all_to_all x2, starting transfers between devices, layer(): lax.all_to_all(conv, 'seq', split_axis=0, concat_axis=0, tiled=True, axis...  20.5 us
    ppermute x19, starting transfers between devices, swap(): lax.ppermute(block, axis, [(i ^ mask, i) for i in range(lax.axis_size(axi...  18.6 us
    all_to_all x2, starting transfers between devices, layer(): lax.all_to_all(turned, 'seq', split_axis=0, concat_axis=0, tiled=True)  14.7 us
    all_to_all x2, waiting for transfers between devices, layer(): lax.all_to_all(turned, 'seq', split_axis=0, concat_axis=0, tiled=True)  14.6 us
    pallas_call x2, Pallas kernels, project(): pl.pallas_call(functools.partial(project_kernel, count, len(kept)), grid_...  14 us
    pallas_call x2, Pallas kernels, mix(): pl.pallas_call(mix_kernel, grid=(2, blocks), in_specs=[rows, rows, pl.Blo...  8.14 us
  transfers between devices with their start and end apart: 24, of which 10 were waited for; matrix products, arithmetic and copies ran while one was open for 5% of the time, Pallas kernels for 32%

profile of v5, /device:TPU:0, one launch (start us, length us, event | category | flops | bytes accessed | tf_op | source)
XLA Modules:
  0.0 202.0 jit_solution(12628246781110328694)
XLA Ops:
  1.6 2.4 %collective-permute-start = (bf16[3,2,2048]{2,1,0:T(2,128)(2,1)S(1)}, bf16[3,2,2048]{2,1,0:T(2,128)(2,1)S(1)}, u32[]{:S(2)}, u32[]{:S(2)}) collective-permute-start(bf16[3,2,2048]{2,1,0:T(2,128)(2,1)S(1)} %pad_maximum_fusion.1), channel_id=1, source_target_pairs={{0,2},{2,4},{4,6},{6,8},{8,10},{10,12},{12,14},{14,16},{16,18},{18... | collective-permute-start | bytes 73736 | tf_op jit(solution)/shard_map/ppermute | solution.py:21
  5.5 4.1 %mix.3 = bf16[2,2,4,96,256]{4,3,2,1,0:T(8,128)(2,1)} custom-call(bf16[256,2048]{1,0:T(8,128)(2,1)} %key_ref.3, bf16[256,2048]{1,0:T(8,128)(2,1)} %value_ref.3, bf16[3,2,2048]{2,1,0:T(2,128)(2,1)} %copy-done.15, f32[3,3,2048]{2,1,0:T(4,128)} %refs_0_.7, f32[1024,256]{1,0:T(8,128)} %refs_0_.6), custom_call_target="tpu_custom_call" | custom-call | tf_op jit(solution)/shard_map/mix/pallas_call | solution.py:175
  9.5 9.3 %all-to-all-start.2 = ((bf16[16,96,256]{2,1,0:T(8,128)(2,1)}), bf16[16,96,256]{2,1,0:T(8,128)(2,1)S(1)}, u32[]{:S(2)}, u32[]{:S(2)}) async-start(bf16[16,96,256]{2,1,0:T(8,128)(2,1)} %bitcast.24), calls=%async_computation.2 | async-start | bytes 1572864 | tf_op jit(solution)/shard_map/all_to_all | solution.py:378
  18.8 4.1 %mix.2 = bf16[2,2,4,96,256]{4,3,2,1,0:T(8,128)(2,1)} custom-call(bf16[256,2048]{1,0:T(8,128)(2,1)} %key_ref.3, bf16[256,2048]{1,0:T(8,128)(2,1)} %value_ref.3, bf16[3,2,2048]{2,1,0:T(2,128)(2,1)} %copy-done.15, f32[3,3,2048]{2,1,0:T(4,128)} %refs_0_.7, f32[1024,256]{1,0:T(8,128)} %refs_0_.6), custom_call_target="tpu_custom_call" | custom-call | tf_op jit(solution)/shard_map/mix/pallas_call | solution.py:175
  22.9 14.6 %all-to-all-done.2.x_ref.f_ref = bf16[16,96,256]{2,1,0:T(8,128)(2,1)S(1)} async-done(((bf16[16,96,256]{2,1,0:T(8,128)(2,1)}), bf16[16,96,256]{2,1,0:T(8,128)(2,1)S(1)}, u32[]{:S(2)}, u32[]{:S(2)}) %all-to-all-start.2) | async-done | bytes 786464 | tf_op jit(solution)/shard_map/all_to_all | solution.py:378
  37.5 5.4 %all-to-all-start = ((bf16[16,96,256]{2,1,0:T(8,128)(2,1)}), bf16[16,96,256]{2,1,0:T(8,128)(2,1)S(1)}, u32[]{:S(2)}, u32[]{:S(2)}) async-start(bf16[16,96,256]{2,1,0:T(8,128)(2,1)} %bitcast.23), calls=%async_computation | async-start | bytes 1572864 | tf_op jit(solution)/shard_map/all_to_all | solution.py:378
  45.7 2.4 %collective-permute-start.9 = (bf16[256,512]{1,0:T(8,128)(2,1)}, bf16[256,512]{1,0:T(8,128)(2,1)}, u32[]{:S(2)}, u32[]{:S(2)}) collective-permute-start(bf16[256,512]{1,0:T(8,128)(2,1)} %get-tuple-element.22), channel_id=1, source_target_pairs={{16,0},{18,2},{20,4},{22,6},{24,8},{26,10},{28,12},{30,14},{0,16},... | collective-permute-start | bytes 786440 | tf_op jit(solution)/shard_map/ppermute | solution.py:329
  49.5 2.4 %collective-permute-start.15 = (bf16[256,1024]{1,0:T(8,128)(2,1)}, bf16[256,1024]{1,0:T(8,128)(2,1)}, u32[]{:S(2)}, u32[]{:S(2)}) collective-permute-start(bf16[256,1024]{1,0:T(8,128)(2,1)} %slice.33), channel_id=1, source_target_pairs={{16,0},{18,2},{20,4},{22,6},{24,8},{26,10},{28,12},{30,14},{0,16},... | collective-permute-start | bytes 1572872 | tf_op jit(solution)/shard_map/ppermute | solution.py:329
  52.8 19.9 %convolve.3 = bf16[16,64,256]{2,1,0:T(8,128)(2,1)} custom-call(bf16[16,96,256]{2,1,0:T(8,128)(2,1)} %copy-done.3, bf16[16,96,256]{2,1,0:T(8,128)(2,1)} %copy-done.3, f32[128,128]{1,0:T(8,128)} %broadcast_in_dim.8.gain_ref), custom_call_target="tpu_custom_call" | custom-call | tf_op jit(solution)/shard_map/convolve/pallas_call | solution.py:149
  72.7 16.9 %all-to-all-start.3 = ((bf16[8,2,64,256]{3,2,1,0:T(8,128)(2,1)}), bf16[8,2,64,256]{3,2,1,0:T(8,128)(2,1)S(1)}, u32[]{:S(2)}, u32[]{:S(2)}) async-start(bf16[8,2,64,256]{3,2,1,0:T(8,128)(2,1)} %bitcast.26), calls=%async_computation.3 | async-start | bytes 1048576 | tf_op jit(solution)/shard_map/all_to_all | solution.py:394
  94.2 9.7 %collective-permute-done.10 = bf16[256,512]{1,0:T(8,128)(2,1)} collective-permute-done((bf16[256,512]{1,0:T(8,128)(2,1)}, bf16[256,512]{1,0:T(8,128)(2,1)}, u32[]{:S(2)}, u32[]{:S(2)}) %collective-permute-start.10) | collective-permute-done | bytes 262176 | tf_op jit(solution)/shard_map/ppermute | solution.py:329
  107.1 19.9 %convolve.2 = bf16[16,64,256]{2,1,0:T(8,128)(2,1)} custom-call(bf16[16,96,256]{2,1,0:T(8,128)(2,1)} %copy-done.2, bf16[16,96,256]{2,1,0:T(8,128)(2,1)} %copy-done.2, f32[128,128]{1,0:T(8,128)} %broadcast_in_dim.8.gain_ref), custom_call_target="tpu_custom_call" | custom-call | tf_op jit(solution)/shard_map/convolve/pallas_call | solution.py:149
  127.0 3.7 %all-to-all-start.1 = ((bf16[8,2,64,256]{3,2,1,0:T(8,128)(2,1)}), bf16[8,2,64,256]{3,2,1,0:T(8,128)(2,1)S(1)}, u32[]{:S(2)}, u32[]{:S(2)}) async-start(bf16[8,2,64,256]{3,2,1,0:T(8,128)(2,1)} %bitcast.25), calls=%async_computation.1 | async-start | bytes 1048576 | tf_op jit(solution)/shard_map/all_to_all | solution.py:394
  134.6 3.1 %gate.3 = (bf16[2,256,256]{2,1,0:T(8,128)(2,1)}, bf16[2,256,256]{2,1,0:T(8,128)(2,1)}) custom-call(s32[5]{0:T(128)} %stack.64.spot_ref, f32[3,3,2048]{2,1,0:T(4,128)} %refs_0_.7, bf16[256,2048]{1,0:T(8,128)(2,1)} %refs_1_.3, bf16[2,2048]{1,0:T(2,128)(2,1)} %copy-done.16, bf16[8,2,64,256]{3,2,1,0:T(8,128)(2,1)} %copy-done.4, ...), custom_call_target="tpu_custom_call" | custom-call | tf_op jit(solution)/shard_map/gate/pallas_call | solution.py:211
  139.3 5.9 %all-to-all-done.1.refs_3_.refs_6_ = bf16[8,2,64,256]{3,2,1,0:T(8,128)(2,1)S(1)} async-done(((bf16[8,2,64,256]{3,2,1,0:T(8,128)(2,1)}), bf16[8,2,64,256]{3,2,1,0:T(8,128)(2,1)S(1)}, u32[]{:S(2)}, u32[]{:S(2)}) %all-to-all-start.1) | async-done | bytes 524320 | tf_op jit(solution)/shard_map/all_to_all | solution.py:394
  146.0 3.1 %gate.2 = (bf16[2,256,256]{2,1,0:T(8,128)(2,1)}, bf16[2,256,256]{2,1,0:T(8,128)(2,1)}) custom-call(s32[5]{0:T(128)} %stack.64.spot_ref, f32[3,3,2048]{2,1,0:T(4,128)} %refs_0_.7, bf16[256,2048]{1,0:T(8,128)(2,1)} %refs_1_.3, bf16[2,2048]{1,0:T(2,128)(2,1)} %copy-done.16, bf16[8,2,64,256]{3,2,1,0:T(8,128)(2,1)} %copy-done.5, ...), custom_call_target="tpu_custom_call" | custom-call | tf_op jit(solution)/shard_map/gate/pallas_call | solution.py:211
  153.8 4.5 %collective-permute-done.5.refs_7_ = bf16[2,256,256]{2,1,0:T(8,128)(2,1)S(1)} collective-permute-done((bf16[2,256,256]{2,1,0:T(8,128)(2,1)S(1)}, bf16[2,256,256]{2,1,0:T(8,128)(2,1)S(1)}, u32[]{:S(2)}, u32[]{:S(2)}) %collective-permute-start.5) | collective-permute-done | bytes 262176 | tf_op jit(solution)/shard_map/ppermute | solution.py:329
  158.3 5.6 %collective-permute-done.2.refs_2_ = bf16[2,256,256]{2,1,0:T(8,128)(2,1)S(1)} collective-permute-done((bf16[2,256,256]{2,1,0:T(8,128)(2,1)}, bf16[2,256,256]{2,1,0:T(8,128)(2,1)S(1)}, u32[]{:S(2)}, u32[]{:S(2)}) %collective-permute-start.2) | collective-permute-done | bytes 262176 | tf_op jit(solution)/shard_map/ppermute | solution.py:329
  163.9 4.7 %collective-permute-done.4.refs_6_ = bf16[2,256,256]{2,1,0:T(8,128)(2,1)S(1)} collective-permute-done((bf16[2,256,256]{2,1,0:T(8,128)(2,1)}, bf16[2,256,256]{2,1,0:T(8,128)(2,1)S(1)}, u32[]{:S(2)}, u32[]{:S(2)}) %collective-permute-start.4) | collective-permute-done | bytes 262176 | tf_op jit(solution)/shard_map/ppermute | solution.py:329
  169.3 7.0 %project.2 = (f32[256,1024]{1,0:T(8,128)}, bf16[256,1024]{1,0:T(8,128)(2,1)}) custom-call(s32[8]{0:T(128)} %stack.60.spots, bf16[2,256,256]{2,1,0:T(8,128)(2,1)} %get-tuple-element.13.refs_0_, bf16[2,256,256]{2,1,0:T(8,128)(2,1)} %get-tuple-element.14.refs_1_, bf16[2,256,256]{2,1,0:T(8,128)(2,1)} %copy-done.10, bf16[2,256,256]{2,1,0:T(8,128)(2,1)} %copy-done.8, ...), custom_call_target="tpu_custom_call" | custom-call | tf_op jit(solution)/shard_map/project/pallas_call | solution.py:291
  177.2 7.0 %project.3 = (f32[256,1024]{1,0:T(8,128)}, bf16[256,1024]{1,0:T(8,128)(2,1)}) custom-call(s32[8]{0:T(128)} %stack.60.spots, bf16[2,256,256]{2,1,0:T(8,128)(2,1)} %get-tuple-element.13.refs_0_, bf16[2,256,256]{2,1,0:T(8,128)(2,1)} %get-tuple-element.14.refs_1_, bf16[2,256,256]{2,1,0:T(8,128)(2,1)} %copy-done.10, bf16[2,256,256]{2,1,0:T(8,128)(2,1)} %copy-done.8, ...), custom_call_target="tpu_custom_call" | custom-call | tf_op jit(solution)/shard_map/project/pallas_call | solution.py:291
  184.2 2.1 %collective-permute-start.19 = (bf16[256,1024]{1,0:T(8,128)(2,1)}, bf16[256,1024]{1,0:T(8,128)(2,1)S(1)}, u32[]{:S(2)}, u32[]{:S(2)}) collective-permute-start(bf16[256,1024]{1,0:T(8,128)(2,1)} %get-tuple-element.20), channel_id=1, source_target_pairs={{8,0},{10,2},{12,4},{14,6},{0,8},{2,10},{4,12},{6,14},{24,16},{26,... | collective-permute-start | bytes 1572872 | tf_op jit(solution)/shard_map/ppermute | solution.py:329
  186.3 5.1 %collective-permute-done.14 = bf16[256,1024]{1,0:T(8,128)(2,1)S(1)} collective-permute-done((bf16[256,1024]{1,0:T(8,128)(2,1)}, bf16[256,1024]{1,0:T(8,128)(2,1)S(1)}, u32[]{:S(2)}, u32[]{:S(2)}) %collective-permute-start.14) | collective-permute-done | bytes 524320 | tf_op jit(solution)/shard_map/ppermute | solution.py:329
  191.6 9.2 %collective-permute-done.19 = bf16[256,1024]{1,0:T(8,128)(2,1)S(1)} collective-permute-done((bf16[256,1024]{1,0:T(8,128)(2,1)}, bf16[256,1024]{1,0:T(8,128)(2,1)S(1)}, u32[]{:S(2)}, u32[]{:S(2)}) %collective-permute-start.19) | collective-permute-done | bytes 524320 | tf_op jit(solution)/shard_map/ppermute | solution.py:329
  (87 shorter events, 29.9 us)
Async XLA Ops:
  1.6 3.2 %collective-permute-start = (bf16[3,2,2048]{2,1,0:T(2,128)(2,1)S(1)}, bf16[3,2,2048]{2,1,0:T(2,128)(2,1)S(1)}, u32[]{:S(2)}, u32[]{:S(2)}) collective-permute-start(bf16[3,2,2048]{2,1,0:T(2,128)(2,1)S(1)} %pad_maximum_fusion.1), channel_id=1, source_target_pairs={{0,2},{2,4},{4,6},{6,8},{8,10},{10,12},{12,14},{14,16},{16,18},{18... | collective-permute-start | bytes 73736 | tf_op jit(solution)/shard_map/ppermute | solution.py:21
  9.5 28.0 %all-to-all-start.2 = ((bf16[16,96,256]{2,1,0:T(8,128)(2,1)}), bf16[16,96,256]{2,1,0:T(8,128)(2,1)S(1)}, u32[]{:S(2)}, u32[]{:S(2)}) async-start(bf16[16,96,256]{2,1,0:T(8,128)(2,1)} %bitcast.24), calls=%async_computation.2 | async-start | bytes 1572864 | tf_op jit(solution)/shard_map/all_to_all | solution.py:378
  37.5 35.2 %all-to-all-start = ((bf16[16,96,256]{2,1,0:T(8,128)(2,1)}), bf16[16,96,256]{2,1,0:T(8,128)(2,1)S(1)}, u32[]{:S(2)}, u32[]{:S(2)}) async-start(bf16[16,96,256]{2,1,0:T(8,128)(2,1)} %bitcast.23), calls=%async_computation | async-start | bytes 1572864 | tf_op jit(solution)/shard_map/all_to_all | solution.py:378
  42.9 64.1 %collective-permute-start.7 = (bf16[256,2048]{1,0:T(8,128)(2,1)S(1)}, bf16[256,2048]{1,0:T(8,128)(2,1)}, u32[]{:S(2)}, u32[]{:S(2)}) collective-permute-start(bf16[256,2048]{1,0:T(8,128)(2,1)S(1)} %copy-done.1), channel_id=1, source_target_pairs={{4,0},{6,2},{0,4},{2,6},{12,8},{14,10},{8,12},{10,14},{20,16},{22,... | collective-permute-start | bytes 3145736 | tf_op jit(solution)/shard_map/ppermute | solution.py:329
  44.9 104.2 %collective-permute-start.6 = (bf16[256,2048]{1,0:T(8,128)(2,1)S(1)}, bf16[256,2048]{1,0:T(8,128)(2,1)}, u32[]{:S(2)}, u32[]{:S(2)}) collective-permute-start(bf16[256,2048]{1,0:T(8,128)(2,1)S(1)} %copy-done.1), channel_id=1, source_target_pairs={{2,0},{0,2},{6,4},{4,6},{10,8},{8,10},{14,12},{12,14},{18,16},{16,... | collective-permute-start | bytes 3145736 | tf_op jit(solution)/shard_map/ppermute | solution.py:329
  45.7 46.8 %collective-permute-start.9 = (bf16[256,512]{1,0:T(8,128)(2,1)}, bf16[256,512]{1,0:T(8,128)(2,1)}, u32[]{:S(2)}, u32[]{:S(2)}) collective-permute-start(bf16[256,512]{1,0:T(8,128)(2,1)} %get-tuple-element.22), channel_id=1, source_target_pairs={{16,0},{18,2},{20,4},{22,6},{24,8},{26,10},{28,12},{30,14},{0,16},... | collective-permute-start | bytes 786440 | tf_op jit(solution)/shard_map/ppermute | solution.py:329
  48.1 55.8 %collective-permute-start.10 = (bf16[256,512]{1,0:T(8,128)(2,1)}, bf16[256,512]{1,0:T(8,128)(2,1)}, u32[]{:S(2)}, u32[]{:S(2)}) collective-permute-start(bf16[256,512]{1,0:T(8,128)(2,1)} %get-tuple-element.21), channel_id=1, source_target_pairs={{16,0},{18,2},{20,4},{22,6},{24,8},{26,10},{28,12},{30,14},{0,16},... | collective-permute-start | bytes 786440 | tf_op jit(solution)/shard_map/ppermute | solution.py:329
  49.5 81.1 %collective-permute-start.15 = (bf16[256,1024]{1,0:T(8,128)(2,1)}, bf16[256,1024]{1,0:T(8,128)(2,1)}, u32[]{:S(2)}, u32[]{:S(2)}) collective-permute-start(bf16[256,1024]{1,0:T(8,128)(2,1)} %slice.33), channel_id=1, source_target_pairs={{16,0},{18,2},{20,4},{22,6},{24,8},{26,10},{28,12},{30,14},{0,16},... | collective-permute-start | bytes 1572872 | tf_op jit(solution)/shard_map/ppermute | solution.py:329
  72.7 54.3 %all-to-all-start.3 = ((bf16[8,2,64,256]{3,2,1,0:T(8,128)(2,1)}), bf16[8,2,64,256]{3,2,1,0:T(8,128)(2,1)S(1)}, u32[]{:S(2)}, u32[]{:S(2)}) async-start(bf16[8,2,64,256]{3,2,1,0:T(8,128)(2,1)} %bitcast.26), calls=%async_computation.3 | async-start | bytes 1048576 | tf_op jit(solution)/shard_map/all_to_all | solution.py:394
  92.6 38.6 %collective-permute-start.1 = (bf16[272,1024]{1,0:T(8,128)(2,1)}, bf16[272,1024]{1,0:T(8,128)(2,1)}, u32[]{:S(2)}, u32[]{:S(2)}) collective-permute-start(bf16[272,1024]{1,0:T(8,128)(2,1)} %fusion.1), channel_id=1, source_target_pairs={{8,0},{10,2},{12,4},{14,6},{0,8},{2,10},{4,12},{6,14},{24,16},{26,... | collective-permute-start | bytes 1671176 | tf_op jit(solution)/shard_map/ppermute | solution.py:329
  105.6 27.0 %collective-permute-start.12 = (bf16[256,1024]{1,0:T(8,128)(2,1)}, bf16[256,1024]{1,0:T(8,128)(2,1)}, u32[]{:S(2)}, u32[]{:S(2)}) collective-permute-start(bf16[256,1024]{1,0:T(8,128)(2,1)} %constant_dynamic-update-slice_fusion.refs_12_), channel_id=1, source_target_pairs={{4,0},{6,2},{0,4},{2,6},{12,8},{14,10},{8,12},{10,14},{20,16},{22,... | collective-permute-start | bytes 1572872 | tf_op jit(solution)/shard_map/ppermute | solution.py:329
  107.0 45.6 %collective-permute-start.8 = (bf16[256,2048]{1,0:T(8,128)(2,1)}, bf16[256,2048]{1,0:T(8,128)(2,1)S(1)}, u32[]{:S(2)}, u32[]{:S(2)}) collective-permute-start(bf16[256,2048]{1,0:T(8,128)(2,1)} %collective-permute-done.7.refs_10_), channel_id=1, source_target_pairs={{2,0},{0,2},{6,4},{4,6},{10,8},{8,10},{14,12},{12,14},{18,16},{16,... | collective-permute-start | bytes 3145736 | tf_op jit(solution)/shard_map/ppermute | solution.py:329
  127.0 18.2 %all-to-all-start.1 = ((bf16[8,2,64,256]{3,2,1,0:T(8,128)(2,1)}), bf16[8,2,64,256]{3,2,1,0:T(8,128)(2,1)S(1)}, u32[]{:S(2)}, u32[]{:S(2)}) async-start(bf16[8,2,64,256]{3,2,1,0:T(8,128)(2,1)} %bitcast.25), calls=%async_computation.1 | async-start | bytes 1048576 | tf_op jit(solution)/shard_map/all_to_all | solution.py:394
  130.7 7.0 %collective-permute-start.11 = (bf16[256,1024]{1,0:T(8,128)(2,1)}, bf16[256,1024]{1,0:T(8,128)(2,1)}, u32[]{:S(2)}, u32[]{:S(2)}) collective-permute-start(bf16[256,1024]{1,0:T(8,128)(2,1)} %constant_dynamic-update-slice_fusion.refs_12_), channel_id=1, source_target_pairs={{2,0},{0,2},{6,4},{4,6},{10,8},{8,10},{14,12},{12,14},{18,16},{16,... | collective-permute-start | bytes 1572872 | tf_op jit(solution)/shard_map/ppermute | solution.py:329
  131.2 19.5 %collective-permute-start.17 = (bf16[256,1024]{1,0:T(8,128)(2,1)}, bf16[256,1024]{1,0:T(8,128)(2,1)}, u32[]{:S(2)}, u32[]{:S(2)}) collective-permute-start(bf16[256,1024]{1,0:T(8,128)(2,1)} %collective-permute-done.15.refs_12_), channel_id=1, source_target_pairs={{4,0},{6,2},{0,4},{2,6},{12,8},{14,10},{8,12},{10,14},{20,16},{22,... | collective-permute-start | bytes 1572872 | tf_op jit(solution)/shard_map/ppermute | solution.py:329
  132.5 19.5 %collective-permute-start.13 = (bf16[256,1024]{1,0:T(8,128)(2,1)}, bf16[256,1024]{1,0:T(8,128)(2,1)}, u32[]{:S(2)}, u32[]{:S(2)}) collective-permute-start(bf16[256,1024]{1,0:T(8,128)(2,1)} %collective-permute-done.12.refs_14_), channel_id=1, source_target_pairs={{2,0},{0,2},{6,4},{4,6},{10,8},{8,10},{14,12},{12,14},{18,16},{16,... | collective-permute-start | bytes 1572872 | tf_op jit(solution)/shard_map/ppermute | solution.py:329
  137.7 15.0 %collective-permute-start.3 = (bf16[2,256,256]{2,1,0:T(8,128)(2,1)}, bf16[2,256,256]{2,1,0:T(8,128)(2,1)S(1)}, u32[]{:S(2)}, u32[]{:S(2)}) collective-permute-start(bf16[2,256,256]{2,1,0:T(8,128)(2,1)} %get-tuple-element.14.refs_1_), channel_id=1, source_target_pairs={{1,0},{0,1},{3,2},{2,3},{5,4},{4,5},{7,6},{6,7},{9,8},{8,9},{11,10... | collective-permute-start | bytes 786440 | tf_op jit(solution)/shard_map/ppermute | solution.py:329
  149.1 9.2 %collective-permute-start.5 = (bf16[2,256,256]{2,1,0:T(8,128)(2,1)S(1)}, bf16[2,256,256]{2,1,0:T(8,128)(2,1)S(1)}, u32[]{:S(2)}, u32[]{:S(2)}) collective-permute-start(bf16[2,256,256]{2,1,0:T(8,128)(2,1)S(1)} %copy-done.7), channel_id=1, source_target_pairs={{1,0},{0,1},{3,2},{2,3},{5,4},{4,5},{7,6},{6,7},{9,8},{8,9},{11,10... | collective-permute-start | bytes 786440 | tf_op jit(solution)/shard_map/ppermute | solution.py:329
  150.7 13.3 %collective-permute-start.2 = (bf16[2,256,256]{2,1,0:T(8,128)(2,1)}, bf16[2,256,256]{2,1,0:T(8,128)(2,1)S(1)}, u32[]{:S(2)}, u32[]{:S(2)}) collective-permute-start(bf16[2,256,256]{2,1,0:T(8,128)(2,1)} %get-tuple-element.13.refs_0_), channel_id=1, source_target_pairs={{1,0},{0,1},{3,2},{2,3},{5,4},{4,5},{7,6},{6,7},{9,8},{8,9},{11,10... | collective-permute-start | bytes 786440 | tf_op jit(solution)/shard_map/ppermute | solution.py:329
  152.1 16.5 %collective-permute-start.4 = (bf16[2,256,256]{2,1,0:T(8,128)(2,1)}, bf16[2,256,256]{2,1,0:T(8,128)(2,1)S(1)}, u32[]{:S(2)}, u32[]{:S(2)}) collective-permute-start(bf16[2,256,256]{2,1,0:T(8,128)(2,1)} %get-tuple-element.15.refs_4_), channel_id=1, source_target_pairs={{1,0},{0,1},{3,2},{2,3},{5,4},{4,5},{7,6},{6,7},{9,8},{8,9},{11,10... | collective-permute-start | bytes 786440 | tf_op jit(solution)/shard_map/ppermute | solution.py:329
  152.7 23.7 %collective-permute-start.16 = (bf16[256,1024]{1,0:T(8,128)(2,1)}, bf16[256,1024]{1,0:T(8,128)(2,1)S(1)}, u32[]{:S(2)}, u32[]{:S(2)}) collective-permute-start(bf16[256,1024]{1,0:T(8,128)(2,1)} %collective-permute-done.15.refs_12_), channel_id=1, source_target_pairs={{2,0},{0,2},{6,4},{4,6},{10,8},{8,10},{14,12},{12,14},{18,16},{16,... | collective-permute-start | bytes 1572872 | tf_op jit(solution)/shard_map/ppermute | solution.py:329
  152.7 23.7 %collective-permute-start.18 = (bf16[256,1024]{1,0:T(8,128)(2,1)}, bf16[256,1024]{1,0:T(8,128)(2,1)}, u32[]{:S(2)}, u32[]{:S(2)}) collective-permute-start(bf16[256,1024]{1,0:T(8,128)(2,1)} %collective-permute-done.17.refs_14_), channel_id=1, source_target_pairs={{2,0},{0,2},{6,4},{4,6},{10,8},{8,10},{14,12},{12,14},{18,16},{16,... | collective-permute-start | bytes 1572872 | tf_op jit(solution)/shard_map/ppermute | solution.py:329
  176.3 15.1 %collective-permute-start.14 = (bf16[256,1024]{1,0:T(8,128)(2,1)}, bf16[256,1024]{1,0:T(8,128)(2,1)S(1)}, u32[]{:S(2)}, u32[]{:S(2)}) collective-permute-start(bf16[256,1024]{1,0:T(8,128)(2,1)} %get-tuple-element.18), channel_id=1, source_target_pairs={{8,0},{10,2},{12,4},{14,6},{0,8},{2,10},{4,12},{6,14},{24,16},{26,... | collective-permute-start | bytes 1572872 | tf_op jit(solution)/shard_map/ppermute | solution.py:329
  184.2 16.6 %collective-permute-start.19 = (bf16[256,1024]{1,0:T(8,128)(2,1)}, bf16[256,1024]{1,0:T(8,128)(2,1)S(1)}, u32[]{:S(2)}, u32[]{:S(2)}) collective-permute-start(bf16[256,1024]{1,0:T(8,128)(2,1)} %get-tuple-element.20), channel_id=1, source_target_pairs={{8,0},{10,2},{12,4},{14,6},{0,8},{2,10},{4,12},{6,14},{24,16},{26,... | collective-permute-start | bytes 1572872 | tf_op jit(solution)/shard_map/ppermute | solution.py:329
  (18 other events, 170.4 us)

commit v6 on v5

--- a/solution.py
+++ b/solution.py
@@ -34,19 +34,25 @@
     return total
 
 
-def mix_kernel(key_ref, value_ref, edge_ref, short_ref, *refs):
+def mix_kernel(wide, key_ref, value_ref, edge_ref, short_ref, *refs):
     sent_ref = refs[-1]
     outer, _, inner, _, tokens = sent_ref.shape
     edge = edge_ref[...].astype(jnp.float32)
     mixed = featurized(key_ref[...], edge[1], short_ref[1]) * featurized(
         value_ref[...], edge[2], short_ref[2]
     )
-    each = mixed.shape[1] // (outer * inner)
+    each = wide // (outer * inner)
     turned = mixed.T.astype(jnp.bfloat16)
-    sent_ref[:, 0, :, 0:each, :] = turned.reshape(outer, inner, each, tokens)
-    for taps_ref in refs[:-1]:
-        taps = taps_ref[...].astype(jnp.bfloat16)
-        sent_ref[:, 0, :, each:, :] = taps.reshape(outer, inner, each // 2, tokens)
+    row = 0
+    for block in range(mixed.shape[1] // wide):
+        part = turned[block * wide : (block + 1) * wide]
+        sent_ref[:, 0, :, row : row + each, :] = part.reshape(outer, inner, each, tokens)
+        row += each
+        for taps_ref in refs[:-1]:
+            half = wide // 2
+            taps = taps_ref[block * half : (block + 1) * half, :].astype(jnp.bfloat16)
+            sent_ref[:, 0, :, row : row + each // 2, :] = taps.reshape(outer, inner, each // 2, tokens)
+            row += each // 2
 
 
 def gate_kernel(count, *refs):
@@ -171,18 +177,20 @@
     each = wide // (outer * inner)
     each += each // 2 * len(taps)
     per = channels // (2 * wide)
-    rows = pl.BlockSpec((tokens, wide), lambda t, g: (0, t * per + start + g))
+    many = 2 if start % 2 == blocks % 2 == per % 2 == 0 else 1
+    rows = pl.BlockSpec((tokens, many * wide), lambda t, g: (0, (t * per + start) // many + g))
     return pl.pallas_call(
-        mix_kernel,
-        grid=(2, blocks),
+        functools.partial(mix_kernel, wide),
+        grid=(2, blocks // many),
         in_specs=[
             rows,
             rows,
-            pl.BlockSpec((3, TAPS - 1, wide), lambda t, g: (0, 0, t * per + start + g)),
-            pl.BlockSpec((3, TAPS, wide), lambda t, g: (0, 0, t * per + start + g)),
+            pl.BlockSpec((3, TAPS - 1, many * wide), lambda t, g: (0, 0, (t * per + start) // many + g)),
+            pl.BlockSpec((3, TAPS, many * wide), lambda t, g: (0, 0, (t * per + start) // many + g)),
         ]
-        + [pl.BlockSpec((wide // 2, tokens), lambda t, g: (t * per + start + g, 0))] * len(taps),
-        out_specs=pl.BlockSpec((outer, 1, inner, each, tokens), lambda t, g: (0, t, 0, g, 0)),
+        + [pl.BlockSpec((many * wide // 2, tokens), lambda t, g: ((t * per + start) // many + g, 0))]
+        * len(taps),
+        out_specs=pl.BlockSpec((outer, 1, inner, many * each, tokens), lambda t, g: (0, t, 0, g, 0)),
         out_shape=jax.ShapeDtypeStruct((outer, 2, inner, blocks * each, tokens), jnp.bfloat16),
         name="mix",
     )(key_feat, value_feat, edges, short_filter, *taps)
@@ -248,22 +256,20 @@
 
 
 def project_kernel(count, per, spots, *refs):
-    gated, pieces = refs[: 2 * per], refs[2 * per : 2 * per + count]
-    kept_ref, given_ref, rows = refs[2 * per + count :]
-    tokens, wide = gated[0].shape[1:]
+    gated, pieces = refs[:per], refs[per : per + count]
+    out_ref, rows = refs[per + count :]
+    wide = gated[0].shape[2]
     places = [(source, block) for source in range(per) for block in range(gated[source].shape[0])]
 
     @pl.when(pl.program_id(0) == 0)
     def _():
         for piece in range(count):
             spot = spots[piece]
-            columns = slice(piece * wide, (piece + 1) * wide)
             for value, (source, block) in enumerate(places):
 
                 @pl.when(spot == value)
                 def _():
-                    rows[:tokens, columns] = gated[source][block]
-                    rows[tokens:, columns] = gated[per + source][block]
+                    rows[:, piece * wide : (piece + 1) * wide] = gated[source][block]
 
     total = None
     for piece in range(count):
@@ -273,12 +279,11 @@
             preferred_element_type=jnp.float32,
         )
         total = out if total is None else total + out
-    kept_ref[...] = total[:tokens]
-    given_ref[...] = total[tokens:].astype(jnp.bfloat16)
-
-
-def project(spots, kept, given, pieces, columns, first):
-    tokens, wide = kept[0].shape[1:]
+    out_ref[...] = total.astype(out_ref.dtype)
+
+
+def project(spots, gated, pieces, columns, first, kind):
+    tokens, wide = gated[0].shape[1:]
     count = len(pieces)
     step = min(512, columns)
 
@@ -286,23 +291,19 @@
         skip = first // step if piece.shape[1] > columns else 0
         return pl.BlockSpec((wide, step), lambda j, spots: (0, j + skip))
 
-    whole = [pl.BlockSpec(block.shape, lambda j, spots: (0, 0, 0)) for block in (*kept, *given)]
-    out = pl.BlockSpec((tokens, step), lambda j, spots: (0, j))
     return pl.pallas_call(
-        functools.partial(project_kernel, count, len(kept)),
+        functools.partial(project_kernel, count, len(gated)),
         grid_spec=pltpu.PrefetchScalarGridSpec(
             num_scalar_prefetch=1,
             grid=(columns // step,),
-            in_specs=whole + [held(piece) for piece in pieces],
-            out_specs=[out, out],
-            scratch_shapes=[pltpu.VMEM((2 * tokens, count * wide), jnp.bfloat16)],
+            in_specs=[pl.BlockSpec(block.shape, lambda j, spots: (0, 0, 0)) for block in gated]
+            + [held(piece) for piece in pieces],
+            out_specs=pl.BlockSpec((tokens, step), lambda j, spots: (0, j)),
+            scratch_shapes=[pltpu.VMEM((tokens, count * wide), jnp.bfloat16)],
         ),
-        out_shape=[
-            jax.ShapeDtypeStruct((tokens, columns), jnp.float32),
-            jax.ShapeDtypeStruct((tokens, columns), jnp.bfloat16),
-        ],
+        out_shape=jax.ShapeDtypeStruct((tokens, columns), kind),
         name="project",
-    )(spots, *kept, *given, *pieces)
+    )(spots, *gated, *pieces)
 
 
 def layer(query_feat, key_feat, value_feat, short_filter, long_filter, direct_gain, out_weight):
@@ -405,11 +406,10 @@
         kept_far.append(swap(kept[part], "ch", 1))
     sums, taken = [], []
     for cut in range(CUTS):
-        held, passed = project(
-            spots, kept + kept_far, given + given_far, pieces[cut], span, cut * span
-        )
-        sums.append(held)
+        passed = project(spots, given + given_far, pieces[cut], span, cut * span, jnp.bfloat16)
         taken.append(swap(passed, "seq", inner))
+    for cut in range(CUTS):
+        sums.append(project(spots, kept + kept_far, pieces[cut], span, cut * span, jnp.float32))
     outs = [(a + b.astype(jnp.float32)).astype(jnp.bfloat16) for a, b in zip(sums, taken)]
     return jnp.concatenate(outs, axis=1)
 

time: 203 us -> 195 us (0.961)
  waiting for transfers between devices: 61.6 us -> 45.1 us
  Pallas kernels: 68.1 us -> 73.8 us
  other arithmetic: 2.25 us -> 5.44 us
    ppermute x19, waiting for transfers between devices: 40.3 us -> 22.2 us  [swap(): lax.ppermute(block, axis, [(i ^ mask, i) for i in range(lax.axis_size(axi...]
    pallas_call x4 -> x6, Pallas kernels: 22.1 us -> 27.7 us  [the longest x4 21.7 us: project(): pl.pallas_call(functools.partial(project_kernel, count, len(gated)), grid...]
    convert_element_type x2, other arithmetic: 0.29 us -> 2.45 us  [layer(): (a + b.astype(jnp.float32)).astype(jnp.bfloat16)]
    unnamed x37 -> x31, local copies, waits for them, and re-layouts: 4.61 us -> 4.76 us
  transfers between devices with their start and end apart: 24 -> 24, of which waited for: 10 -> 9; matrix products, arithmetic and copies ran while one was open for 5% -> 6% of each run, Pallas kernels for 32% -> 36%
where the time goes in v6:
time: 195 us; the launch traced here: 194 us
  Pallas kernels  73.8 us (38%)
  starting transfers between devices  56.6 us (29%)
  waiting for transfers between devices  45.1 us (23%)
  local copies, waits for them, and re-layouts  13 us (7%)
  other arithmetic  5.44 us (3%)
    pallas_call x2, Pallas kernels, convolve(): pl.pallas_call(functools.partial(conv_kernel, n, tok, width, place), grid...  39.8 us
    ppermute x19, waiting for transfers between devices, swap(): lax.ppermute(block, axis, [(i ^ mask, i) for i in range(lax.axis_size(axi...  22.2 us
    pallas_call x4, Pallas kernels, project(): pl.pallas_call(functools.partial(project_kernel, count, len(gated)), grid...  21.7 us
    all_to_all x2, starting transfers between devices, layer(): lax.all_to_all(conv, 'seq', split_axis=0, concat_axis=0, tiled=True, axis...  21.3 us
    ppermute x19, starting transfers between devices, swap(): lax.ppermute(block, axis, [(i ^ mask, i) for i in range(lax.axis_size(axi...  18.2 us
    all_to_all x2, waiting for transfers between devices, layer(): lax.all_to_all(turned, 'seq', split_axis=0, concat_axis=0, tiled=True)  15.7 us
    all_to_all x2, starting transfers between devices, layer(): lax.all_to_all(turned, 'seq', split_axis=0, concat_axis=0, tiled=True)  14.7 us
    all_to_all x2, waiting for transfers between devices, layer(): lax.all_to_all(conv, 'seq', split_axis=0, concat_axis=0, tiled=True, axis...  6.44 us
  transfers between devices with their start and end apart: 24, of which 9 were waited for; matrix products, arithmetic and copies ran while one was open for 6% of the time, Pallas kernels for 36%

profile of v6, /device:TPU:0, one launch (start us, length us, event | category | flops | bytes accessed | tf_op | source)
XLA Modules:
  0.0 194.2 jit_solution(14827208840432434095)
XLA Ops:
  1.6 2.4 %collective-permute-start = (bf16[3,2,2048]{2,1,0:T(2,128)(2,1)S(1)}, bf16[3,2,2048]{2,1,0:T(2,128)(2,1)S(1)}, u32[]{:S(2)}, u32[]{:S(2)}) collective-permute-start(bf16[3,2,2048]{2,1,0:T(2,128)(2,1)S(1)} %pad_maximum_fusion.1), channel_id=1, source_target_pairs={{0,2},{2,4},{4,6},{6,8},{8,10},{10,12},{12,14},{14,16},{16,18},{18... | collective-permute-start | bytes 73736 | tf_op jit(solution)/shard_map/ppermute | solution.py:21
  5.5 3.0 %mix.3 = bf16[2,2,4,96,256]{4,3,2,1,0:T(8,128)(2,1)} custom-call(bf16[256,2048]{1,0:T(8,128)(2,1)} %key_ref.3, bf16[256,2048]{1,0:T(8,128)(2,1)} %value_ref.3, bf16[3,2,2048]{2,1,0:T(2,128)(2,1)} %copy-done.12, f32[3,3,2048]{2,1,0:T(4,128)} %refs_0_.7, f32[1024,256]{1,0:T(8,128)} %refs_0_.6), custom_call_target="tpu_custom_call" | custom-call | tf_op jit(solution)/shard_map/mix/pallas_call | solution.py:182
  8.5 9.3 %all-to-all-start.2 = ((bf16[16,96,256]{2,1,0:T(8,128)(2,1)}), bf16[16,96,256]{2,1,0:T(8,128)(2,1)S(1)}, u32[]{:S(2)}, u32[]{:S(2)}) async-start(bf16[16,96,256]{2,1,0:T(8,128)(2,1)} %bitcast.24), calls=%async_computation.2 | async-start | bytes 1572864 | tf_op jit(solution)/shard_map/all_to_all | solution.py:379
  17.8 3.0 %mix.2 = bf16[2,2,4,96,256]{4,3,2,1,0:T(8,128)(2,1)} custom-call(bf16[256,2048]{1,0:T(8,128)(2,1)} %key_ref.3, bf16[256,2048]{1,0:T(8,128)(2,1)} %value_ref.3, bf16[3,2,2048]{2,1,0:T(2,128)(2,1)} %copy-done.12, f32[3,3,2048]{2,1,0:T(4,128)} %refs_0_.7, f32[1024,256]{1,0:T(8,128)} %refs_0_.6), custom_call_target="tpu_custom_call" | custom-call | tf_op jit(solution)/shard_map/mix/pallas_call | solution.py:182
  20.8 15.7 %all-to-all-done.2.x_ref.f_ref = bf16[16,96,256]{2,1,0:T(8,128)(2,1)S(1)} async-done(((bf16[16,96,256]{2,1,0:T(8,128)(2,1)}), bf16[16,96,256]{2,1,0:T(8,128)(2,1)S(1)}, u32[]{:S(2)}, u32[]{:S(2)}) %all-to-all-start.2) | async-done | bytes 786464 | tf_op jit(solution)/shard_map/all_to_all | solution.py:379
  36.4 5.4 %all-to-all-start = ((bf16[16,96,256]{2,1,0:T(8,128)(2,1)}), bf16[16,96,256]{2,1,0:T(8,128)(2,1)}, u32[]{:S(2)}, u32[]{:S(2)}) async-start(bf16[16,96,256]{2,1,0:T(8,128)(2,1)} %bitcast.23), calls=%async_computation | async-start | bytes 1572864 | tf_op jit(solution)/shard_map/all_to_all | solution.py:379
  44.7 2.4 %collective-permute-start.7 = (bf16[256,512]{1,0:T(8,128)(2,1)}, bf16[256,512]{1,0:T(8,128)(2,1)}, u32[]{:S(2)}, u32[]{:S(2)}) collective-permute-start(bf16[256,512]{1,0:T(8,128)(2,1)} %get-tuple-element.14), channel_id=1, source_target_pairs={{16,0},{18,2},{20,4},{22,6},{24,8},{26,10},{28,12},{30,14},{0,16},... | collective-permute-start | bytes 786440 | tf_op jit(solution)/shard_map/ppermute | solution.py:330
  48.5 2.4 %collective-permute-start.15 = (bf16[256,1024]{1,0:T(8,128)(2,1)}, bf16[256,1024]{1,0:T(8,128)(2,1)}, u32[]{:S(2)}, u32[]{:S(2)}) collective-permute-start(bf16[256,1024]{1,0:T(8,128)(2,1)} %slice.33), channel_id=1, source_target_pairs={{16,0},{18,2},{20,4},{22,6},{24,8},{26,10},{28,12},{30,14},{0,16},... | collective-permute-start | bytes 1572872 | tf_op jit(solution)/shard_map/ppermute | solution.py:330
  51.8 19.9 %convolve.3 = bf16[16,64,256]{2,1,0:T(8,128)(2,1)} custom-call(bf16[16,96,256]{2,1,0:T(8,128)(2,1)} %copy-done.3, bf16[16,96,256]{2,1,0:T(8,128)(2,1)} %copy-done.3, f32[128,128]{1,0:T(8,128)} %broadcast_in_dim.8.gain_ref), custom_call_target="tpu_custom_call" | custom-call | tf_op jit(solution)/shard_map/convolve/pallas_call | solution.py:155
  71.7 16.9 %all-to-all-start.3 = ((bf16[8,2,64,256]{3,2,1,0:T(8,128)(2,1)}), bf16[8,2,64,256]{3,2,1,0:T(8,128)(2,1)}, u32[]{:S(2)}, u32[]{:S(2)}) async-start(bf16[8,2,64,256]{3,2,1,0:T(8,128)(2,1)} %bitcast.26), calls=%async_computation.3 | async-start | bytes 1048576 | tf_op jit(solution)/shard_map/all_to_all | solution.py:395
  93.8 8.9 %collective-permute-done.8 = bf16[256,512]{1,0:T(8,128)(2,1)S(1)} collective-permute-done((bf16[256,512]{1,0:T(8,128)(2,1)}, bf16[256,512]{1,0:T(8,128)(2,1)S(1)}, u32[]{:S(2)}, u32[]{:S(2)}) %collective-permute-start.8) | collective-permute-done | bytes 262176 | tf_op jit(solution)/shard_map/ppermute | solution.py:330
  104.9 19.9 %convolve.2 = bf16[16,64,256]{2,1,0:T(8,128)(2,1)} custom-call(bf16[16,96,256]{2,1,0:T(8,128)(2,1)} %all-to-all-done.x_ref.f_ref, bf16[16,96,256]{2,1,0:T(8,128)(2,1)} %all-to-all-done.x_ref.f_ref, f32[128,128]{1,0:T(8,128)} %broadcast_in_dim.8.gain_ref), custom_call_target="tpu_custom_call" | custom-call | tf_op jit(solution)/shard_map/convolve/pallas_call | solution.py:155
  124.8 4.3 %all-to-all-start.1 = ((bf16[8,2,64,256]{3,2,1,0:T(8,128)(2,1)}), bf16[8,2,64,256]{3,2,1,0:T(8,128)(2,1)}, u32[]{:S(2)}, u32[]{:S(2)}) async-start(bf16[8,2,64,256]{3,2,1,0:T(8,128)(2,1)} %bitcast.25), calls=%async_computation.1 | async-start | bytes 1048576 | tf_op jit(solution)/shard_map/all_to_all | solution.py:395
  133.5 3.1 %gate.3 = (bf16[2,256,256]{2,1,0:T(8,128)(2,1)}, bf16[2,256,256]{2,1,0:T(8,128)(2,1)}) custom-call(s32[5]{0:T(128)} %stack.64.spot_ref, f32[3,3,2048]{2,1,0:T(4,128)} %refs_0_.7, bf16[256,2048]{1,0:T(8,128)(2,1)} %refs_1_.3, bf16[2,2048]{1,0:T(2,128)(2,1)} %copy-done.13, bf16[8,2,64,256]{3,2,1,0:T(8,128)(2,1)} %all-to-all-done.3.refs_3_.refs_6_, ...), custom_call_target="tpu_custom_call" | custom-call | tf_op jit(solution)/shard_map/gate/pallas_call | solution.py:219
  136.6 6.4 %all-to-all-done.1.refs_3_.refs_6_ = bf16[8,2,64,256]{3,2,1,0:T(8,128)(2,1)} async-done(((bf16[8,2,64,256]{3,2,1,0:T(8,128)(2,1)}), bf16[8,2,64,256]{3,2,1,0:T(8,128)(2,1)}, u32[]{:S(2)}, u32[]{:S(2)}) %all-to-all-start.1) | async-done | bytes 524320 | tf_op jit(solution)/shard_map/all_to_all | solution.py:395
  143.0 3.1 %gate.2 = (bf16[2,256,256]{2,1,0:T(8,128)(2,1)}, bf16[2,256,256]{2,1,0:T(8,128)(2,1)}) custom-call(s32[5]{0:T(128)} %stack.64.spot_ref, f32[3,3,2048]{2,1,0:T(4,128)} %refs_0_.7, bf16[256,2048]{1,0:T(8,128)(2,1)} %refs_1_.3, bf16[2,2048]{1,0:T(2,128)(2,1)} %copy-done.13, bf16[8,2,64,256]{3,2,1,0:T(8,128)(2,1)} %all-to-all-done.1.refs_3_.refs_6_, ...), custom_call_target="tpu_custom_call" | custom-call | tf_op jit(solution)/shard_map/gate/pallas_call | solution.py:219
  150.2 5.6 %collective-permute-done.13.refs_3_ = bf16[2,256,256]{2,1,0:T(8,128)(2,1)} collective-permute-done((bf16[2,256,256]{2,1,0:T(8,128)(2,1)}, bf16[2,256,256]{2,1,0:T(8,128)(2,1)}, u32[]{:S(2)}, u32[]{:S(2)}) %collective-permute-start.13) | collective-permute-done | bytes 262176 | tf_op jit(solution)/shard_map/ppermute | solution.py:330
  155.7 4.7 %collective-permute-done.12.refs_2_ = bf16[2,256,256]{2,1,0:T(8,128)(2,1)} collective-permute-done((bf16[2,256,256]{2,1,0:T(8,128)(2,1)}, bf16[2,256,256]{2,1,0:T(8,128)(2,1)}, u32[]{:S(2)}, u32[]{:S(2)}) %collective-permute-start.12) | collective-permute-done | bytes 262176 | tf_op jit(solution)/shard_map/ppermute | solution.py:330
  160.4 5.3 %project.5 = bf16[256,1024]{1,0:T(8,128)(2,1)} custom-call(s32[8]{0:T(128)} %stack.60.spots, bf16[2,256,256]{2,1,0:T(8,128)(2,1)} %get-tuple-element.11.refs_0_, bf16[2,256,256]{2,1,0:T(8,128)(2,1)} %get-tuple-element.12.refs_1_, bf16[2,256,256]{2,1,0:T(8,128)(2,1)} %collective-permute-done.12.refs_2_, bf16[2,256,256]{2,1,0:T(8,128)(2,1)} %collective-permute-done.13.refs_3_, ...), custom_call_target="tpu_custom_call" | custom-call | tf_op jit(solution)/shard_map/project/pallas_call | solution.py:294
  169.5 5.4 %project.7 = bf16[256,1024]{1,0:T(8,128)(2,1)} custom-call(s32[8]{0:T(128)} %stack.60.spots, bf16[2,256,256]{2,1,0:T(8,128)(2,1)} %get-tuple-element.11.refs_0_, bf16[2,256,256]{2,1,0:T(8,128)(2,1)} %get-tuple-element.12.refs_1_, bf16[2,256,256]{2,1,0:T(8,128)(2,1)} %collective-permute-done.12.refs_2_, bf16[2,256,256]{2,1,0:T(8,128)(2,1)} %collective-permute-done.13.refs_3_, ...), custom_call_target="tpu_custom_call" | custom-call | tf_op jit(solution)/shard_map/project/pallas_call | solution.py:294
  174.9 1.9 %collective-permute-start.19 = (bf16[256,1024]{1,0:T(8,128)(2,1)}, bf16[256,1024]{1,0:T(8,128)(2,1)}, u32[]{:S(2)}, u32[]{:S(2)}) collective-permute-start(bf16[256,1024]{1,0:T(8,128)(2,1)} %project.7), channel_id=1, source_target_pairs={{8,0},{10,2},{12,4},{14,6},{0,8},{2,10},{4,12},{6,14},{24,16},{26,... | collective-permute-start | bytes 1572872 | tf_op jit(solution)/shard_map/ppermute | solution.py:330
  176.8 1.9 %collective-permute-done.2.refs_2_ = bf16[2,256,256]{2,1,0:T(8,128)(2,1)S(1)} collective-permute-done((bf16[2,256,256]{2,1,0:T(8,128)(2,1)S(1)}, bf16[2,256,256]{2,1,0:T(8,128)(2,1)S(1)}, u32[]{:S(2)}, u32[]{:S(2)}) %collective-permute-start.2) | collective-permute-done | bytes 262176 | tf_op jit(solution)/shard_map/ppermute | solution.py:330
  179.5 5.4 %project.4 = f32[256,1024]{1,0:T(8,128)} custom-call(s32[8]{0:T(128)} %stack.60.spots, bf16[2,256,256]{2,1,0:T(8,128)(2,1)} %get-tuple-element.9.refs_0_, bf16[2,256,256]{2,1,0:T(8,128)(2,1)} %get-tuple-element.10.refs_1_, bf16[2,256,256]{2,1,0:T(8,128)(2,1)} %copy-done.11, bf16[2,256,256]{2,1,0:T(8,128)(2,1)} %copy-done.10, bf16[256,2048]{1,0:T(8,128)(2,1)} %refs_4_.7, ...), custom_call_target="tpu_custom_call" | custom-call | tf_op jit(solution)/shard_map/project/pallas_call | solution.py:294
  184.9 5.6 %project.6 = f32[256,1024]{1,0:T(8,128)} custom-call(s32[8]{0:T(128)} %stack.60.spots, bf16[2,256,256]{2,1,0:T(8,128)(2,1)} %get-tuple-element.9.refs_0_, bf16[2,256,256]{2,1,0:T(8,128)(2,1)} %get-tuple-element.10.refs_1_, bf16[2,256,256]{2,1,0:T(8,128)(2,1)} %copy-done.11, bf16[2,256,256]{2,1,0:T(8,128)(2,1)} %copy-done.10, bf16[256,2048]{1,0:T(8,128)(2,1)} %refs_4_.7, ...), custom_call_target="tpu_custom_call" | custom-call | tf_op jit(solution)/shard_map/project/pallas_call | solution.py:294
  (83 shorter events, 31.9 us)
Async XLA Ops:
  1.6 3.2 %collective-permute-start = (bf16[3,2,2048]{2,1,0:T(2,128)(2,1)S(1)}, bf16[3,2,2048]{2,1,0:T(2,128)(2,1)S(1)}, u32[]{:S(2)}, u32[]{:S(2)}) collective-permute-start(bf16[3,2,2048]{2,1,0:T(2,128)(2,1)S(1)} %pad_maximum_fusion.1), channel_id=1, source_target_pairs={{0,2},{2,4},{4,6},{6,8},{8,10},{10,12},{12,14},{14,16},{16,18},{18... | collective-permute-start | bytes 73736 | tf_op jit(solution)/shard_map/ppermute | solution.py:21
  8.5 28.0 %all-to-all-start.2 = ((bf16[16,96,256]{2,1,0:T(8,128)(2,1)}), bf16[16,96,256]{2,1,0:T(8,128)(2,1)S(1)}, u32[]{:S(2)}, u32[]{:S(2)}) async-start(bf16[16,96,256]{2,1,0:T(8,128)(2,1)} %bitcast.24), calls=%async_computation.2 | async-start | bytes 1572864 | tf_op jit(solution)/shard_map/all_to_all | solution.py:379
  36.4 35.2 %all-to-all-start = ((bf16[16,96,256]{2,1,0:T(8,128)(2,1)}), bf16[16,96,256]{2,1,0:T(8,128)(2,1)}, u32[]{:S(2)}, u32[]{:S(2)}) async-start(bf16[16,96,256]{2,1,0:T(8,128)(2,1)} %bitcast.23), calls=%async_computation | async-start | bytes 1572864 | tf_op jit(solution)/shard_map/all_to_all | solution.py:379
  41.9 87.3 %collective-permute-start.5 = (bf16[256,2048]{1,0:T(8,128)(2,1)S(1)}, bf16[256,2048]{1,0:T(8,128)(2,1)S(1)}, u32[]{:S(2)}, u32[]{:S(2)}) collective-permute-start(bf16[256,2048]{1,0:T(8,128)(2,1)S(1)} %copy-done), channel_id=1, source_target_pairs={{4,0},{6,2},{0,4},{2,6},{12,8},{14,10},{8,12},{10,14},{20,16},{22,... | collective-permute-start | bytes 3145736 | tf_op jit(solution)/shard_map/ppermute | solution.py:330
  43.8 103.9 %collective-permute-start.4 = (bf16[256,2048]{1,0:T(8,128)(2,1)S(1)}, bf16[256,2048]{1,0:T(8,128)(2,1)S(1)}, u32[]{:S(2)}, u32[]{:S(2)}) collective-permute-start(bf16[256,2048]{1,0:T(8,128)(2,1)S(1)} %copy-done), channel_id=1, source_target_pairs={{2,0},{0,2},{6,4},{4,6},{10,8},{8,10},{14,12},{12,14},{18,16},{16,... | collective-permute-start | bytes 3145736 | tf_op jit(solution)/shard_map/ppermute | solution.py:330
  44.7 46.8 %collective-permute-start.7 = (bf16[256,512]{1,0:T(8,128)(2,1)}, bf16[256,512]{1,0:T(8,128)(2,1)}, u32[]{:S(2)}, u32[]{:S(2)}) collective-permute-start(bf16[256,512]{1,0:T(8,128)(2,1)} %get-tuple-element.14), channel_id=1, source_target_pairs={{16,0},{18,2},{20,4},{22,6},{24,8},{26,10},{28,12},{30,14},{0,16},... | collective-permute-start | bytes 786440 | tf_op jit(solution)/shard_map/ppermute | solution.py:330
  47.1 55.6 %collective-permute-start.8 = (bf16[256,512]{1,0:T(8,128)(2,1)}, bf16[256,512]{1,0:T(8,128)(2,1)S(1)}, u32[]{:S(2)}, u32[]{:S(2)}) collective-permute-start(bf16[256,512]{1,0:T(8,128)(2,1)} %get-tuple-element.13), channel_id=1, source_target_pairs={{16,0},{18,2},{20,4},{22,6},{24,8},{26,10},{28,12},{30,14},{0,16},... | collective-permute-start | bytes 786440 | tf_op jit(solution)/shard_map/ppermute | solution.py:330
  48.5 81.0 %collective-permute-start.15 = (bf16[256,1024]{1,0:T(8,128)(2,1)}, bf16[256,1024]{1,0:T(8,128)(2,1)}, u32[]{:S(2)}, u32[]{:S(2)}) collective-permute-start(bf16[256,1024]{1,0:T(8,128)(2,1)} %slice.33), channel_id=1, source_target_pairs={{16,0},{18,2},{20,4},{22,6},{24,8},{26,10},{28,12},{30,14},{0,16},... | collective-permute-start | bytes 1572872 | tf_op jit(solution)/shard_map/ppermute | solution.py:330
  71.7 53.2 %all-to-all-start.3 = ((bf16[8,2,64,256]{3,2,1,0:T(8,128)(2,1)}), bf16[8,2,64,256]{3,2,1,0:T(8,128)(2,1)}, u32[]{:S(2)}, u32[]{:S(2)}) async-start(bf16[8,2,64,256]{3,2,1,0:T(8,128)(2,1)} %bitcast.26), calls=%async_computation.3 | async-start | bytes 1048576 | tf_op jit(solution)/shard_map/all_to_all | solution.py:395
  91.5 38.3 %collective-permute-start.1 = (bf16[272,1024]{1,0:T(8,128)(2,1)}, bf16[272,1024]{1,0:T(8,128)(2,1)}, u32[]{:S(2)}, u32[]{:S(2)}) collective-permute-start(bf16[272,1024]{1,0:T(8,128)(2,1)} %fusion.1), channel_id=1, source_target_pairs={{8,0},{10,2},{12,4},{14,6},{0,8},{2,10},{4,12},{6,14},{24,16},{26,... | collective-permute-start | bytes 1671176 | tf_op jit(solution)/shard_map/ppermute | solution.py:330
  103.5 28.0 %collective-permute-start.10 = (bf16[256,1024]{1,0:T(8,128)(2,1)}, bf16[256,1024]{1,0:T(8,128)(2,1)}, u32[]{:S(2)}, u32[]{:S(2)}) collective-permute-start(bf16[256,1024]{1,0:T(8,128)(2,1)} %constant_dynamic-update-slice_fusion.refs_8_), channel_id=1, source_target_pairs={{4,0},{6,2},{0,4},{2,6},{12,8},{14,10},{8,12},{10,14},{20,16},{22,... | collective-permute-start | bytes 1572872 | tf_op jit(solution)/shard_map/ppermute | solution.py:330
  124.8 18.2 %all-to-all-start.1 = ((bf16[8,2,64,256]{3,2,1,0:T(8,128)(2,1)}), bf16[8,2,64,256]{3,2,1,0:T(8,128)(2,1)}, u32[]{:S(2)}, u32[]{:S(2)}) async-start(bf16[8,2,64,256]{3,2,1,0:T(8,128)(2,1)} %bitcast.25), calls=%async_computation.1 | async-start | bytes 1048576 | tf_op jit(solution)/shard_map/all_to_all | solution.py:395
  129.2 21.0 %collective-permute-start.6 = (bf16[256,2048]{1,0:T(8,128)(2,1)S(1)}, bf16[256,2048]{1,0:T(8,128)(2,1)}, u32[]{:S(2)}, u32[]{:S(2)}) collective-permute-start(bf16[256,2048]{1,0:T(8,128)(2,1)S(1)} %collective-permute-done.5.refs_6_), channel_id=1, source_target_pairs={{2,0},{0,2},{6,4},{4,6},{10,8},{8,10},{14,12},{12,14},{18,16},{16,... | collective-permute-start | bytes 3145736 | tf_op jit(solution)/shard_map/ppermute | solution.py:330
  129.4 16.7 %collective-permute-start.9 = (bf16[256,1024]{1,0:T(8,128)(2,1)}, bf16[256,1024]{1,0:T(8,128)(2,1)}, u32[]{:S(2)}, u32[]{:S(2)}) collective-permute-start(bf16[256,1024]{1,0:T(8,128)(2,1)} %constant_dynamic-update-slice_fusion.refs_8_), channel_id=1, source_target_pairs={{2,0},{0,2},{6,4},{4,6},{10,8},{8,10},{14,12},{12,14},{18,16},{16,... | collective-permute-start | bytes 1572872 | tf_op jit(solution)/shard_map/ppermute | solution.py:330
  129.8 19.3 %collective-permute-start.17 = (bf16[256,1024]{1,0:T(8,128)(2,1)}, bf16[256,1024]{1,0:T(8,128)(2,1)}, u32[]{:S(2)}, u32[]{:S(2)}) collective-permute-start(bf16[256,1024]{1,0:T(8,128)(2,1)} %collective-permute-done.15.refs_8_), channel_id=1, source_target_pairs={{4,0},{6,2},{0,4},{2,6},{12,8},{14,10},{8,12},{10,14},{20,16},{22,... | collective-permute-start | bytes 1572872 | tf_op jit(solution)/shard_map/ppermute | solution.py:330
  131.5 17.5 %collective-permute-start.11 = (bf16[256,1024]{1,0:T(8,128)(2,1)}, bf16[256,1024]{1,0:T(8,128)(2,1)}, u32[]{:S(2)}, u32[]{:S(2)}) collective-permute-start(bf16[256,1024]{1,0:T(8,128)(2,1)} %collective-permute-done.10.refs_10_), channel_id=1, source_target_pairs={{2,0},{0,2},{6,4},{4,6},{10,8},{8,10},{14,12},{12,14},{18,16},{16,... | collective-permute-start | bytes 1572872 | tf_op jit(solution)/shard_map/ppermute | solution.py:330
  146.2 9.6 %collective-permute-start.13 = (bf16[2,256,256]{2,1,0:T(8,128)(2,1)}, bf16[2,256,256]{2,1,0:T(8,128)(2,1)}, u32[]{:S(2)}, u32[]{:S(2)}) collective-permute-start(bf16[2,256,256]{2,1,0:T(8,128)(2,1)} %get-tuple-element.12.refs_1_), channel_id=1, source_target_pairs={{1,0},{0,1},{3,2},{2,3},{5,4},{4,5},{7,6},{6,7},{9,8},{8,9},{11,10... | collective-permute-start | bytes 786440 | tf_op jit(solution)/shard_map/ppermute | solution.py:330
  147.8 12.6 %collective-permute-start.12 = (bf16[2,256,256]{2,1,0:T(8,128)(2,1)}, bf16[2,256,256]{2,1,0:T(8,128)(2,1)}, u32[]{:S(2)}, u32[]{:S(2)}) collective-permute-start(bf16[2,256,256]{2,1,0:T(8,128)(2,1)} %get-tuple-element.11.refs_0_), channel_id=1, source_target_pairs={{1,0},{0,1},{3,2},{2,3},{5,4},{4,5},{7,6},{6,7},{9,8},{8,9},{11,10... | collective-permute-start | bytes 786440 | tf_op jit(solution)/shard_map/ppermute | solution.py:330
  149.0 18.8 %collective-permute-start.16 = (bf16[256,1024]{1,0:T(8,128)(2,1)}, bf16[256,1024]{1,0:T(8,128)(2,1)S(1)}, u32[]{:S(2)}, u32[]{:S(2)}) collective-permute-start(bf16[256,1024]{1,0:T(8,128)(2,1)} %collective-permute-done.15.refs_8_), channel_id=1, source_target_pairs={{2,0},{0,2},{6,4},{4,6},{10,8},{8,10},{14,12},{12,14},{18,16},{16,... | collective-permute-start | bytes 1572872 | tf_op jit(solution)/shard_map/ppermute | solution.py:330
  149.0 18.8 %collective-permute-start.18 = (bf16[256,1024]{1,0:T(8,128)(2,1)}, bf16[256,1024]{1,0:T(8,128)(2,1)S(1)}, u32[]{:S(2)}, u32[]{:S(2)}) collective-permute-start(bf16[256,1024]{1,0:T(8,128)(2,1)} %collective-permute-done.17.refs_10_), channel_id=1, source_target_pairs={{2,0},{0,2},{6,4},{4,6},{10,8},{8,10},{14,12},{12,14},{18,16},{16,... | collective-permute-start | bytes 1572872 | tf_op jit(solution)/shard_map/ppermute | solution.py:330
  165.7 24.8 %collective-permute-start.14 = (bf16[256,1024]{1,0:T(8,128)(2,1)}, bf16[256,1024]{1,0:T(8,128)(2,1)}, u32[]{:S(2)}, u32[]{:S(2)}) collective-permute-start(bf16[256,1024]{1,0:T(8,128)(2,1)} %project.5), channel_id=1, source_target_pairs={{8,0},{10,2},{12,4},{14,6},{0,8},{2,10},{4,12},{6,14},{24,16},{26,... | collective-permute-start | bytes 1572872 | tf_op jit(solution)/shard_map/ppermute | solution.py:330
  165.7 11.1 %collective-permute-start.3 = (bf16[2,256,256]{2,1,0:T(8,128)(2,1)S(1)}, bf16[2,256,256]{2,1,0:T(8,128)(2,1)S(1)}, u32[]{:S(2)}, u32[]{:S(2)}) collective-permute-start(bf16[2,256,256]{2,1,0:T(8,128)(2,1)S(1)} %copy-done.8), channel_id=1, source_target_pairs={{1,0},{0,1},{3,2},{2,3},{5,4},{4,5},{7,6},{6,7},{9,8},{8,9},{11,10... | collective-permute-start | bytes 786440 | tf_op jit(solution)/shard_map/ppermute | solution.py:330
  167.3 11.5 %collective-permute-start.2 = (bf16[2,256,256]{2,1,0:T(8,128)(2,1)S(1)}, bf16[2,256,256]{2,1,0:T(8,128)(2,1)S(1)}, u32[]{:S(2)}, u32[]{:S(2)}) collective-permute-start(bf16[2,256,256]{2,1,0:T(8,128)(2,1)S(1)} %copy-done.9), channel_id=1, source_target_pairs={{1,0},{0,1},{3,2},{2,3},{5,4},{4,5},{7,6},{6,7},{9,8},{8,9},{11,10... | collective-permute-start | bytes 786440 | tf_op jit(solution)/shard_map/ppermute | solution.py:330
  174.9 17.0 %collective-permute-start.19 = (bf16[256,1024]{1,0:T(8,128)(2,1)}, bf16[256,1024]{1,0:T(8,128)(2,1)}, u32[]{:S(2)}, u32[]{:S(2)}) collective-permute-start(bf16[256,1024]{1,0:T(8,128)(2,1)} %project.7), channel_id=1, source_target_pairs={{8,0},{10,2},{12,4},{14,6},{0,8},{2,10},{4,12},{6,14},{24,16},{26,... | collective-permute-start | bytes 1572872 | tf_op jit(solution)/shard_map/ppermute | solution.py:330
  (15 other events, 104.7 us)

commit v7 on v6

--- a/solution.py
+++ b/solution.py
@@ -410,8 +410,11 @@
         taken.append(swap(passed, "seq", inner))
     for cut in range(CUTS):
         sums.append(project(spots, kept + kept_far, pieces[cut], span, cut * span, jnp.float32))
-    outs = [(a + b.astype(jnp.float32)).astype(jnp.bfloat16) for a, b in zip(sums, taken)]
-    return jnp.concatenate(outs, axis=1)
+    result = jnp.zeros((tokens, columns), jnp.bfloat16)
+    for cut, (ours, theirs) in enumerate(zip(sums, taken)):
+        block = (ours + theirs.astype(jnp.float32)).astype(jnp.bfloat16)
+        result = lax.dynamic_update_slice(result, block, (0, cut * span))
+    return result
 
 
 def solution(mesh):

time: 195 us -> 195 us (level)
  no operation moved by 1% of the time
where the time goes in v7:
time: 195 us; the launch traced here: 194 us
  Pallas kernels  73.8 us (38%)
  starting transfers between devices  56.6 us (29%)
  waiting for transfers between devices  45.1 us (23%)
  local copies, waits for them, and re-layouts  13 us (7%)
  other arithmetic  5.44 us (3%)
    pallas_call x2, Pallas kernels, convolve(): pl.pallas_call(functools.partial(conv_kernel, n, tok, width, place), grid...  39.8 us
    ppermute x19, waiting for transfers between devices, swap(): lax.ppermute(block, axis, [(i ^ mask, i) for i in range(lax.axis_size(axi...  22.2 us
    pallas_call x4, Pallas kernels, project(): pl.pallas_call(functools.partial(project_kernel, count, len(gated)), grid...  21.7 us
    all_to_all x2, starting transfers between devices, layer(): lax.all_to_all(conv, 'seq', split_axis=0, concat_axis=0, tiled=True, axis...  21.3 us
    ppermute x19, starting transfers between devices, swap(): lax.ppermute(block, axis, [(i ^ mask, i) for i in range(lax.axis_size(axi...  18.2 us
    all_to_all x2, waiting for transfers between devices, layer(): lax.all_to_all(turned, 'seq', split_axis=0, concat_axis=0, tiled=True)  15.7 us
    all_to_all x2, starting transfers between devices, layer(): lax.all_to_all(turned, 'seq', split_axis=0, concat_axis=0, tiled=True)  14.7 us
    all_to_all x2, waiting for transfers between devices, layer(): lax.all_to_all(conv, 'seq', split_axis=0, concat_axis=0, tiled=True, axis...  6.44 us
  transfers between devices with their start and end apart: 24, of which 9 were waited for; matrix products, arithmetic and copies ran while one was open for 6% of the time, Pallas kernels for 36%

profile of v7, /device:TPU:0, one launch (start us, length us, event | category | flops | bytes accessed | tf_op | source)
XLA Modules:
  0.0 194.2 jit_solution(14827208840432434095)
XLA Ops:
  1.6 2.4 %collective-permute-start = (bf16[3,2,2048]{2,1,0:T(2,128)(2,1)S(1)}, bf16[3,2,2048]{2,1,0:T(2,128)(2,1)S(1)}, u32[]{:S(2)}, u32[]{:S(2)}) collective-permute-start(bf16[3,2,2048]{2,1,0:T(2,128)(2,1)S(1)} %pad_maximum_fusion.1), channel_id=1, source_target_pairs={{0,2},{2,4},{4,6},{6,8},{8,10},{10,12},{12,14},{14,16},{16,18},{18... | collective-permute-start | bytes 73736 | tf_op jit(solution)/shard_map/ppermute | solution.py:21
  5.5 3.0 %mix.3 = bf16[2,2,4,96,256]{4,3,2,1,0:T(8,128)(2,1)} custom-call(bf16[256,2048]{1,0:T(8,128)(2,1)} %key_ref.3, bf16[256,2048]{1,0:T(8,128)(2,1)} %value_ref.3, bf16[3,2,2048]{2,1,0:T(2,128)(2,1)} %copy-done.12, f32[3,3,2048]{2,1,0:T(4,128)} %refs_0_.7, f32[1024,256]{1,0:T(8,128)} %refs_0_.6), custom_call_target="tpu_custom_call" | custom-call | tf_op jit(solution)/shard_map/mix/pallas_call | solution.py:182
  8.5 9.3 %all-to-all-start.2 = ((bf16[16,96,256]{2,1,0:T(8,128)(2,1)}), bf16[16,96,256]{2,1,0:T(8,128)(2,1)S(1)}, u32[]{:S(2)}, u32[]{:S(2)}) async-start(bf16[16,96,256]{2,1,0:T(8,128)(2,1)} %bitcast.24), calls=%async_computation.2 | async-start | bytes 1572864 | tf_op jit(solution)/shard_map/all_to_all | solution.py:379
  17.8 3.0 %mix.2 = bf16[2,2,4,96,256]{4,3,2,1,0:T(8,128)(2,1)} custom-call(bf16[256,2048]{1,0:T(8,128)(2,1)} %key_ref.3, bf16[256,2048]{1,0:T(8,128)(2,1)} %value_ref.3, bf16[3,2,2048]{2,1,0:T(2,128)(2,1)} %copy-done.12, f32[3,3,2048]{2,1,0:T(4,128)} %refs_0_.7, f32[1024,256]{1,0:T(8,128)} %refs_0_.6), custom_call_target="tpu_custom_call" | custom-call | tf_op jit(solution)/shard_map/mix/pallas_call | solution.py:182
  20.8 15.7 %all-to-all-done.2.x_ref.f_ref = bf16[16,96,256]{2,1,0:T(8,128)(2,1)S(1)} async-done(((bf16[16,96,256]{2,1,0:T(8,128)(2,1)}), bf16[16,96,256]{2,1,0:T(8,128)(2,1)S(1)}, u32[]{:S(2)}, u32[]{:S(2)}) %all-to-all-start.2) | async-done | bytes 786464 | tf_op jit(solution)/shard_map/all_to_all | solution.py:379
  36.4 5.4 %all-to-all-start = ((bf16[16,96,256]{2,1,0:T(8,128)(2,1)}), bf16[16,96,256]{2,1,0:T(8,128)(2,1)}, u32[]{:S(2)}, u32[]{:S(2)}) async-start(bf16[16,96,256]{2,1,0:T(8,128)(2,1)} %bitcast.23), calls=%async_computation | async-start | bytes 1572864 | tf_op jit(solution)/shard_map/all_to_all | solution.py:379
  44.7 2.4 %collective-permute-start.7 = (bf16[256,512]{1,0:T(8,128)(2,1)}, bf16[256,512]{1,0:T(8,128)(2,1)}, u32[]{:S(2)}, u32[]{:S(2)}) collective-permute-start(bf16[256,512]{1,0:T(8,128)(2,1)} %get-tuple-element.14), channel_id=1, source_target_pairs={{16,0},{18,2},{20,4},{22,6},{24,8},{26,10},{28,12},{30,14},{0,16},... | collective-permute-start | bytes 786440 | tf_op jit(solution)/shard_map/ppermute | solution.py:330
  48.5 2.4 %collective-permute-start.15 = (bf16[256,1024]{1,0:T(8,128)(2,1)}, bf16[256,1024]{1,0:T(8,128)(2,1)}, u32[]{:S(2)}, u32[]{:S(2)}) collective-permute-start(bf16[256,1024]{1,0:T(8,128)(2,1)} %slice.33), channel_id=1, source_target_pairs={{16,0},{18,2},{20,4},{22,6},{24,8},{26,10},{28,12},{30,14},{0,16},... | collective-permute-start | bytes 1572872 | tf_op jit(solution)/shard_map/ppermute | solution.py:330
  51.8 19.9 %convolve.3 = bf16[16,64,256]{2,1,0:T(8,128)(2,1)} custom-call(bf16[16,96,256]{2,1,0:T(8,128)(2,1)} %copy-done.3, bf16[16,96,256]{2,1,0:T(8,128)(2,1)} %copy-done.3, f32[128,128]{1,0:T(8,128)} %broadcast_in_dim.9.gain_ref), custom_call_target="tpu_custom_call" | custom-call | tf_op jit(solution)/shard_map/convolve/pallas_call | solution.py:155
  71.7 16.9 %all-to-all-start.3 = ((bf16[8,2,64,256]{3,2,1,0:T(8,128)(2,1)}), bf16[8,2,64,256]{3,2,1,0:T(8,128)(2,1)}, u32[]{:S(2)}, u32[]{:S(2)}) async-start(bf16[8,2,64,256]{3,2,1,0:T(8,128)(2,1)} %bitcast.26), calls=%async_computation.3 | async-start | bytes 1048576 | tf_op jit(solution)/shard_map/all_to_all | solution.py:395
  93.8 8.9 %collective-permute-done.8 = bf16[256,512]{1,0:T(8,128)(2,1)S(1)} collective-permute-done((bf16[256,512]{1,0:T(8,128)(2,1)}, bf16[256,512]{1,0:T(8,128)(2,1)S(1)}, u32[]{:S(2)}, u32[]{:S(2)}) %collective-permute-start.8) | collective-permute-done | bytes 262176 | tf_op jit(solution)/shard_map/ppermute | solution.py:330
  104.9 19.9 %convolve.2 = bf16[16,64,256]{2,1,0:T(8,128)(2,1)} custom-call(bf16[16,96,256]{2,1,0:T(8,128)(2,1)} %all-to-all-done.x_ref.f_ref, bf16[16,96,256]{2,1,0:T(8,128)(2,1)} %all-to-all-done.x_ref.f_ref, f32[128,128]{1,0:T(8,128)} %broadcast_in_dim.9.gain_ref), custom_call_target="tpu_custom_call" | custom-call | tf_op jit(solution)/shard_map/convolve/pallas_call | solution.py:155
  124.8 4.3 %all-to-all-start.1 = ((bf16[8,2,64,256]{3,2,1,0:T(8,128)(2,1)}), bf16[8,2,64,256]{3,2,1,0:T(8,128)(2,1)}, u32[]{:S(2)}, u32[]{:S(2)}) async-start(bf16[8,2,64,256]{3,2,1,0:T(8,128)(2,1)} %bitcast.25), calls=%async_computation.1 | async-start | bytes 1048576 | tf_op jit(solution)/shard_map/all_to_all | solution.py:395
  133.5 3.1 %gate.3 = (bf16[2,256,256]{2,1,0:T(8,128)(2,1)}, bf16[2,256,256]{2,1,0:T(8,128)(2,1)}) custom-call(s32[5]{0:T(128)} %stack.64.spot_ref, f32[3,3,2048]{2,1,0:T(4,128)} %refs_0_.7, bf16[256,2048]{1,0:T(8,128)(2,1)} %refs_1_.3, bf16[2,2048]{1,0:T(2,128)(2,1)} %copy-done.13, bf16[8,2,64,256]{3,2,1,0:T(8,128)(2,1)} %all-to-all-done.3.refs_3_.refs_6_, ...), custom_call_target="tpu_custom_call" | custom-call | tf_op jit(solution)/shard_map/gate/pallas_call | solution.py:219
  136.6 6.4 %all-to-all-done.1.refs_3_.refs_6_ = bf16[8,2,64,256]{3,2,1,0:T(8,128)(2,1)} async-done(((bf16[8,2,64,256]{3,2,1,0:T(8,128)(2,1)}), bf16[8,2,64,256]{3,2,1,0:T(8,128)(2,1)}, u32[]{:S(2)}, u32[]{:S(2)}) %all-to-all-start.1) | async-done | bytes 524320 | tf_op jit(solution)/shard_map/all_to_all | solution.py:395
  143.0 3.1 %gate.2 = (bf16[2,256,256]{2,1,0:T(8,128)(2,1)}, bf16[2,256,256]{2,1,0:T(8,128)(2,1)}) custom-call(s32[5]{0:T(128)} %stack.64.spot_ref, f32[3,3,2048]{2,1,0:T(4,128)} %refs_0_.7, bf16[256,2048]{1,0:T(8,128)(2,1)} %refs_1_.3, bf16[2,2048]{1,0:T(2,128)(2,1)} %copy-done.13, bf16[8,2,64,256]{3,2,1,0:T(8,128)(2,1)} %all-to-all-done.1.refs_3_.refs_6_, ...), custom_call_target="tpu_custom_call" | custom-call | tf_op jit(solution)/shard_map/gate/pallas_call | solution.py:219
  150.2 5.6 %collective-permute-done.13.refs_3_ = bf16[2,256,256]{2,1,0:T(8,128)(2,1)} collective-permute-done((bf16[2,256,256]{2,1,0:T(8,128)(2,1)}, bf16[2,256,256]{2,1,0:T(8,128)(2,1)}, u32[]{:S(2)}, u32[]{:S(2)}) %collective-permute-start.13) | collective-permute-done | bytes 262176 | tf_op jit(solution)/shard_map/ppermute | solution.py:330
  155.7 4.7 %collective-permute-done.12.refs_2_ = bf16[2,256,256]{2,1,0:T(8,128)(2,1)} collective-permute-done((bf16[2,256,256]{2,1,0:T(8,128)(2,1)}, bf16[2,256,256]{2,1,0:T(8,128)(2,1)}, u32[]{:S(2)}, u32[]{:S(2)}) %collective-permute-start.12) | collective-permute-done | bytes 262176 | tf_op jit(solution)/shard_map/ppermute | solution.py:330
  160.4 5.3 %project.5 = bf16[256,1024]{1,0:T(8,128)(2,1)} custom-call(s32[8]{0:T(128)} %stack.60.spots, bf16[2,256,256]{2,1,0:T(8,128)(2,1)} %get-tuple-element.11.refs_0_, bf16[2,256,256]{2,1,0:T(8,128)(2,1)} %get-tuple-element.12.refs_1_, bf16[2,256,256]{2,1,0:T(8,128)(2,1)} %collective-permute-done.12.refs_2_, bf16[2,256,256]{2,1,0:T(8,128)(2,1)} %collective-permute-done.13.refs_3_, ...), custom_call_target="tpu_custom_call" | custom-call | tf_op jit(solution)/shard_map/project/pallas_call | solution.py:294
  169.5 5.4 %project.7 = bf16[256,1024]{1,0:T(8,128)(2,1)} custom-call(s32[8]{0:T(128)} %stack.60.spots, bf16[2,256,256]{2,1,0:T(8,128)(2,1)} %get-tuple-element.11.refs_0_, bf16[2,256,256]{2,1,0:T(8,128)(2,1)} %get-tuple-element.12.refs_1_, bf16[2,256,256]{2,1,0:T(8,128)(2,1)} %collective-permute-done.12.refs_2_, bf16[2,256,256]{2,1,0:T(8,128)(2,1)} %collective-permute-done.13.refs_3_, ...), custom_call_target="tpu_custom_call" | custom-call | tf_op jit(solution)/shard_map/project/pallas_call | solution.py:294
  174.9 1.9 %collective-permute-start.19 = (bf16[256,1024]{1,0:T(8,128)(2,1)}, bf16[256,1024]{1,0:T(8,128)(2,1)}, u32[]{:S(2)}, u32[]{:S(2)}) collective-permute-start(bf16[256,1024]{1,0:T(8,128)(2,1)} %project.7), channel_id=1, source_target_pairs={{8,0},{10,2},{12,4},{14,6},{0,8},{2,10},{4,12},{6,14},{24,16},{26,... | collective-permute-start | bytes 1572872 | tf_op jit(solution)/shard_map/ppermute | solution.py:330
  176.8 1.9 %collective-permute-done.2.refs_2_ = bf16[2,256,256]{2,1,0:T(8,128)(2,1)S(1)} collective-permute-done((bf16[2,256,256]{2,1,0:T(8,128)(2,1)S(1)}, bf16[2,256,256]{2,1,0:T(8,128)(2,1)S(1)}, u32[]{:S(2)}, u32[]{:S(2)}) %collective-permute-start.2) | collective-permute-done | bytes 262176 | tf_op jit(solution)/shard_map/ppermute | solution.py:330
  179.5 5.4 %project.4 = f32[256,1024]{1,0:T(8,128)} custom-call(s32[8]{0:T(128)} %stack.60.spots, bf16[2,256,256]{2,1,0:T(8,128)(2,1)} %get-tuple-element.9.refs_0_, bf16[2,256,256]{2,1,0:T(8,128)(2,1)} %get-tuple-element.10.refs_1_, bf16[2,256,256]{2,1,0:T(8,128)(2,1)} %copy-done.11, bf16[2,256,256]{2,1,0:T(8,128)(2,1)} %copy-done.10, bf16[256,2048]{1,0:T(8,128)(2,1)} %refs_4_.7, ...), custom_call_target="tpu_custom_call" | custom-call | tf_op jit(solution)/shard_map/project/pallas_call | solution.py:294
  184.9 5.6 %project.6 = f32[256,1024]{1,0:T(8,128)} custom-call(s32[8]{0:T(128)} %stack.60.spots, bf16[2,256,256]{2,1,0:T(8,128)(2,1)} %get-tuple-element.9.refs_0_, bf16[2,256,256]{2,1,0:T(8,128)(2,1)} %get-tuple-element.10.refs_1_, bf16[2,256,256]{2,1,0:T(8,128)(2,1)} %copy-done.11, bf16[2,256,256]{2,1,0:T(8,128)(2,1)} %copy-done.10, bf16[256,2048]{1,0:T(8,128)(2,1)} %refs_4_.7, ...), custom_call_target="tpu_custom_call" | custom-call | tf_op jit(solution)/shard_map/project/pallas_call | solution.py:294
  (83 shorter events, 31.9 us)
Async XLA Ops:
  1.6 3.2 %collective-permute-start = (bf16[3,2,2048]{2,1,0:T(2,128)(2,1)S(1)}, bf16[3,2,2048]{2,1,0:T(2,128)(2,1)S(1)}, u32[]{:S(2)}, u32[]{:S(2)}) collective-permute-start(bf16[3,2,2048]{2,1,0:T(2,128)(2,1)S(1)} %pad_maximum_fusion.1), channel_id=1, source_target_pairs={{0,2},{2,4},{4,6},{6,8},{8,10},{10,12},{12,14},{14,16},{16,18},{18... | collective-permute-start | bytes 73736 | tf_op jit(solution)/shard_map/ppermute | solution.py:21
  8.5 28.0 %all-to-all-start.2 = ((bf16[16,96,256]{2,1,0:T(8,128)(2,1)}), bf16[16,96,256]{2,1,0:T(8,128)(2,1)S(1)}, u32[]{:S(2)}, u32[]{:S(2)}) async-start(bf16[16,96,256]{2,1,0:T(8,128)(2,1)} %bitcast.24), calls=%async_computation.2 | async-start | bytes 1572864 | tf_op jit(solution)/shard_map/all_to_all | solution.py:379
  36.4 35.2 %all-to-all-start = ((bf16[16,96,256]{2,1,0:T(8,128)(2,1)}), bf16[16,96,256]{2,1,0:T(8,128)(2,1)}, u32[]{:S(2)}, u32[]{:S(2)}) async-start(bf16[16,96,256]{2,1,0:T(8,128)(2,1)} %bitcast.23), calls=%async_computation | async-start | bytes 1572864 | tf_op jit(solution)/shard_map/all_to_all | solution.py:379
  41.9 87.3 %collective-permute-start.5 = (bf16[256,2048]{1,0:T(8,128)(2,1)S(1)}, bf16[256,2048]{1,0:T(8,128)(2,1)S(1)}, u32[]{:S(2)}, u32[]{:S(2)}) collective-permute-start(bf16[256,2048]{1,0:T(8,128)(2,1)S(1)} %copy-done), channel_id=1, source_target_pairs={{4,0},{6,2},{0,4},{2,6},{12,8},{14,10},{8,12},{10,14},{20,16},{22,... | collective-permute-start | bytes 3145736 | tf_op jit(solution)/shard_map/ppermute | solution.py:330
  43.8 103.9 %collective-permute-start.4 = (bf16[256,2048]{1,0:T(8,128)(2,1)S(1)}, bf16[256,2048]{1,0:T(8,128)(2,1)S(1)}, u32[]{:S(2)}, u32[]{:S(2)}) collective-permute-start(bf16[256,2048]{1,0:T(8,128)(2,1)S(1)} %copy-done), channel_id=1, source_target_pairs={{2,0},{0,2},{6,4},{4,6},{10,8},{8,10},{14,12},{12,14},{18,16},{16,... | collective-permute-start | bytes 3145736 | tf_op jit(solution)/shard_map/ppermute | solution.py:330
  44.7 46.8 %collective-permute-start.7 = (bf16[256,512]{1,0:T(8,128)(2,1)}, bf16[256,512]{1,0:T(8,128)(2,1)}, u32[]{:S(2)}, u32[]{:S(2)}) collective-permute-start(bf16[256,512]{1,0:T(8,128)(2,1)} %get-tuple-element.14), channel_id=1, source_target_pairs={{16,0},{18,2},{20,4},{22,6},{24,8},{26,10},{28,12},{30,14},{0,16},... | collective-permute-start | bytes 786440 | tf_op jit(solution)/shard_map/ppermute | solution.py:330
  47.1 55.6 %collective-permute-start.8 = (bf16[256,512]{1,0:T(8,128)(2,1)}, bf16[256,512]{1,0:T(8,128)(2,1)S(1)}, u32[]{:S(2)}, u32[]{:S(2)}) collective-permute-start(bf16[256,512]{1,0:T(8,128)(2,1)} %get-tuple-element.13), channel_id=1, source_target_pairs={{16,0},{18,2},{20,4},{22,6},{24,8},{26,10},{28,12},{30,14},{0,16},... | collective-permute-start | bytes 786440 | tf_op jit(solution)/shard_map/ppermute | solution.py:330
  48.5 81.0 %collective-permute-start.15 = (bf16[256,1024]{1,0:T(8,128)(2,1)}, bf16[256,1024]{1,0:T(8,128)(2,1)}, u32[]{:S(2)}, u32[]{:S(2)}) collective-permute-start(bf16[256,1024]{1,0:T(8,128)(2,1)} %slice.33), channel_id=1, source_target_pairs={{16,0},{18,2},{20,4},{22,6},{24,8},{26,10},{28,12},{30,14},{0,16},... | collective-permute-start | bytes 1572872 | tf_op jit(solution)/shard_map/ppermute | solution.py:330
  71.7 53.2 %all-to-all-start.3 = ((bf16[8,2,64,256]{3,2,1,0:T(8,128)(2,1)}), bf16[8,2,64,256]{3,2,1,0:T(8,128)(2,1)}, u32[]{:S(2)}, u32[]{:S(2)}) async-start(bf16[8,2,64,256]{3,2,1,0:T(8,128)(2,1)} %bitcast.26), calls=%async_computation.3 | async-start | bytes 1048576 | tf_op jit(solution)/shard_map/all_to_all | solution.py:395
  91.5 38.3 %collective-permute-start.1 = (bf16[272,1024]{1,0:T(8,128)(2,1)}, bf16[272,1024]{1,0:T(8,128)(2,1)}, u32[]{:S(2)}, u32[]{:S(2)}) collective-permute-start(bf16[272,1024]{1,0:T(8,128)(2,1)} %fusion.1), channel_id=1, source_target_pairs={{8,0},{10,2},{12,4},{14,6},{0,8},{2,10},{4,12},{6,14},{24,16},{26,... | collective-permute-start | bytes 1671176 | tf_op jit(solution)/shard_map/ppermute | solution.py:330
  103.5 28.0 %collective-permute-start.10 = (bf16[256,1024]{1,0:T(8,128)(2,1)}, bf16[256,1024]{1,0:T(8,128)(2,1)}, u32[]{:S(2)}, u32[]{:S(2)}) collective-permute-start(bf16[256,1024]{1,0:T(8,128)(2,1)} %constant_dynamic-update-slice_fusion.refs_8_), channel_id=1, source_target_pairs={{4,0},{6,2},{0,4},{2,6},{12,8},{14,10},{8,12},{10,14},{20,16},{22,... | collective-permute-start | bytes 1572872 | tf_op jit(solution)/shard_map/ppermute | solution.py:330
  124.8 18.2 %all-to-all-start.1 = ((bf16[8,2,64,256]{3,2,1,0:T(8,128)(2,1)}), bf16[8,2,64,256]{3,2,1,0:T(8,128)(2,1)}, u32[]{:S(2)}, u32[]{:S(2)}) async-start(bf16[8,2,64,256]{3,2,1,0:T(8,128)(2,1)} %bitcast.25), calls=%async_computation.1 | async-start | bytes 1048576 | tf_op jit(solution)/shard_map/all_to_all | solution.py:395
  129.2 21.0 %collective-permute-start.6 = (bf16[256,2048]{1,0:T(8,128)(2,1)S(1)}, bf16[256,2048]{1,0:T(8,128)(2,1)}, u32[]{:S(2)}, u32[]{:S(2)}) collective-permute-start(bf16[256,2048]{1,0:T(8,128)(2,1)S(1)} %collective-permute-done.5.refs_6_), channel_id=1, source_target_pairs={{2,0},{0,2},{6,4},{4,6},{10,8},{8,10},{14,12},{12,14},{18,16},{16,... | collective-permute-start | bytes 3145736 | tf_op jit(solution)/shard_map/ppermute | solution.py:330
  129.4 16.7 %collective-permute-start.9 = (bf16[256,1024]{1,0:T(8,128)(2,1)}, bf16[256,1024]{1,0:T(8,128)(2,1)}, u32[]{:S(2)}, u32[]{:S(2)}) collective-permute-start(bf16[256,1024]{1,0:T(8,128)(2,1)} %constant_dynamic-update-slice_fusion.refs_8_), channel_id=1, source_target_pairs={{2,0},{0,2},{6,4},{4,6},{10,8},{8,10},{14,12},{12,14},{18,16},{16,... | collective-permute-start | bytes 1572872 | tf_op jit(solution)/shard_map/ppermute | solution.py:330
  129.8 19.3 %collective-permute-start.17 = (bf16[256,1024]{1,0:T(8,128)(2,1)}, bf16[256,1024]{1,0:T(8,128)(2,1)}, u32[]{:S(2)}, u32[]{:S(2)}) collective-permute-start(bf16[256,1024]{1,0:T(8,128)(2,1)} %collective-permute-done.15.refs_8_), channel_id=1, source_target_pairs={{4,0},{6,2},{0,4},{2,6},{12,8},{14,10},{8,12},{10,14},{20,16},{22,... | collective-permute-start | bytes 1572872 | tf_op jit(solution)/shard_map/ppermute | solution.py:330
  131.5 17.5 %collective-permute-start.11 = (bf16[256,1024]{1,0:T(8,128)(2,1)}, bf16[256,1024]{1,0:T(8,128)(2,1)}, u32[]{:S(2)}, u32[]{:S(2)}) collective-permute-start(bf16[256,1024]{1,0:T(8,128)(2,1)} %collective-permute-done.10.refs_10_), channel_id=1, source_target_pairs={{2,0},{0,2},{6,4},{4,6},{10,8},{8,10},{14,12},{12,14},{18,16},{16,... | collective-permute-start | bytes 1572872 | tf_op jit(solution)/shard_map/ppermute | solution.py:330
  146.2 9.6 %collective-permute-start.13 = (bf16[2,256,256]{2,1,0:T(8,128)(2,1)}, bf16[2,256,256]{2,1,0:T(8,128)(2,1)}, u32[]{:S(2)}, u32[]{:S(2)}) collective-permute-start(bf16[2,256,256]{2,1,0:T(8,128)(2,1)} %get-tuple-element.12.refs_1_), channel_id=1, source_target_pairs={{1,0},{0,1},{3,2},{2,3},{5,4},{4,5},{7,6},{6,7},{9,8},{8,9},{11,10... | collective-permute-start | bytes 786440 | tf_op jit(solution)/shard_map/ppermute | solution.py:330
  147.8 12.6 %collective-permute-start.12 = (bf16[2,256,256]{2,1,0:T(8,128)(2,1)}, bf16[2,256,256]{2,1,0:T(8,128)(2,1)}, u32[]{:S(2)}, u32[]{:S(2)}) collective-permute-start(bf16[2,256,256]{2,1,0:T(8,128)(2,1)} %get-tuple-element.11.refs_0_), channel_id=1, source_target_pairs={{1,0},{0,1},{3,2},{2,3},{5,4},{4,5},{7,6},{6,7},{9,8},{8,9},{11,10... | collective-permute-start | bytes 786440 | tf_op jit(solution)/shard_map/ppermute | solution.py:330
  149.0 18.8 %collective-permute-start.16 = (bf16[256,1024]{1,0:T(8,128)(2,1)}, bf16[256,1024]{1,0:T(8,128)(2,1)S(1)}, u32[]{:S(2)}, u32[]{:S(2)}) collective-permute-start(bf16[256,1024]{1,0:T(8,128)(2,1)} %collective-permute-done.15.refs_8_), channel_id=1, source_target_pairs={{2,0},{0,2},{6,4},{4,6},{10,8},{8,10},{14,12},{12,14},{18,16},{16,... | collective-permute-start | bytes 1572872 | tf_op jit(solution)/shard_map/ppermute | solution.py:330
  149.0 18.8 %collective-permute-start.18 = (bf16[256,1024]{1,0:T(8,128)(2,1)}, bf16[256,1024]{1,0:T(8,128)(2,1)S(1)}, u32[]{:S(2)}, u32[]{:S(2)}) collective-permute-start(bf16[256,1024]{1,0:T(8,128)(2,1)} %collective-permute-done.17.refs_10_), channel_id=1, source_target_pairs={{2,0},{0,2},{6,4},{4,6},{10,8},{8,10},{14,12},{12,14},{18,16},{16,... | collective-permute-start | bytes 1572872 | tf_op jit(solution)/shard_map/ppermute | solution.py:330
  165.7 24.8 %collective-permute-start.14 = (bf16[256,1024]{1,0:T(8,128)(2,1)}, bf16[256,1024]{1,0:T(8,128)(2,1)}, u32[]{:S(2)}, u32[]{:S(2)}) collective-permute-start(bf16[256,1024]{1,0:T(8,128)(2,1)} %project.5), channel_id=1, source_target_pairs={{8,0},{10,2},{12,4},{14,6},{0,8},{2,10},{4,12},{6,14},{24,16},{26,... | collective-permute-start | bytes 1572872 | tf_op jit(solution)/shard_map/ppermute | solution.py:330
  165.7 11.1 %collective-permute-start.3 = (bf16[2,256,256]{2,1,0:T(8,128)(2,1)S(1)}, bf16[2,256,256]{2,1,0:T(8,128)(2,1)S(1)}, u32[]{:S(2)}, u32[]{:S(2)}) collective-permute-start(bf16[2,256,256]{2,1,0:T(8,128)(2,1)S(1)} %copy-done.8), channel_id=1, source_target_pairs={{1,0},{0,1},{3,2},{2,3},{5,4},{4,5},{7,6},{6,7},{9,8},{8,9},{11,10... | collective-permute-start | bytes 786440 | tf_op jit(solution)/shard_map/ppermute | solution.py:330
  167.3 11.5 %collective-permute-start.2 = (bf16[2,256,256]{2,1,0:T(8,128)(2,1)S(1)}, bf16[2,256,256]{2,1,0:T(8,128)(2,1)S(1)}, u32[]{:S(2)}, u32[]{:S(2)}) collective-permute-start(bf16[2,256,256]{2,1,0:T(8,128)(2,1)S(1)} %copy-done.9), channel_id=1, source_target_pairs={{1,0},{0,1},{3,2},{2,3},{5,4},{4,5},{7,6},{6,7},{9,8},{8,9},{11,10... | collective-permute-start | bytes 786440 | tf_op jit(solution)/shard_map/ppermute | solution.py:330
  174.9 17.0 %collective-permute-start.19 = (bf16[256,1024]{1,0:T(8,128)(2,1)}, bf16[256,1024]{1,0:T(8,128)(2,1)}, u32[]{:S(2)}, u32[]{:S(2)}) collective-permute-start(bf16[256,1024]{1,0:T(8,128)(2,1)} %project.7), channel_id=1, source_target_pairs={{8,0},{10,2},{12,4},{14,6},{0,8},{2,10},{4,12},{6,14},{24,16},{26,... | collective-permute-start | bytes 1572872 | tf_op jit(solution)/shard_map/ppermute | solution.py:330
  (15 other events, 104.7 us)
